TPU v7x, 256 devices: a whole 4x4x8 slice. The times are simulated.
256 devices in a mesh: replica: 16 (over z, core), ctx: 16 (over x, y).
Axes of the slice: x: 4, y: 4, z: 8, core: 2. Of those that a mesh axis runs over, the one named last changes fastest.
Arguments:
- queries: bfloat16 [64, 128, 3584], P('replica', 'ctx'), may hold values from -128 to 128
- key_cache: bfloat16 [16384, 512], P('ctx'), may hold values from -6 to 6
- value_cache: bfloat16 [16384, 512], P('ctx'), may hold values from -6 to 6
- key_scale: float32 [128, 4], P('ctx'), may hold values from 0.7 to 1.4
- value_scale: float32 [128, 4], P('ctx'), may hold values from 0.5 to 2
- pattern: int32 [28, 64, 32], replicated, may hold values from 0 to 127
- target: int32 [64], replicated, may hold values from 0 to 15, as said below
Outputs:
- landed: bfloat16 [64, 128, 3584], P('replica', 'ctx')
Inputs may be any that keep to these rules, and one draw needn't show every extreme that they name: `target`: query block j belongs to group j // 4. The blocks of one group go to distinct groups, and every group receives exactly 4 blocks.
All inputs are finite; a program needn't handle non-finite values.
Results may differ from a plain program's by a relative error of at most 0.018.
Values may be sent and summed in bfloat16 or wider, within the bound.
A program may use at most 64 MiB of HBM per device.

v0:
```python
import math

import jax
import jax.numpy as jnp
from jax import lax
from jax.sharding import Mesh
from jax.sharding import PartitionSpec as P

CTX = ("ctx_0", "ctx_1")


def gather_axes(shard, axes, dim):
    for axis in reversed(axes):
        shard = lax.all_gather(shard, axis, axis=dim, tiled=True)
    return shard


def copy_for_each(shard, axis):
    devices = lax.axis_size(axis)
    return lax.all_to_all(
        jnp.broadcast_to(shard[None], (devices, *shard.shape)), axis, 0, 0, tiled=True
    )


def taken_together(shard, axis):
    return copy_for_each(shard, axis).max(axis=0)


def split_up(shard, dim, devices):
    before, after = (shard.shape[:dim], shard.shape[dim + 1 :])
    return jnp.moveaxis(shard.reshape(*before, devices, -1, *after), dim, 0)


def sum_at_owner(shard, axis, dim):
    devices = lax.axis_size(axis)
    tiles = lax.all_to_all(split_up(shard, dim, devices), axis, 0, 0, tiled=True)
    return jnp.sum(tiles.astype(jnp.float32), axis=0)


def sent_together(arrays, axis, dim, along):
    both = jnp.concatenate(arrays, axis=along)
    filled, at, finished = (sum_at_owner(both, axis, dim), 0, [])
    for a in arrays:
        finished.append(lax.slice_in_dim(filled, at, at + a.shape[along], axis=along))
        at += a.shape[along]
    return tuple(finished)


def arrivals(target, group_index, group_count, per_group):
    block_grid = target.reshape(group_count, per_group)
    hit_table = (block_grid == group_index).astype(jnp.int32)
    coming = jnp.sum(hit_table, axis=1)
    arrival_slot = jnp.cumsum(coming) - 1
    places = jnp.arange(per_group, dtype=jnp.int32)
    matched = (coming[None, :] > 0) & (arrival_slot[None, :] == places[:, None])
    anchor = jnp.arange(group_count, dtype=jnp.int32) * per_group + jnp.sum(
        hit_table * places[None, :], axis=1
    )
    arriving = jnp.sum(jnp.where(matched, anchor[None, :], 0), axis=1)
    return (matched.astype(jnp.bfloat16), arriving)


def relocate(blocks, target, group_index, group_count, per_group, picker):
    own_targets = lax.dynamic_slice_in_dim(target, group_index * per_group, per_group)
    outgoing = (own_targets[None, :] == jnp.arange(group_count, dtype=jnp.int32)[:, None]).astype(
        jnp.bfloat16
    )
    packed = jnp.einsum("dk,kxh->dxh", outgoing, blocks, preferred_element_type=jnp.float32).astype(
        jnp.bfloat16
    )
    received = lax.all_to_all(packed, "replica", split_axis=0, concat_axis=0, tiled=True)
    return jnp.einsum("sr,rxh->sxh", picker, received, preferred_element_type=jnp.float32).astype(
        jnp.bfloat16
    )


def collect(blocks):
    return gather_axes(blocks, CTX, 1)


def attend(
    whole,
    block_list,
    key_cache,
    value_cache,
    key_scale,
    value_scale,
    pattern,
    shard_index,
    kv_blocks,
):
    block_count, block_rows, row_width = whole.shape
    kv_heads = key_scale.shape[1]
    head_size = key_cache.shape[1] // kv_heads
    head_count = row_width // head_size
    group_size = head_count // kv_heads
    local_blocks = key_cache.shape[0] // block_rows
    first_block = kv_blocks - pattern.shape[1]
    query = whole.reshape(block_count, block_rows, kv_heads, group_size, head_size)
    keys = key_cache.reshape(local_blocks, block_rows, kv_heads, head_size)
    values = value_cache.reshape(local_blocks, block_rows, kv_heads, head_size)
    listed = jnp.take(pattern, block_list, axis=1).reshape(
        kv_heads, group_size, block_count, pattern.shape[2]
    )
    diagonal = first_block + block_list
    row_ids = jnp.arange(block_rows, dtype=jnp.int32)
    block_ids = shard_index * local_blocks + jnp.arange(local_blocks, dtype=jnp.int32)
    key_pos = block_ids[:, None] * block_rows + row_ids[None, :]
    inv_root = 1.0 / math.sqrt(head_size)

    def one_item(item):
        block_slot = item // kv_heads
        head = item % kv_heads
        query_tile = lax.dynamic_index_in_dim(
            lax.dynamic_index_in_dim(query, block_slot, 0, keepdims=False), head, 1, keepdims=False
        )
        key_head = lax.dynamic_index_in_dim(keys, head, 2, keepdims=False)
        value_head = lax.dynamic_index_in_dim(values, head, 2, keepdims=False)
        heads_listed = lax.dynamic_index_in_dim(
            lax.dynamic_index_in_dim(listed, head, 0, keepdims=False), block_slot, 1, keepdims=False
        )
        diag = lax.dynamic_index_in_dim(diagonal, block_slot, 0, keepdims=False)
        chosen = (
            jnp.any(heads_listed[:, :, None] == block_ids[None, None, :], axis=1)
            | (block_ids == diag)[None, :]
        )
        query_pos = diag * block_rows + row_ids
        causal = key_pos[None, :, :] <= query_pos[:, None, None]
        allowed = chosen[:, None, :, None] & causal[None]
        key_factor = lax.dynamic_index_in_dim(key_scale, head, 1, keepdims=False) * inv_root
        value_factor = lax.dynamic_index_in_dim(value_scale, head, 1, keepdims=False)
        product = jnp.einsum(
            "rkd,btd->krbt", query_tile, key_head, preferred_element_type=jnp.float32
        )
        scores = product * key_factor[None, None, :, None]
        local_top = jnp.max(jnp.where(allowed, scores, -jnp.inf), axis=(2, 3))
        expo = jnp.where(allowed, jnp.exp(scores - local_top[:, :, None, None]), 0.0)
        weight = (expo * value_factor[None, None, :, None]).astype(jnp.bfloat16)
        numer = jnp.einsum("krbt,btd->rkd", weight, value_head, preferred_element_type=jnp.float32)
        denom = jnp.transpose(jnp.sum(expo, axis=(2, 3)))
        return (numer, denom, jnp.transpose(local_top))

    numer_all, denom_all, top_all = lax.map(
        one_item, jnp.arange(block_count * kv_heads, dtype=jnp.int32)
    )
    numer_all = numer_all.reshape(block_count, kv_heads, block_rows, group_size, head_size)
    denom_all = denom_all.reshape(block_count, kv_heads, block_rows, group_size)
    local_top = top_all.reshape(block_count, kv_heads, block_rows, group_size)
    top_score = taken_together(local_top.astype(jnp.bfloat16), CTX).astype(local_top.dtype)
    rescale = jnp.exp(local_top - top_score)
    numer_scaled = jnp.transpose(numer_all * rescale[..., None], (0, 2, 1, 3, 4)).reshape(
        block_count, block_rows, row_width
    )
    denom_scaled = jnp.transpose(denom_all * rescale, (0, 2, 1, 3)).reshape(
        block_count, block_rows, head_count
    )
    numer_sum, denom_sum = sent_together(
        (numer_scaled.astype(jnp.bfloat16), denom_scaled.astype(jnp.bfloat16)), CTX, 1, 2
    )
    own_rows = numer_sum.shape[1]
    attended = (
        numer_sum.reshape(block_count, own_rows, head_count, head_size) / denom_sum[..., None]
    )
    return attended.reshape(block_count, own_rows, row_width).astype(jnp.bfloat16)


def per_device(queries, key_cache, value_cache, key_scale, value_scale, pattern, target):
    group_count = lax.axis_size("replica")
    shard_count = lax.axis_size(CTX)
    group_index = lax.axis_index("replica")
    shard_index = lax.axis_index(CTX)
    per_group = queries.shape[0]
    block_rows = queries.shape[1] * shard_count
    kv_blocks = key_cache.shape[0] // block_rows * shard_count
    picker, arriving = arrivals(target, group_index, group_count, per_group)
    moved = relocate(queries, target, group_index, group_count, per_group, picker)
    whole = collect(moved)
    return attend(
        whole,
        arriving,
        key_cache,
        value_cache,
        key_scale,
        value_scale,
        pattern,
        shard_index,
        kv_blocks,
    )


def solution(mesh):
    finer = Mesh(mesh.devices.reshape(mesh.shape["replica"], 4, 4), ("replica", "ctx_0", "ctx_1"))
    return jax.shard_map(
        per_device,
        mesh=finer,
        in_specs=(
            P("replica", CTX, None),
            P(CTX, None),
            P(CTX, None),
            P(CTX, None),
            P(CTX, None),
            P(),
            P(),
        ),
        out_specs=P("replica", CTX, None),
        check_vma=False,
    )
```

profile of v0, /device:TPU:1, one launch (start us, length us, event | category | flops | bytes accessed | tf_op | source)
XLA Modules:
  0.0 392.5 jit_solution(897643463920521804)
XLA Ops:
  8.1 1.4 copy.123
  9.5 10.1 %all-to-all-start = ((bf16[16,8,3584]{2,1,0:T(8,128)(2,1)}), bf16[16,8,3584]{2,1,0:T(8,128)(2,1)S(1)}, u32[]{:S(2)}, u32[]{:S(2)}) async-start(bf16[16,8,3584]{2,1,0:T(8,128)(2,1)} %copy.123), calls=%async_computation | async-start | bytes 1835008 | tf_op jit(solution)/shard_map/all_to_all | solution.py:71
  20.1 24.8 %all-to-all-done = bf16[16,8,3584]{2,1,0:T(8,128)(2,1)S(1)} async-done(((bf16[16,8,3584]{2,1,0:T(8,128)(2,1)}), bf16[16,8,3584]{2,1,0:T(8,128)(2,1)S(1)}, u32[]{:S(2)}, u32[]{:S(2)}) %all-to-all-start) | async-done | bytes 917536 | tf_op jit(solution)/shard_map/all_to_all | solution.py:71
  45.5 13.9 %all_gather.6 = bf16[4,32,3584]{2,0,1:T(4,128)(2,1)} all-gather(bf16[4,8,3584]{2,0,1:T(4,128)(2,1)S(1)} %convolution_convert_fusion.1), channel_id=1, replica_groups=mesh['replica'=16,'ctx_0'=4,'ctx_1'=4] {'ctx_1'}, dimensions={1}, use_global_device_ids=true | all-gather | bytes 1146880 | tf_op jit(solution)/shard_map/all_gather | solution.py:14
  59.5 2.0 copy.119
  64.1 40.4 %all-gather.2.cloned.1.call-done = bf16[4,128,3584]{2,0,1:T(4,128)(2,1)} async-done(((bf16[4,32,3584]{2,0,1:T(4,128)(2,1)}), bf16[4,128,3584]{2,0,1:T(4,128)(2,1)}) %all-gather.2.cloned.1.call-update) | async-done | bytes 3670032 | tf_op jit(solution)/shard_map/all_gather | solution.py:14
  104.5 7.2 %copy.125 = bf16[4,128,3584]{1,2,0:T(8,128)(2,1)} copy(bf16[4,128,3584]{2,0,1:T(4,128)(2,1)} %all-gather.2.cloned.1.call-done) | data formatting | bytes 7340032 | tf_op jit(solution)/shard_map/all_gather | solution.py:14
  111.7 185.7 %while.18 = (s32[]{:T(128)}, f32[16,128,7,128]{1,3,2,0:T(8,128)}, f32[16,128,7]{1,2,0:T(8,128)S(1)}, f32[16,128,7]{1,0,2:T(8,128)S(1)}, s32[16]{0:T(128)S(1)}, /...) while((s32[]{:T(128)}, f32[16,128,7,128]{1,3,2,0:T(8,128)}, ...), condition=%wide.region_8.9_spmd.clone, body=%wide.region_4.8_spmd.clone.sunk | while | flops 483658688 | bytes 12803092 | solution.py:143
  118.3 1.7 fusion.49
  120.0 2.2 fusion.50
  122.2 1.1 fusion.51
  129.9 1.7 fusion.49
  131.6 2.2 fusion.50
  133.8 1.1 fusion.51
  141.6 1.7 fusion.49
  143.3 2.1 fusion.50
  145.4 1.1 fusion.51
  153.2 1.7 fusion.49
  154.9 2.1 fusion.50
  157.0 1.1 fusion.51
  164.8 1.7 fusion.49
  166.5 2.1 fusion.50
  168.6 1.1 fusion.51
  176.4 1.7 fusion.49
  178.1 2.1 fusion.50
  180.2 1.1 fusion.51
  188.0 1.7 fusion.49
  189.7 2.1 fusion.50
  191.8 1.1 fusion.51
  199.6 1.7 fusion.49
  201.3 2.1 fusion.50
  203.4 1.1 fusion.51
  211.2 1.7 fusion.49
  212.9 2.1 fusion.50
  215.0 1.1 fusion.51
  222.7 1.7 fusion.49
  224.5 2.1 fusion.50
  226.6 1.1 fusion.51
  234.4 1.7 fusion.49
  236.1 2.1 fusion.50
  238.2 1.1 fusion.51
  246.0 1.7 fusion.49
  247.7 2.1 fusion.50
  249.8 1.1 fusion.51
  257.6 1.7 fusion.49
  259.3 2.1 fusion.50
  261.4 1.1 fusion.51
  269.2 1.7 fusion.49
  270.9 2.1 fusion.50
  273.0 1.1 fusion.51
  280.8 1.7 fusion.49
  282.5 2.1 fusion.50
  284.6 1.1 fusion.51
  292.4 1.7 fusion.49
  294.1 2.1 fusion.50
  296.2 1.1 fusion.51
  297.4 0.9 broadcast_in_dim.95
  298.3 5.5 %all-to-all-start.1 = ((bf16[16,4,4,128,7]{3,2,4,1,0:T(4,128)(2,1)}), bf16[16,4,4,128,7]{3,2,4,1,0:T(4,128)(2,1)S(1)}, u32[]{:S(2)}, u32[]{:S(2)}) async-start(bf16[16,4,4,128,7]{3,2,4,1,0:T(4,128)(2,1)} %broadcast_in_dim.95), calls=%async_computation.1 | async-start | bytes 917504 | tf_op jit(solution)/shard_map/all_to_all | solution.py:20
  303.9 9.9 %copy.134 = f32[4,4,128,7,128]{4,3,1,2,0:T(8,128)} copy(f32[4,4,128,7,128]{2,4,3,1,0:T(8,128)} %bitcast.116) | data formatting | bytes 14680064 | tf_op jit(solution)/shard_map/reshape | solution.py:146
  314.4 7.3 %fusion.25 = bf16[4,128,4,7,128]{4,3,2,1,0:T(8,128)(2,1)} fusion(f32[4,4,128,7,128]{4,3,1,2,0:T(8,128)} %copy.134, f32[4,4,128,7]{3,1,2,0:T(4,128)S(1)} %copy.133), kind=kLoop, calls=%fused_computation.43 | loop fusion | flops 3670016 | bytes 11067392 | tf_op jit(solution)/shard_map/convert_element_type | solution.py:158
  321.7 8.0 %convert_element_type.65 = bf16[4,16,8,3584]{3,2,1,0:T(8,128)(2,1)} reshape(bf16[4,128,4,7,128]{4,3,2,1,0:T(8,128)(2,1)} %fusion.25) | data formatting | bytes 7340032 | tf_op jit(solution)/shard_map/convert_element_type | solution.py:158
  330.3 2.3 maximum_bitcast_fusion
  332.9 51.2 %all_to_all.15 = bf16[16,4,8,3612]{3,2,1,0:T(8,128)(2,1)S(1)} all-to-all(bf16[16,4,8,3612]{3,2,1,0:T(8,128)(2,1)S(1)} %copy.139), channel_id=1, replica_groups=mesh['replica'=16,'ctx_0'=4,'ctx_1'=4] {'ctx_0','ctx_1'}, dimensions={0} | all-to-all | bytes 7397376 | tf_op jit(solution)/shard_map/all_to_all | solution.py:36
  384.8 0.9 fusion.27
  (312 shorter events, 59.9 us)
Async XLA Ops:
  6.5 1.0 copy-start
  6.5 13.1 %copy-start.6 = (s32[64]{0:T(128)S(1)}, s32[64]{0:T(128)}, u32[]{:S(2)}) copy-start(s32[64]{0:T(128)} %param.15) | copy-start | bytes 772
  9.5 52.8 %copy-start.1 = (bf16[1024,512]{1,0:T(8,128)(2,1)S(1)}, bf16[1024,512]{1,0:T(8,128)(2,1)}, u32[]{:S(2)}) copy-start(bf16[1024,512]{1,0:T(8,128)(2,1)} %param.11) | copy-start | bytes 3145732
  9.5 35.4 %all-to-all-start = ((bf16[16,8,3584]{2,1,0:T(8,128)(2,1)}), bf16[16,8,3584]{2,1,0:T(8,128)(2,1)S(1)}, u32[]{:S(2)}, u32[]{:S(2)}) async-start(bf16[16,8,3584]{2,1,0:T(8,128)(2,1)} %copy.123), calls=%async_computation | async-start | bytes 1835008 | tf_op jit(solution)/shard_map/all_to_all | solution.py:71
  19.6 84.9 %all-gather.2.cloned.1.call-start = ((), (), s32[]{:S(2)}) async-start(), calls=%async_computation.3 | async-start | bytes 4587520 | tf_op jit(solution)/shard_map/all_gather | solution.py:14
  59.4 4.0 %copy-start.2 = (bf16[1024,512]{1,0:T(8,128)(2,1)S(1)}, bf16[1024,512]{1,0:T(8,128)(2,1)}, u32[]{:S(2)}) copy-start(bf16[1024,512]{1,0:T(8,128)(2,1)} %param.10) | copy-start | bytes 3145732
  61.6 0.6 copy-start.4
  62.6 1.4 copy-start.5
  64.1 47.6 %copy-start.3 = (f32[16,128,7]{1,2,0:T(8,128)S(1)}, f32[16,128,7]{1,2,0:T(8,128)}, u32[]{:S(2)}) copy-start(f32[16,128,7]{1,2,0:T(8,128)} %custom-call.3) | copy-start | bytes 172036
  298.3 15.4 %all-to-all-start.1 = ((bf16[16,4,4,128,7]{3,2,4,1,0:T(4,128)(2,1)}), bf16[16,4,4,128,7]{3,2,4,1,0:T(4,128)(2,1)S(1)}, u32[]{:S(2)}, u32[]{:S(2)}) async-start(bf16[16,4,4,128,7]{3,2,4,1,0:T(4,128)(2,1)} %broadcast_in_dim.95), calls=%async_computation.1 | async-start | bytes 917504 | tf_op jit(solution)/shard_map/all_to_all | solution.py:20
Sparse Core Ops, SparseCore 0:
  59.6 44.8 all-gather.1
where the time goes:
time: 396 us; the launch traced here: 393 us
  waiting for transfers between devices  65.2 us (16%)
  blocking collectives  65.1 us (16%)
  matrix products  62.5 us (16%)
  other arithmetic  60.2 us (15%)
  local copies, waits for them, and re-layouts  55.8 us (14%)
  loops' own time  54.3 us (14%)
  starting transfers between devices  15.7 us (4%)
  between operations  13.7 us (3%)
    another operation x1, loops' own time, attend(): lax.map(one_item, jnp.arange(block_count * kv_heads, dtype=jnp.int32))  54.3 us
    all_to_all x1, blocking collectives, sum_at_owner(): lax.all_to_all(split_up(shard, dim, devices), axis, 0, 0, tiled=True)  51.2 us
    all_gather x1, waiting for transfers between devices, gather_axes(): shard = lax.all_gather(shard, axis, axis=dim, tiled=True)  40.4 us
    dot_general x16, matrix products, one_item(): jnp.einsum('krbt,btd->rkd', weight, value_head, preferred_element_type=jn...  34 us
    dot_general x16, matrix products, one_item(): jnp.einsum('rkd,btd->krbt', query_tile, key_head, preferred_element_type=...  27.4 us
    all_to_all x1, waiting for transfers between devices, relocate(): lax.all_to_all(packed, 'replica', split_axis=0, concat_axis=0, tiled=True)  24.8 us
    reduce_sum x16, other arithmetic, one_item(): denom = jnp.transpose(jnp.sum(expo, axis=(2, 3)))  17.3 us
    all_gather x1, blocking collectives, gather_axes(): shard = lax.all_gather(shard, axis, axis=dim, tiled=True)  13.9 us
  transfers between devices with their start and end apart: 3, of which 2 were waited for; matrix products, arithmetic and copies ran while one was open for 4% of the time, Pallas kernels for 0%

commit v1 on v0

v1 whole, which is shorter than its diff:
```python
import functools
import math

import jax
import jax.numpy as jnp
from jax import lax
from jax.experimental import pallas as pl
from jax.experimental.pallas import tpu as pltpu
from jax.sharding import PartitionSpec as P

MESH = pl.DeviceIdType.MESH
BF16 = jnp.bfloat16
F32 = jnp.float32

NX = 4
NY = 4
NZ = 8
HEADS = 7
D = 128
B = 128
QB = 4
KB = 32
SLICE = HEADS * D
WIDE = SLICE + 128
ROWS = B // (NX * NY)
SUM_LANE = 64
NEG = -(2.0**100)
STEP = 2
FIRST = 64


def place():
    rep = lax.axis_index("replica")
    ctx = lax.axis_index("ctx")
    return rep, rep // 2, rep % 2, ctx // NY, ctx % NY


def greet(partners):
    barrier = pltpu.get_barrier_semaphore()
    for who in partners:
        pl.semaphore_signal(barrier, inc=1, device_id=who, device_id_type=MESH)
    pl.semaphore_wait(barrier, len(partners))


def remote(src, dst, send, recv, who):
    return pltpu.make_async_remote_copy(
        src_ref=src, dst_ref=dst, send_sem=send, recv_sem=recv, device_id=who, device_id_type=MESH
    )


def spread_kernel(
    q, k, v, sc, q_all, k_all, v_all, s_all,
    q_send, q_recv, k_send, k_recv, v_send, v_recv, s_send, s_recv,
    up_send, up_recv, dn_send, dn_recv, f_send, f_recv, kc_send, kc_recv, vc_send, vc_recv, own,
):
    rep, z, c, x, y = place()
    sib = (rep + 1 - 2 * c, x * NY + y)
    xs = [(x + d) % NX for d in range(NX)]
    back = [(x + NX - d) % NX for d in range(NX)]
    at_x = [(rep, xs[d] * NY + y) for d in range(NX)]
    up = (rep, x * NY + (y + 1) % NY)
    down = (rep, x * NY + (y + NY - 1) % NY)
    below, above = (y + NY - 1) % NY, (y + 1) % NY
    half = pl.ds(c * 512, 512)
    greet([at_x[1], at_x[2], at_x[3], up, down, sib])

    def cols(d, n):
        return pl.ds(pl.multiple_of(xs[d] * n, n), n)

    qx = [None] * NX
    kx = [None] * NX
    vx = [None] * NX
    sx = [None] * NX
    order = (1, 3, 2)
    for d in order:
        qx[d] = remote(q.at[:, :, cols(d, SLICE)], q_all.at[y, x], q_send.at[d], q_recv.at[d], at_x[d])
        qx[d].start()
    own_q = q.at[:, :, cols(0, SLICE)]
    ups = [None] * NX
    dns = [None] * NX
    ups[0] = remote(own_q, q_all.at[y, x], up_send.at[0], up_recv.at[0], up)
    dns[0] = remote(own_q, q_all.at[y, x], dn_send.at[0], dn_recv.at[0], down)
    ups[0].start()
    dns[0].start()
    for d in order:
        kx[d] = remote(k.at[half, cols(d, D)], k_all.at[x, half], k_send.at[d], k_recv.at[d], at_x[d])
        vx[d] = remote(v.at[half, cols(d, D)], v_all.at[x, half], v_send.at[d], v_recv.at[d], at_x[d])
        sx[d] = remote(sc, s_all.at[x], s_send.at[d], s_recv.at[d], at_x[d])
        kx[d].start()
        vx[d].start()
        sx[d].start()
    stay = [
        pltpu.make_async_copy(own_q, q_all.at[y, x], own.at[0]),
        pltpu.make_async_copy(k.at[:, cols(0, D)], k_all.at[x], own.at[1]),
        pltpu.make_async_copy(v.at[:, cols(0, D)], v_all.at[x], own.at[2]),
        pltpu.make_async_copy(sc, s_all.at[x], own.at[3]),
    ]
    for copy in stay:
        copy.start()
    for d in order:
        qx[d].wait_recv()
        piece = q_all.at[y, back[d]]
        ups[d] = remote(piece, piece, up_send.at[d], up_recv.at[d], up)
        dns[d] = remote(piece, piece, dn_send.at[d], dn_recv.at[d], down)
        ups[d].start()
        dns[d].start()
    on = [None] * NX
    for d in (0, 1):
        ups[d].wait_recv()
        piece = q_all.at[below, back[d]]
        on[d] = remote(piece, piece, f_send.at[d], f_recv.at[d], up)
        on[d].start()
    for d in (3, 2):
        dns[d].wait_recv()
        piece = q_all.at[above, back[d]]
        on[d] = remote(piece, piece, f_send.at[d], f_recv.at[d], down)
        on[d].start()
    kc = [None] * NX
    vc = [None] * NX
    for d in order:
        kx[d].wait_recv()
        piece = k_all.at[back[d], half]
        kc[d] = remote(piece, piece, kc_send.at[d], kc_recv.at[d], sib)
        kc[d].start()
        vx[d].wait_recv()
        piece = v_all.at[back[d], half]
        vc[d] = remote(piece, piece, vc_send.at[d], vc_recv.at[d], sib)
        vc[d].start()
        sx[d].wait_recv()
    for d in (2, 3):
        ups[d].wait_recv()
    for d in (0, 1):
        dns[d].wait_recv()
    for d in range(NX):
        on[d].wait_recv()
        on[d].wait_send()
        ups[d].wait_send()
        dns[d].wait_send()
    for d in order:
        kc[d].wait_recv()
        vc[d].wait_recv()
        kc[d].wait_send()
        vc[d].wait_send()
        qx[d].wait_send()
        kx[d].wait_send()
        vx[d].wait_send()
        sx[d].wait_send()
    for copy in stay:
        copy.wait()


def spread(q, k, v, sc):
    dma = pltpu.SemaphoreType.DMA((NX,))
    any_space = pl.BlockSpec(memory_space=pl.ANY)
    return pl.pallas_call(
        spread_kernel,
        out_shape=[
            jax.ShapeDtypeStruct((NY, NX, QB, ROWS, SLICE), BF16),
            jax.ShapeDtypeStruct((NX, 1024, D), BF16),
            jax.ShapeDtypeStruct((NX, 1024, D), BF16),
            jax.ShapeDtypeStruct((NX, 8, 128), F32),
        ],
        in_specs=[any_space] * 4,
        out_specs=[any_space] * 4,
        scratch_shapes=[dma] * 19,
        compiler_params=pltpu.CompilerParams(collective_id=0, has_side_effects=True),
        name="spread",
    )(q, k, v, sc)


def attend_kernel(
    ints, steps, where_x, q_ref, k_ref, v_ref, s_ref, out_ref, vs, qs, sc, mx, acc, su
):
    qb = pl.program_id(0)
    hx = where_x[0]

    @pl.when(qb == 0)
    def _():
        @pl.loop(0, KB)
        def _(kb):
            factor = s_ref[kb // 8, kb % 8, 4 + hx]
            vs[kb] = (v_ref[kb].astype(F32) * factor).astype(BF16)

    qs[...] = q_ref[:, :, 0].astype(F32).reshape(B, SLICE).astype(BF16)
    mx[...] = jnp.full(mx.shape, NEG, F32)
    acc[...] = jnp.zeros(acc.shape, F32)
    su[...] = jnp.zeros(su.shape, F32)
    row = lax.broadcasted_iota(jnp.int32, (B, B), 0)
    row = ((row // 8) % 4) * 32 + (row // 32) * 8 + row % 8
    ahead = lax.broadcasted_iota(jnp.int32, (B, B), 1) - row
    count = steps[qb]
    to_log2 = math.log2(math.e) / math.sqrt(D)

    @pl.loop(0, count)
    def _(t):
        for h in range(HEADS):
            top = mx[h]
            for u in range(STEP):
                code = ints[(qb * HEADS + h) * KB + t * STEP + u]
                kb = code & (KB - 1)
                reach = (code >> 5) * B
                factor = s_ref[kb // 8, kb % 8, hx] * to_log2
                score = lax.dot_general(
                    qs[:, h * D : (h + 1) * D],
                    k_ref[kb],
                    (((1,), (1,)), ((), ())),
                    preferred_element_type=F32,
                )
                score = jnp.where(ahead <= reach, score * factor, NEG)
                sc[h, t * STEP + u] = score
                top = jnp.maximum(top, score)
            mx[h] = top

    for h in range(HEADS):
        top = jnp.max(mx[h], axis=1, keepdims=True)
        mx[h] = jnp.broadcast_to(top, (B, B)).astype(BF16).astype(F32)

    @pl.loop(0, count)
    def _(t):
        for h in range(HEADS):
            top = mx[h]
            total = su[h]
            weights = []
            values = []
            for u in range(STEP):
                code = ints[(qb * HEADS + h) * KB + t * STEP + u]
                weight = jnp.exp2(sc[h, t * STEP + u] - top)
                total = total + weight
                weights.append(weight.astype(BF16))
                values.append(vs[code & (KB - 1)])
            su[h] = total
            acc[h] += jnp.dot(
                jnp.concatenate(weights, axis=1),
                jnp.concatenate(values, axis=0),
                preferred_element_type=F32,
            )

    lane = lax.broadcasted_iota(jnp.int32, (B, 128), 1)
    extra = jnp.zeros((B, 128), F32)
    for h in range(HEADS):
        extra = jnp.where(lane == h, mx[h], extra)
        total = jnp.sum(su[h], axis=1, keepdims=True)
        extra = jnp.where(lane == SUM_LANE + h, jnp.broadcast_to(total, (B, 128)), extra)
        part = acc[h].astype(BF16)
        for d in range(NY):
            out_ref[d, 0, :, h * D : (h + 1) * D] = part[d * 32 : (d + 1) * 32]
    extra = extra.astype(BF16)
    for d in range(NY):
        out_ref[d, 0, :, SLICE:WIDE] = extra[d * 32 : (d + 1) * 32]


def attend(ints, steps, where_x, q_all, k_all, v_all, s_all):
    whole = lambda qb, *_: (0, 0, 0)
    once = pl.Buffered(1)
    return pl.pallas_call(
        attend_kernel,
        out_shape=jax.ShapeDtypeStruct((NY, QB, 32, WIDE), BF16),
        grid_spec=pltpu.PrefetchScalarGridSpec(
            num_scalar_prefetch=3,
            grid=(QB,),
            in_specs=[
                pl.BlockSpec((NY, NX, 1, ROWS, SLICE), lambda qb, *_: (0, 0, qb, 0, 0)),
                pl.BlockSpec((KB, B, D), whole, pipeline_mode=once),
                pl.BlockSpec((KB, B, D), whole, pipeline_mode=once),
                pl.BlockSpec(memory_space=pltpu.SMEM),
            ],
            out_specs=pl.BlockSpec((NY, 1, 32, WIDE), lambda qb, *_: (0, qb, 0, 0)),
            scratch_shapes=[
                pltpu.VMEM((KB, B, D), BF16),
                pltpu.VMEM((B, SLICE), BF16),
                pltpu.VMEM((HEADS, KB, B, B), F32),
                pltpu.VMEM((HEADS, B, B), F32),
                pltpu.VMEM((HEADS, B, D), F32),
                pltpu.VMEM((HEADS, B, B), F32),
            ],
        ),
        compiler_params=pltpu.CompilerParams(vmem_limit_bytes=40 << 20),
        name="attend",
    )(ints, steps, where_x, q_all, k_all.reshape(KB, B, D), v_all.reshape(KB, B, D), s_all)


def gather_kernel(
    p, got, parts, att,
    up_send, up_recv, dn_send, dn_recv, far_send, far_recv,
    x_send, x_recv, zu_send, zu_recv, zd_send, zd_recv, c_send, c_recv, own, own_x,
):
    rep, z, c, x, y = place()
    group = rep
    other = rep + 1 - 2 * c
    here = x * NY + y
    sib = (other, here)
    xs = [(x + d) % NX for d in range(NX)]
    at_x = [(rep, xs[d] * NY + y) for d in range(NX)]
    ys = [(y + d) % NY for d in range(NY)]
    at_y = [(rep, x * NY + ys[d]) for d in range(NY)]
    zup = (((z + 1) % NZ) * 2 + c, here)
    zdn = (((z + NZ - 1) % NZ) * 2 + c, here)
    greet([at_x[1], at_x[2], at_x[3], at_y[1], at_y[2], at_y[3], zup, zdn, sib])

    py = [[None] * NY for _ in range(QB)]
    sems = {1: (up_send, up_recv), 3: (dn_send, dn_recv), 2: (far_send, far_recv)}
    for b in range(QB):
        for d in (1, 3, 2):
            s, r = sems[d]
            py[b][d] = remote(p.at[ys[d], b], parts.at[y, b], s.at[b], r.at[b], at_y[d])
            py[b][d].start()
        py[b][0] = pltpu.make_async_copy(p.at[y, b], parts.at[y, b], own.at[b])
        py[b][0].start()

    px = [[None] * NX for _ in range(QB)]
    lane = lax.broadcasted_iota(jnp.int32, (32, 128), 1)

    def combine(b):
        for d in (1, 3, 2):
            py[b][d].wait_recv()
        py[b][0].wait()
        extra = [parts[s, b, :, SLICE:WIDE].astype(F32) for s in range(NY)]
        top = functools.reduce(jnp.maximum, extra)
        shift = [jnp.exp2(e - top) for e in extra]
        total = sum(w * pltpu.roll(e, SUM_LANE, 1) for w, e in zip(shift, extra))
        total = jnp.where(lane < HEADS, total, 1.0)
        ratio = [w / total for w in shift]
        for h in range(HEADS):
            cols = slice(h * D, (h + 1) * D)
            value = sum(
                jnp.broadcast_to(ratio[s][:, h : h + 1], (32, D)) * parts[s, b, :, cols].astype(F32)
                for s in range(NY)
            )
            value = value.reshape(NX, ROWS, D).astype(BF16)
            for d in range(NX):
                att[b, d, :, cols] = value[d]
        mine = pl.ds(pl.multiple_of(x * SLICE, SLICE), SLICE)
        for d in (1, 3, 2):
            px[b][d] = remote(
                att.at[b, xs[d]], got.at[group, b, :, mine], x_send.at[b, d], x_recv.at[b, d], at_x[d]
            )
            px[b][d].start()
        px[b][0] = pltpu.make_async_copy(att.at[b, x], got.at[group, b, :, mine], own_x.at[b])
        px[b][0].start()

    def across(src, b, k):
        piece = got.at[src, b]
        copy = remote(piece, piece, c_send.at[b, k], c_recv.at[b, k], sib)
        copy.start()
        return copy

    zu = [[None] * 5 for _ in range(QB)]
    zd = [[None] * 5 for _ in range(QB)]
    cs = [[None] * NZ for _ in range(QB)]

    def upward(src, b, k):
        piece = got.at[src, b]
        zu[b][k] = remote(piece, piece, zu_send.at[b, k], zu_recv.at[b, k], zup)
        zu[b][k].start()

    def downward(src, b, k):
        piece = got.at[src, b]
        zd[b][k] = remote(piece, piece, zd_send.at[b, k], zd_recv.at[b, k], zdn)
        zd[b][k].start()

    def land(b):
        for d in (1, 3, 2):
            px[b][d].wait_recv()
        px[b][0].wait()
        upward(group, b, 1)
        downward(group, b, 1)
        cs[b][0] = across(group, b, 0)

    def hop(b, k):
        if zu[b][k] is not None:
            src = ((z + NZ - k) % NZ) * 2 + c
            zu[b][k].wait_recv()
            if k < 3 or (k == 3 and b % 2 == 0):
                upward(src, b, k + 1)
            cs[b][k] = across(src, b, k)
        if zd[b][k] is not None:
            src = ((z + k) % NZ) * 2 + c
            zd[b][k].wait_recv()
            if k < 3 or (k == 3 and b % 2 == 1):
                downward(src, b, k + 1)
            cs[b][NZ - k] = across(src, b, NZ - k)

    for wave in range(QB + 5):
        for b in range(QB):
            stage = wave - b
            if stage == 0:
                combine(b)
            elif stage == 1:
                land(b)
            elif 2 <= stage <= 5:
                hop(b, stage - 1)

    for b in range(QB):
        for d in (1, 2, 3):
            py[b][d].wait_send()
            px[b][d].wait_send()
        for k in range(1, 5):
            for copy in (zu[b][k], zd[b][k]):
                if copy is not None:
                    copy.wait_send()
        for k in range(NZ):
            cs[b][k].wait_send()
            cs[b][k].wait_recv()


def gather(p):
    dma = pltpu.SemaphoreType.DMA
    return pl.pallas_call(
        gather_kernel,
        out_shape=jax.ShapeDtypeStruct((2 * NZ, QB, ROWS, NX * SLICE), BF16),
        in_specs=[pl.BlockSpec(memory_space=pl.ANY)],
        out_specs=pl.BlockSpec(memory_space=pl.ANY),
        scratch_shapes=[
            pltpu.VMEM((NY, QB, 32, WIDE), BF16),
            pltpu.VMEM((QB, NX, ROWS, SLICE), BF16),
        ]
        + [dma((QB,))] * 6
        + [dma((QB, NX))] * 2
        + [dma((QB, 5))] * 4
        + [dma((QB, NZ))] * 2
        + [dma((QB,))] * 2,
        compiler_params=pltpu.CompilerParams(
            collective_id=1, has_side_effects=True, vmem_limit_bytes=16 << 20
        ),
        name="gather",
    )(p)


def pick_kernel(target, me, got, out, sem):
    def look(j, found):
        hit = target[j] == me[0]

        @pl.when(hit)
        def _():
            pltpu.make_async_copy(got.at[j], out.at[found], sem.at[found]).start()

        return found + hit.astype(jnp.int32)

    lax.fori_loop(0, 2 * NZ * QB, look, jnp.int32(0))
    for s in range(QB):
        pltpu.make_async_copy(got.at[s], out.at[s], sem.at[s]).wait()


def pick(target, me, got):
    smem = pl.BlockSpec(memory_space=pltpu.SMEM)
    return pl.pallas_call(
        pick_kernel,
        out_shape=jax.ShapeDtypeStruct((QB, ROWS, NX * SLICE), BF16),
        in_specs=[smem, smem, pl.BlockSpec(memory_space=pl.ANY)],
        out_specs=pl.BlockSpec(memory_space=pl.ANY),
        scratch_shapes=[pltpu.SemaphoreType.DMA((QB,))],
        name="pick",
    )(target, me, got.reshape(2 * NZ * QB, ROWS, NX * SLICE))


def block_lists(pattern, group, x, y):
    mine = lax.dynamic_slice(pattern, (x * HEADS, group * QB, 0), (HEADS, QB, pattern.shape[2]))
    mine = jnp.transpose(mine, (1, 0, 2))
    kb = jnp.arange(KB, dtype=jnp.int32)
    block = ((kb // 8) * NY + y) * 8 + kb % 8
    diagonal = (FIRST + group * QB + jnp.arange(QB, dtype=jnp.int32))[:, None, None]
    chosen = jnp.any(mine[:, :, None, :] == block[None, None, :, None], axis=3)
    chosen = (chosen | (block == diagonal)) & (block <= diagonal)
    ones = chosen.astype(jnp.int32)
    rank = jnp.sum(jnp.where(kb[None, :] < kb[:, None], ones[:, :, None, :], 0), axis=3)
    code = kb + KB * (diagonal - block)
    empty = -KB * 1024
    hit = chosen[:, :, None, :] & (rank[:, :, None, :] == kb[:, None])
    ints = jnp.sum(jnp.where(hit, code[:, :, None, :] - empty, 0), axis=3) + empty
    most = jnp.max(jnp.sum(ones, axis=2), axis=1)
    return ints.reshape(-1), (most + STEP - 1) // STEP


def per_device(queries, key_cache, value_cache, key_scale, value_scale, pattern, target):
    rep, z, c, x, y = place()
    scales = jnp.pad(jnp.concatenate([key_scale, value_scale], axis=1), ((0, 0), (0, 120)))
    ints, steps = block_lists(pattern, rep, x, y)
    q_all, k_all, v_all, s_all = spread(queries, key_cache, value_cache, scales)
    partial = attend(ints, steps, x.reshape(1), q_all, k_all, v_all, s_all)
    got = gather(partial)
    return pick(target, rep.reshape(1), got)


def solution(mesh):
    return jax.shard_map(
        per_device,
        mesh=mesh,
        in_specs=(
            P("replica", "ctx", None),
            P("ctx", None),
            P("ctx", None),
            P("ctx", None),
            P("ctx", None),
            P(),
            P(),
        ),
        out_specs=P("replica", "ctx", None),
        check_vma=False,
    )
```

time: 396 us -> 113 us (0.29)
  Pallas kernels: 0 us -> 102 us
  waiting for transfers between devices: 65.2 us -> 0 us
  blocking collectives: 65.1 us -> 0 us
  matrix products: 62.5 us -> 0 us
  other arithmetic: 60.2 us -> 2.88 us
  loops' own time: 54.3 us -> 0 us
  local copies, waits for them, and re-layouts: 55.8 us -> 7.92 us
  starting transfers between devices: 15.7 us -> 0 us
  between operations: 13.7 us -> 0.09 us
    pallas_call x0 -> x4, Pallas kernels: none -> 102 us  [the longest x1 50.6 us: gather(): pl.pallas_call(gather_kernel, out_shape=jax.ShapeDtypeStruct((2 * NZ, QB,...]
    dot_general x34 -> x0, matrix products: 62.5 us -> none  [the longest x16 34 us: one_item(): jnp.einsum('krbt,btd->rkd', weight, value_head, preferred_element_type=jn...]
    another operation x1 -> x0, loops' own time: 54.3 us -> none  [attend(): lax.map(one_item, jnp.arange(block_count * kv_heads, dtype=jnp.int32))]
    all_to_all x1 -> x0, blocking collectives: 51.2 us -> none  [sum_at_owner(): lax.all_to_all(split_up(shard, dim, devices), axis, 0, 0, tiled=True)]
    all_gather x1 -> x0, waiting for transfers between devices: 40.4 us -> none  [gather_axes(): shard = lax.all_gather(shard, axis, axis=dim, tiled=True)]
    all_to_all x2 -> x0, waiting for transfers between devices: 24.8 us -> none  [the longest x1 24.8 us: relocate(): lax.all_to_all(packed, 'replica', split_axis=0, concat_axis=0, tiled=True)]
    dynamic_slice x65 -> x0, local copies, waits for them, and re-layouts: 19.8 us -> none  [the longest x16 9.42 us: attend(): lax.map(one_item, jnp.arange(block_count * kv_heads, dtype=jnp.int32))]
    reduce_sum x19 -> x3, other arithmetic: 18.1 us -> 1.26 us  [the longest x1 0.55 us: block_lists(): jnp.sum(jnp.where(hit, code[:, :, None, :] - empty, 0), axis=3) + empty]
  transfers between devices with their start and end apart: 3 -> 0, of which waited for: 2 -> 0; matrix products, arithmetic and copies ran while one was open for 4% -> 0% of each run, Pallas kernels for 0% -> 0%
where the time goes in v1:
time: 113 us
  Pallas kernels  102 us (90%)
  local copies, waits for them, and re-layouts  7.92 us (7%)
  other arithmetic  2.88 us (3%)
    pallas_call x1, Pallas kernels, gather(): pl.pallas_call(gather_kernel, out_shape=jax.ShapeDtypeStruct((2 * NZ, QB,...  50.6 us
    pallas_call x1, Pallas kernels, spread(): pl.pallas_call(spread_kernel, out_shape=[jax.ShapeDtypeStruct((NY, NX, QB...  24.1 us
    pallas_call x1, Pallas kernels, attend(): pl.pallas_call(attend_kernel, out_shape=jax.ShapeDtypeStruct((NY, QB, 32,...  18.4 us
    pallas_call x1, Pallas kernels, pick(): pl.pallas_call(pick_kernel, out_shape=jax.ShapeDtypeStruct((QB, ROWS, NX...  8.82 us
    unnamed x14, local copies, waits for them, and re-layouts  7.64 us

profile of v1, /device:TPU:1, one launch (start us, length us, event | category | flops | bytes accessed | tf_op | source)
XLA Modules:
  0.0 112.8 jit_solution(6066734838858027741)
XLA Ops:
  0.0 0.0 copy-start
  0.0 0.1 broadcast_compare_fusion.1
  0.1 0.1 add_add_fusion
  0.2 0.8 copy.17
  0.9 0.8 copy.18
  1.7 0.7 select_maximum_fusion.sc
  2.4 0.0 copy-done
  2.4 0.1 dynamic-slice_bitcast_fusion
  2.5 0.1 copy.14
  2.6 0.6 compare_reduce_fusion
  3.2 0.2 convert_reduce_fusion
  3.4 0.1 reduce_max.9
  3.5 0.5 select_reduce_fusion.1
  4.1 0.6 select_reduce_fusion
  4.7 0.1 add.121.ints
  4.7 24.1 %spread.1 = (bf16[4,4,4,8,896]{4,3,2,1,0:T(8,128)(2,1)}, bf16[4,1024,128]{2,1,0:T(8,128)(2,1)}, bf16[4,1024,128]{2,1,0:T(8,128)(2,1)}, f32[4,8,128]{2,1,0:T(8,128)}) custom-call(bf16[4,8,3584]{2,1,0:T(8,128)(2,1)} %q.1, bf16[1024,512]{1,0:T(8,128)(2,1)} %k.1, bf16[1024,512]{1,0:T(8,128)(2,1)} %v.1, f32[8,128]{1,0:T(8,128)} %select_maximum_fusion.sc), custom_call_target="tpu_custom_call" | custom-call | tf_op jit(solution)/shard_map/spread/pallas_call | solution.py:155
  28.8 0.0 copy-start.2
  28.9 1.2 %copy-done.2 = bf16[4,1024,128]{2,1,0:T(8,128)(2,1)S(1)} copy-done((bf16[4,1024,128]{2,1,0:T(8,128)(2,1)S(1)}, bf16[4,1024,128]{2,1,0:T(8,128)(2,1)}, u32[]{:S(2)}) %copy-start.2) | copy-done | bytes 1048600
  30.1 0.0 copy-start.3
  30.1 1.2 %copy-done.3 = bf16[4,1024,128]{2,1,0:T(8,128)(2,1)S(1)} copy-done((bf16[4,1024,128]{2,1,0:T(8,128)(2,1)S(1)}, bf16[4,1024,128]{2,1,0:T(8,128)(2,1)}, u32[]{:S(2)}) %copy-start.3) | copy-done | bytes 1048600
  31.3 0.0 copy-start.4
  31.3 1.2 %copy-done.4 = bf16[4,4,4,8,896]{4,3,2,1,0:T(8,128)(2,1)S(1)} copy-done((bf16[4,4,4,8,896]{4,3,2,1,0:T(8,128)(2,1)S(1)}, bf16[4,4,4,8,896]{4,3,2,1,0:T(8,128)(2,1)}, u32[]{:S(2)}) %copy-start.4) | copy-done | bytes 917528
  32.5 0.0 copy-start.5
  32.5 0.7 copy-done.5
  33.2 18.4 %attend.1.p = bf16[4,4,32,1024]{3,2,1,0:T(8,128)(2,1)S(1)} custom-call(s32[896]{0:T(1024)S(1)} %add.121.ints, s32[4]{0:T(128)S(1)} %and_select_fusion.steps, s32[1]{0:T(128)} %bitcast.2.where_x, bf16[4,4,4,8,896]{4,3,2,1,0:T(8,128)(2,1)S(1)} %copy-done.4, bf16[32,128,128]{2,1,0:T(8,128)(2,1)S(1)} %bitcast.8, bf16[32,128,128]{2,1,0:T(8,128)(2,1)S(1)} %bitcast.9, ...), custom_call_target="tpu_custom_call" | custom-call | tf_op jit(solution)/shard_map/attend/pallas_call | solution.py:255
  51.6 50.6 %gather.1 = bf16[16,4,8,3584]{3,2,1,0:T(8,128)(2,1)S(1)} custom-call(bf16[4,4,32,1024]{3,2,1,0:T(8,128)(2,1)S(1)} %attend.1.p), custom_call_target="tpu_custom_call" | custom-call | tf_op jit(solution)/shard_map/gather/pallas_call | solution.py:408
  102.2 0.0 copy-start.1
  102.2 1.8 %copy-done.1 = bf16[16,4,8,3584]{3,2,1,0:T(8,128)(2,1)} copy-done((bf16[16,4,8,3584]{3,2,1,0:T(8,128)(2,1)}, bf16[16,4,8,3584]{3,2,1,0:T(8,128)(2,1)S(1)}, u32[]{:S(2)}) %copy-start.1) | copy-done | bytes 3670040
  104.0 8.8 %pick.1 = bf16[4,8,3584]{2,1,0:T(8,128)(2,1)} custom-call(s32[64]{0:T(128)} %target.1, s32[1]{0:T(128)} %bitcast.me, bf16[64,8,3584]{2,1,0:T(8,128)(2,1)} %bitcast.7), custom_call_target="tpu_custom_call" | custom-call | tf_op jit(solution)/shard_map/pick/pallas_call | solution.py:446
  (6 shorter events, 0.0 us)
Async XLA Ops:
  0.0 2.4 %copy-start = (s32[28,64,32]{1,2,0:T(8,128)S(1)}, s32[28,64,32]{1,2,0:T(8,128)}, u32[]{:S(2)}) copy-start(s32[28,64,32]{1,2,0:T(8,128)} %param.12) | copy-start | bytes 688132
  28.8 1.2 %copy-start.2 = (bf16[4,1024,128]{2,1,0:T(8,128)(2,1)S(1)}, bf16[4,1024,128]{2,1,0:T(8,128)(2,1)}, u32[]{:S(2)}) copy-start(bf16[4,1024,128]{2,1,0:T(8,128)(2,1)} %get-tuple-element.10) | copy-start | bytes 3145732
  30.1 1.2 %copy-start.3 = (bf16[4,1024,128]{2,1,0:T(8,128)(2,1)S(1)}, bf16[4,1024,128]{2,1,0:T(8,128)(2,1)}, u32[]{:S(2)}) copy-start(bf16[4,1024,128]{2,1,0:T(8,128)(2,1)} %get-tuple-element.11) | copy-start | bytes 3145732
  31.3 1.2 %copy-start.4 = (bf16[4,4,4,8,896]{4,3,2,1,0:T(8,128)(2,1)S(1)}, bf16[4,4,4,8,896]{4,3,2,1,0:T(8,128)(2,1)}, u32[]{:S(2)}) copy-start(bf16[4,4,4,8,896]{4,3,2,1,0:T(8,128)(2,1)} %get-tuple-element.9.q_ref) | copy-start | bytes 2752516
  32.5 0.7 copy-start.5
  102.2 1.8 %copy-start.1 = (bf16[16,4,8,3584]{3,2,1,0:T(8,128)(2,1)}, bf16[16,4,8,3584]{3,2,1,0:T(8,128)(2,1)S(1)}, u32[]{:S(2)}) copy-start(bf16[16,4,8,3584]{3,2,1,0:T(8,128)(2,1)S(1)} %gather.1) | copy-start | bytes 11010052

commit v2 on v0

v2 whole, which is shorter than its diff:
```python
import functools
import math

import jax
import jax.numpy as jnp
from jax import lax
from jax.experimental import pallas as pl
from jax.experimental.pallas import tpu as pltpu
from jax.sharding import PartitionSpec as P

MESH = pl.DeviceIdType.MESH
BF16 = jnp.bfloat16
F32 = jnp.float32
I32 = jnp.int32

NX = 4
NY = 4
NZ = 8
HEADS = 7
D = 128
B = 128
QB = 4
KB = 32
SHARD = 8
SLICE = HEADS * D
ROWS = B // (NX * NY)
PART = NX * ROWS
KEYS = SHARD * B
PAIRS = 32
SUM_LANE = 64
NEG = -(2.0**100)
STEP = 4
FIRST = 64
FAR = (1, 3, 2)
TO_LOG2 = math.log2(math.e) / math.sqrt(D)

DMA = pltpu.SemaphoreType.DMA
ANY = pl.BlockSpec(memory_space=pl.ANY)
VMEM = pl.BlockSpec(memory_space=pltpu.VMEM)
SMEM = pl.BlockSpec(memory_space=pltpu.SMEM)


def place():
    rep = lax.axis_index("replica")
    ctx = lax.axis_index("ctx")
    return rep, rep // 2, rep % 2, ctx // NY, ctx % NY


def greet(partners):
    barrier = pltpu.get_barrier_semaphore()
    for who in partners:
        pl.semaphore_signal(barrier, inc=1, device_id=who, device_id_type=MESH)
    pl.semaphore_wait(barrier, len(partners))


def remote(src, dst, send, recv, who):
    return pltpu.make_async_remote_copy(
        src_ref=src, dst_ref=dst, send_sem=send, recv_sem=recv, device_id=who, device_id_type=MESH
    )


def iota(shape, dim):
    return lax.broadcasted_iota(I32, shape, dim)


def block_lists(mine, rep, y):
    shape = (PAIRS, 128)
    lane, row = iota(shape, 1), iota(shape, 0)
    of_pair = sum((row >= n * HEADS).astype(I32) for n in range(1, QB))
    below = FIRST + rep * QB + of_pair - ((lane >> 3) * (SHARD * NY) + y * SHARD + (lane & 7))
    block = (lane >> 3) * (SHARD * NY) + y * SHARD + (lane & 7)
    hits = (below == 0).astype(I32)
    for e in range(mine.shape[1]):
        hits = hits | (jnp.broadcast_to(mine[:, e : e + 1], shape) == block).astype(I32)
    hits = jnp.where((below >= 0) & (lane < KB), hits, 0)
    upto = hits
    for s in (1, 2, 4, 8, 16):
        upto = upto + jnp.where(lane >= s, pltpu.roll(upto, s, 1), 0)
    slot = jnp.where(hits > 0, upto - 1, -1)
    code = lane + KB * below
    packed = jnp.full(shape, -KB * 1024, I32)
    for b in range(KB):
        at = jnp.broadcast_to(slot[:, b : b + 1], shape) == lane
        packed = jnp.where(at, jnp.broadcast_to(code[:, b : b + 1], shape), packed)
    number = jnp.broadcast_to(upto[:, KB - 1 : KB], shape)
    return jnp.where(lane == KB, number, packed)


def spread_kernel(
    q, k, v, ks, vs, mine,
    q_all, keys, values, factors, lists,
    k_land, v_land, scales, k_loc, v_loc,
    q_send, q_recv, y_send, y_recv, k_send, k_recv, v_send, v_recv, s_send, s_recv,
    kc_send, kc_recv, vc_send, vc_recv, own,
):
    rep, z, c, x, y = place()
    sib = (rep + 1 - 2 * c, x * NY + y)
    xs = [(x + d) % NX for d in range(NX)]
    back = [(x + NX - d) % NX for d in range(NX)]
    at_x = [(rep, xs[d] * NY + y) for d in range(NX)]
    at_y = [(rep, x * NY + (y + d) % NY) for d in range(NY)]
    half = pl.ds(pl.multiple_of(c * (KEYS // 2), KEYS // 2), KEYS // 2)

    def cols(d, n):
        return pl.ds(pl.multiple_of(xs[d] * n, n), n)

    own_q = q.at[:, :, cols(0, SLICE)]
    stay = [
        pltpu.make_async_copy(ks, k_loc, own.at[0]),
        pltpu.make_async_copy(vs, v_loc, own.at[1]),
        pltpu.make_async_copy(own_q, q_all.at[y, x], own.at[2]),
        pltpu.make_async_copy(k.at[:, cols(0, D)], k_land.at[0], own.at[3]),
        pltpu.make_async_copy(v.at[:, cols(0, D)], v_land.at[0], own.at[4]),
    ]
    for copy in stay:
        copy.start()
    greet([at_x[1], at_x[2], at_x[3], at_y[1], at_y[2], at_y[3], sib])

    qx, kx, vx, sx, kc, vc = ([None] * NX for _ in range(6))
    qy = [[None] * NY for _ in range(NX)]

    def over_y(d, src):
        for e in FAR:
            qy[d][e] = remote(src, q_all.at[y, back[d]], y_send.at[d, e], y_recv.at[d, e], at_y[e])
            qy[d][e].start()

    for d in FAR:
        qx[d] = remote(q.at[:, :, cols(d, SLICE)], q_all.at[y, x], q_send.at[d], q_recv.at[d], at_x[d])
        qx[d].start()
    over_y(0, own_q)
    for d in FAR:
        kx[d] = remote(k.at[half, cols(d, D)], k_land.at[d, half], k_send.at[d], k_recv.at[d], at_x[d])
        vx[d] = remote(v.at[half, cols(d, D)], v_land.at[d, half], v_send.at[d], v_recv.at[d], at_x[d])
        kx[d].start()
        vx[d].start()
    stay[0].wait()
    stay[1].wait()
    scales[0] = jnp.zeros((SHARD, 128), F32)
    scales[0, :, 0:NX] = k_loc[...]
    scales[0, :, NX : 2 * NX] = v_loc[...]
    for d in FAR:
        sx[d] = remote(scales.at[0], scales.at[d], s_send.at[d], s_recv.at[d], at_x[d])
        sx[d].start()
    for d in FAR:
        qx[d].wait_recv()
        over_y(d, q_all.at[y, back[d]])

    lists[...] = block_lists(mine[...], rep, y)

    lane = iota((SHARD, 128), 1)

    def column(tile, n):
        return jnp.sum(jnp.where(lane == n, tile, 0.0), axis=1, keepdims=True)

    def finish(d):
        tile = scales[d]
        for_keys = jnp.broadcast_to(column(tile, x) * TO_LOG2, (SHARD, 128))
        for_values = jnp.broadcast_to(column(tile, NX + x), (SHARD, 128))
        for b in range(SHARD):
            at = back[d] * SHARD + b
            factors[at] = jnp.broadcast_to(for_keys[b : b + 1], (8, 128))
            rows = slice(b * B, (b + 1) * B)
            keys[at] = k_land[d, rows].T
            values[at] = (v_land[d, rows].astype(F32) * for_values[b : b + 1]).astype(BF16)

    def hand_over(d):
        kx[d].wait_recv()
        kc[d] = remote(k_land.at[d, half], k_land.at[d, half], kc_send.at[d], kc_recv.at[d], sib)
        kc[d].start()
        vx[d].wait_recv()
        vc[d] = remote(v_land.at[d, half], v_land.at[d, half], vc_send.at[d], vc_recv.at[d], sib)
        vc[d].start()
        sx[d].wait_recv()

    def whole(d):
        kc[d].wait_recv()
        vc[d].wait_recv()

    for copy in stay[2:]:
        copy.wait()
    finish(0)
    hand_over(1)
    hand_over(3)
    whole(1)
    finish(1)
    hand_over(2)
    whole(3)
    finish(3)
    whole(2)
    finish(2)
    for d in range(NX):
        for e in FAR:
            qy[d][e].wait_recv()
            qy[d][e].wait_send()
    for d in FAR:
        for copy in (qx[d], kx[d], vx[d], sx[d], kc[d], vc[d]):
            copy.wait_send()


def spread(q, k, v, ks, vs, mine):
    return pl.pallas_call(
        spread_kernel,
        out_shape=[
            jax.ShapeDtypeStruct((NY, NX, QB, ROWS, SLICE), BF16),
            jax.ShapeDtypeStruct((KB, D, B), BF16),
            jax.ShapeDtypeStruct((KB, B, D), BF16),
            jax.ShapeDtypeStruct((KB, 8, 128), F32),
            jax.ShapeDtypeStruct((PAIRS, 128), I32),
        ],
        in_specs=[ANY] * 5 + [VMEM],
        out_specs=[VMEM] * 5,
        scratch_shapes=[
            pltpu.VMEM((NX, KEYS, D), BF16),
            pltpu.VMEM((NX, KEYS, D), BF16),
            pltpu.VMEM((NX, SHARD, 128), F32),
            pltpu.VMEM((SHARD, NX), F32),
            pltpu.VMEM((SHARD, NX), F32),
        ]
        + [DMA((NX,))] * 2
        + [DMA((NX, NY))] * 2
        + [DMA((NX,))] * 10
        + [DMA((5,))],
        compiler_params=pltpu.CompilerParams(
            collective_id=0, has_side_effects=True, vmem_limit_bytes=24 << 20
        ),
        name="spread",
    )(q, k, v, ks, vs, mine)


def attend_kernel(ints, q_ref, keys, values, factors, out, extra_out, qs, sc, mx, acc, su, extra):
    row = iota((B, B), 0)
    row = ((row >> 3) & 3) * PART + (row >> 5) * ROWS + (row & 7)
    lane = iota((B, B), 1)
    ahead = lane - row
    extra[...] = jnp.zeros((B, B), F32)

    @pl.loop(0, QB)
    def _(qb):
        qs[...] = q_ref[:, :, qb].astype(F32).reshape(B, SLICE).astype(BF16)
        mx[...] = jnp.full(mx.shape, NEG, F32)
        acc[...] = jnp.zeros(acc.shape, F32)
        su[...] = jnp.zeros(su.shape, F32)
        most = ints[qb * HEADS, KB]
        for h in range(1, HEADS):
            most = jnp.maximum(most, ints[qb * HEADS + h, KB])
        count = (most + STEP - 1) // STEP

        @pl.loop(0, count)
        def _(t):
            for h in range(HEADS):
                head = qs[:, h * D : (h + 1) * D]
                top = mx[h]
                for u in range(STEP):
                    code = ints[qb * HEADS + h, t * STEP + u]
                    kb = code & (KB - 1)
                    score = jnp.dot(head, keys[kb], preferred_element_type=F32)
                    factor = jnp.broadcast_to(factors[kb][None], (B // 8, 8, B)).reshape(B, B)
                    score = jnp.where(ahead <= (code >> 5) * B, score * factor, NEG)
                    sc[h, t * STEP + u] = score
                    top = jnp.maximum(top, score)
                mx[h] = top

        for h in range(HEADS):
            top = jnp.max(mx[h], axis=1, keepdims=True)
            mx[h] = jnp.broadcast_to(top, (B, B)).astype(BF16).astype(F32)

        @pl.loop(0, count)
        def _(t):
            for h in range(HEADS):
                top = mx[h]
                total = su[h]
                weights, columns = [], []
                for u in range(STEP):
                    code = ints[qb * HEADS + h, t * STEP + u]
                    weight = jnp.exp2(sc[h, t * STEP + u] - top)
                    total = total + weight
                    weights.append(weight.astype(BF16))
                    columns.append(values[code & (KB - 1)])
                su[h] = total
                for u in range(0, STEP, 2):
                    acc[h] += jnp.dot(
                        jnp.concatenate(weights[u : u + 2], axis=1),
                        jnp.concatenate(columns[u : u + 2], axis=0),
                        preferred_element_type=F32,
                    )

        tile = extra[...]
        for h in range(HEADS):
            tile = jnp.where(lane == qb * 8 + h, mx[h], tile)
            total = jnp.broadcast_to(jnp.sum(su[h], axis=1, keepdims=True), (B, B))
            tile = jnp.where(lane == SUM_LANE + qb * 8 + h, total, tile)
            part = acc[h].astype(BF16)
            for d in range(NY):
                out[d, qb, :, h * D : (h + 1) * D] = part[d * PART : (d + 1) * PART]
        extra[...] = tile

    for d in range(NY):
        extra_out[d] = extra[d * PART : (d + 1) * PART].astype(BF16)


def attend(lists, q_all, keys, values, factors):
    return pl.pallas_call(
        attend_kernel,
        out_shape=[
            jax.ShapeDtypeStruct((NY, QB, PART, SLICE), BF16),
            jax.ShapeDtypeStruct((NY, PART, 128), BF16),
        ],
        in_specs=[SMEM] + [VMEM] * 4,
        out_specs=[VMEM] * 2,
        scratch_shapes=[
            pltpu.VMEM((B, SLICE), BF16),
            pltpu.VMEM((HEADS, KB, B, B), F32),
            pltpu.VMEM((HEADS, B, B), F32),
            pltpu.VMEM((HEADS, B, D), F32),
            pltpu.VMEM((HEADS, B, B), F32),
            pltpu.VMEM((B, B), F32),
        ],
        compiler_params=pltpu.CompilerParams(vmem_limit_bytes=36 << 20),
        name="attend",
    )(lists, q_all, keys, values, factors)


def gather_kernel(
    target, p, extra_in, out, parts, extra, att, got, swap_out, swap_in,
    e_send, e_recv, y_send, y_recv, x_send, x_recv, z_send, z_recv, c_send, c_recv, own,
):
    rep, z, c, x, y = place()
    other = rep + 1 - 2 * c
    here = x * NY + y
    sib = (other, here)
    xs = [(x + d) % NX for d in range(NX)]
    ys = [(y + d) % NY for d in range(NY)]
    at_x = [(rep, xs[d] * NY + y) for d in range(NX)]
    at_y = [(rep, x * NY + ys[d]) for d in range(NY)]
    at_z = [(((z + d) % NZ) * 2 + c, here) for d in range(NZ)]
    greet(at_x[1:] + at_y[1:] + at_z[1:] + [sib])

    ex = [None] * NY
    py = [[None] * NY for _ in range(QB)]
    px = [[None] * NX for _ in range(QB)]
    pz = [[None] * NZ for _ in range(QB)]
    for d in FAR:
        ex[d] = remote(extra_in.at[ys[d]], extra.at[d], e_send.at[d], e_recv.at[d], at_y[d])
        ex[d].start()
    for b in range(QB):
        for d in FAR:
            py[b][d] = remote(p.at[ys[d], b], parts.at[d, b], y_send.at[b, d], y_recv.at[b, d], at_y[d])
            py[b][d].start()

    def look(j, state):
        code = target[j]
        mine = code == rep
        theirs = code == other
        found, passed, *at = state
        at = [
            jnp.where(hit & (n == s), j, a)
            for a, (hit, n, s) in zip(
                at,
                [(mine, found, s) for s in range(QB)] + [(theirs, passed, s) for s in range(QB)],
            )
        ]
        return (found + mine.astype(I32), passed + theirs.astype(I32), *at)

    _, _, *at = lax.fori_loop(0, 2 * NZ * QB, look, (jnp.int32(0),) * (2 + 2 * QB))
    to_keep, to_pass = at[:QB], at[QB:]

    for d in FAR:
        ex[d].wait_recv()
    marks = [extra_in[y].astype(F32)] + [extra[d].astype(F32) for d in range(1, NY)]
    top = functools.reduce(jnp.maximum, marks)
    shift = [jnp.exp2(e - top) for e in marks]
    total = sum(w * pltpu.roll(e, SUM_LANE, 1) for w, e in zip(shift, marks))
    lane = iota((PART, 128), 1)
    total = jnp.where((lane < QB * 8) & ((lane & 7) < HEADS), total, 1.0)
    ratio = [w / total for w in shift]
    mine = pl.ds(pl.multiple_of(x * SLICE, SLICE), SLICE)

    def combine(b):
        for d in FAR:
            py[b][d].wait_recv()
        for h in range(HEADS):
            cols = slice(h * D, (h + 1) * D)
            at = b * 8 + h
            value = sum(
                jnp.broadcast_to(ratio[d][:, at : at + 1], (PART, D))
                * (parts[d, b, :, cols] if d else p[y, b, :, cols]).astype(F32)
                for d in range(NY)
            )
            value = value.reshape(NX, ROWS, D).astype(BF16)
            for d in range(NX):
                att[b, d, :, cols] = value[d]
        for d in FAR:
            px[b][d] = remote(
                att.at[b, xs[d]], got.at[z, b, :, mine], x_send.at[b, d], x_recv.at[b, d], at_x[d]
            )
            px[b][d].start()
        px[b][0] = pltpu.make_async_copy(att.at[b, x], got.at[z, b, :, mine], own.at[b])
        px[b][0].start()

    def land(b):
        for d in FAR:
            px[b][d].wait_recv()
        px[b][0].wait()
        for d in (4, 3, 5, 2, 6, 1, 7):
            pz[b][d] = remote(got.at[z, b], got.at[z, b], z_send.at[b, d], z_recv.at[b, d], at_z[d])
            pz[b][d].start()

    for b in range(QB):
        combine(b)
        if b:
            land(b - 1)
    land(QB - 1)
    for b in range(QB):
        for d in range(1, NZ):
            pz[b][d].wait_recv()

    def where(j):
        return j >> 3, j & 3

    for s in range(QB):
        from_z, b = where(to_pass[s])
        swap_out[s] = got[from_z, b]
    cross = remote(swap_out, swap_in, c_send, c_recv, sib)
    cross.start()
    for s in range(QB):
        from_z, b = where(to_keep[s])
        out[s] = got[from_z, b]
    cross.wait_recv()
    for s in range(QB):
        here_too = ((to_keep[s] >> 2) & 1) == c
        out[s] = jnp.where(here_too, out[s], swap_in[s])

    cross.wait_send()
    for d in FAR:
        ex[d].wait_send()
    for b in range(QB):
        for d in FAR:
            py[b][d].wait_send()
            px[b][d].wait_send()
        for d in range(1, NZ):
            pz[b][d].wait_send()


def gather(target, p, extra):
    return pl.pallas_call(
        gather_kernel,
        out_shape=jax.ShapeDtypeStruct((QB, ROWS, NX * SLICE), BF16),
        in_specs=[SMEM, VMEM, VMEM],
        out_specs=VMEM,
        scratch_shapes=[
            pltpu.VMEM((NY, QB, PART, SLICE), BF16),
            pltpu.VMEM((NY, PART, 128), BF16),
            pltpu.VMEM((QB, NX, ROWS, SLICE), BF16),
            pltpu.VMEM((NZ, QB, ROWS, NX * SLICE), BF16),
            pltpu.VMEM((QB, ROWS, NX * SLICE), BF16),
            pltpu.VMEM((QB, ROWS, NX * SLICE), BF16),
        ]
        + [DMA((NY,))] * 2
        + [DMA((QB, NY))] * 2
        + [DMA((QB, NX))] * 2
        + [DMA((QB, NZ))] * 2
        + [DMA] * 2
        + [DMA((QB,))],
        compiler_params=pltpu.CompilerParams(
            collective_id=1, has_side_effects=True, vmem_limit_bytes=24 << 20
        ),
        name="gather",
    )(target, p, extra)


def per_device(queries, key_cache, value_cache, key_scale, value_scale, pattern, target):
    rep, z, c, x, y = place()
    listed = pattern.shape[2]
    mine = lax.dynamic_slice(pattern, (x * HEADS, rep * QB, 0), (HEADS, QB, listed))
    mine = jnp.transpose(mine, (1, 0, 2)).reshape(HEADS * QB, listed)
    mine = jnp.pad(mine, ((0, PAIRS - HEADS * QB), (0, 0)))
    q_all, keys, values, factors, lists = spread(
        queries, key_cache, value_cache, key_scale, value_scale, mine
    )
    part, extra = attend(lists, q_all, keys, values, factors)
    return gather(target, part, extra)


def solution(mesh):
    return jax.shard_map(
        per_device,
        mesh=mesh,
        in_specs=(
            P("replica", "ctx", None),
            P("ctx", None),
            P("ctx", None),
            P("ctx", None),
            P("ctx", None),
            P(),
            P(),
        ),
        out_specs=P("replica", "ctx", None),
        check_vma=False,
    )
```

time: 396 us -> 103 us (0.26)
  Pallas kernels: 0 us -> 97.5 us
  waiting for transfers between devices: 65.2 us -> 0 us
  blocking collectives: 65.1 us -> 0 us
  matrix products: 62.5 us -> 0 us
  other arithmetic: 60.2 us -> 0 us
  loops' own time: 54.3 us -> 0 us
  local copies, waits for them, and re-layouts: 55.8 us -> 5.03 us
  starting transfers between devices: 15.7 us -> 0 us
  between operations: 13.7 us -> 0.09 us
    pallas_call x0 -> x3, Pallas kernels: none -> 97.5 us  [the longest x1 62.2 us: gather(): pl.pallas_call(gather_kernel, out_shape=jax.ShapeDtypeStruct((QB, ROWS, N...]
    dot_general x34 -> x0, matrix products: 62.5 us -> none  [the longest x16 34 us: one_item(): jnp.einsum('krbt,btd->rkd', weight, value_head, preferred_element_type=jn...]
    another operation x1 -> x0, loops' own time: 54.3 us -> none  [attend(): lax.map(one_item, jnp.arange(block_count * kv_heads, dtype=jnp.int32))]
    all_to_all x1 -> x0, blocking collectives: 51.2 us -> none  [sum_at_owner(): lax.all_to_all(split_up(shard, dim, devices), axis, 0, 0, tiled=True)]
    all_gather x1 -> x0, waiting for transfers between devices: 40.4 us -> none  [gather_axes(): shard = lax.all_gather(shard, axis, axis=dim, tiled=True)]
    all_to_all x2 -> x0, waiting for transfers between devices: 24.8 us -> none  [the longest x1 24.8 us: relocate(): lax.all_to_all(packed, 'replica', split_axis=0, concat_axis=0, tiled=True)]
    dynamic_slice x65 -> x0, local copies, waits for them, and re-layouts: 19.8 us -> none  [the longest x16 9.42 us: attend(): lax.map(one_item, jnp.arange(block_count * kv_heads, dtype=jnp.int32))]
    reduce_sum x19 -> x0, other arithmetic: 18.1 us -> none  [the longest x16 17.3 us: one_item(): denom = jnp.transpose(jnp.sum(expo, axis=(2, 3)))]
  transfers between devices with their start and end apart: 3 -> 0, of which waited for: 2 -> 0; matrix products, arithmetic and copies ran while one was open for 4% -> 0% of each run, Pallas kernels for 0% -> 0%
where the time goes in v2:
time: 103 us
  Pallas kernels  97.5 us (95%)
  local copies, waits for them, and re-layouts  5.03 us (5%)
    pallas_call x1, Pallas kernels, gather(): pl.pallas_call(gather_kernel, out_shape=jax.ShapeDtypeStruct((QB, ROWS, N...  62.2 us
    pallas_call x1, Pallas kernels, spread(): pl.pallas_call(spread_kernel, out_shape=[jax.ShapeDtypeStruct((NY, NX, QB...  23.9 us
    pallas_call x1, Pallas kernels, attend(): pl.pallas_call(attend_kernel, out_shape=[jax.ShapeDtypeStruct((NY, QB, PA...  11.3 us
    unnamed x17, local copies, waits for them, and re-layouts  4.81 us

profile of v2, /device:TPU:1, one launch (start us, length us, event | category | flops | bytes accessed | tf_op | source)
XLA Modules:
  0.0 102.6 jit_solution(2865463703089035013)
XLA Ops:
  0.0 0.0 copy-start
  0.0 0.0 copy-start.5
  0.0 0.0 copy-start.6
  0.0 0.0 copy-start.3
  0.0 0.7 copy-done.5
  0.7 0.1 copy.12.ks
  0.8 0.0 copy-done.6
  0.8 0.1 copy.13.vs
  0.9 0.1 copy-done
  1.1 0.1 dynamic-slice_bitcast_fusion
  1.2 0.1 copy.11
  1.3 0.0 copy-done.3
  1.3 0.0 copy-start.1
  1.3 1.2 %copy-done.1 = bf16[1024,512]{1,0:T(8,128)(2,1)S(1)} copy-done((bf16[1024,512]{1,0:T(8,128)(2,1)S(1)}, bf16[1024,512]{1,0:T(8,128)(2,1)}, u32[]{:S(2)}) %copy-start.1) | copy-done | bytes 1048600
  2.5 0.0 copy-start.2
  2.5 1.2 %copy-done.2 = bf16[1024,512]{1,0:T(8,128)(2,1)S(1)} copy-done((bf16[1024,512]{1,0:T(8,128)(2,1)S(1)}, bf16[1024,512]{1,0:T(8,128)(2,1)}, u32[]{:S(2)}) %copy-start.2) | copy-done | bytes 1048600
  3.8 23.9 %spread.1 = (bf16[4,4,4,8,896]{4,3,2,1,0:T(8,128)(2,1)S(1)}, bf16[32,128,128]{2,1,0:T(8,128)(2,1)S(1)}, bf16[32,128,128]{2,1,0:T(8,128)(2,1)S(1)}, f32[32,8,128]{2,1,0:T(8,128)S(1)}, s32[32,128]{1,0:T(8,128)S(1)}) custom-call(bf16[4,8,3584]{2,1,0:T(8,128)(2,1)S(1)} %copy-done.3, bf16[1024,512]{1,0:T(8,128)(2,1)S(1)} %copy-done.1, ...), custom_call_target="tpu_custom_call" | custom-call | tf_op jit(solution)/shard_map/spread/pallas_call | solution.py:201
  27.6 11.3 %attend.1 = (bf16[4,4,32,896]{3,2,1,0:T(8,128)(2,1)S(1)}, bf16[4,32,128]{2,1,0:T(8,128)(2,1)S(1)}) custom-call(s32[32,128]{1,0:T(8,128)S(1)} %get-tuple-element.12.ints, bf16[4,4,4,8,896]{4,3,2,1,0:T(8,128)(2,1)S(1)} %get-tuple-element.13.q_ref, bf16[32,128,128]{2,1,0:T(8,128)(2,1)S(1)} %get-tuple-element.14.keys, ...), custom_call_target="tpu_custom_call" | custom-call | tf_op jit(solution)/shard_map/attend/pallas_call | solution.py:302
  39.0 0.0 copy-start.4
  39.0 0.6 copy-done.4
  39.6 62.2 %gather.1 = bf16[4,8,3584]{2,1,0:T(8,128)(2,1)S(1)} custom-call(s32[64]{0:T(128)S(1)} %copy-done.4, bf16[4,4,32,896]{3,2,1,0:T(8,128)(2,1)S(1)} %get-tuple-element.17.p, bf16[4,32,128]{2,1,0:T(8,128)(2,1)S(1)} %get-tuple-element.18.extra_in), custom_call_target="tpu_custom_call" | custom-call | tf_op jit(solution)/shard_map/gather/pallas_call | solution.py:445
  101.9 0.7 copy.15
  (2 shorter events, 0.0 us)
Async XLA Ops:
  0.0 1.1 %copy-start = (s32[28,64,32]{1,2,0:T(8,128)S(1)}, s32[28,64,32]{1,2,0:T(8,128)}, u32[]{:S(2)}) copy-start(s32[28,64,32]{1,2,0:T(8,128)} %param.12) | copy-start | bytes 688132
  0.0 0.7 copy-start.5
  0.0 0.8 copy-start.6
  0.0 1.3 %copy-start.3 = (bf16[4,8,3584]{2,1,0:T(8,128)(2,1)S(1)}, bf16[4,8,3584]{2,1,0:T(8,128)(2,1)}, u32[]{:S(2)}) copy-start(bf16[4,8,3584]{2,1,0:T(8,128)(2,1)} %q.1) | copy-start | bytes 688132
  1.3 1.2 %copy-start.1 = (bf16[1024,512]{1,0:T(8,128)(2,1)S(1)}, bf16[1024,512]{1,0:T(8,128)(2,1)}, u32[]{:S(2)}) copy-start(bf16[1024,512]{1,0:T(8,128)(2,1)} %k.1) | copy-start | bytes 3145732
  2.5 1.2 %copy-start.2 = (bf16[1024,512]{1,0:T(8,128)(2,1)S(1)}, bf16[1024,512]{1,0:T(8,128)(2,1)}, u32[]{:S(2)}) copy-start(bf16[1024,512]{1,0:T(8,128)(2,1)} %v.1) | copy-start | bytes 3145732
  39.0 0.7 copy-start.4

commit v3 on v2

v3 whole, which is shorter than its diff:
```python
import functools
import math

import jax
import jax.numpy as jnp
from jax import lax
from jax.experimental import pallas as pl
from jax.experimental.pallas import tpu as pltpu
from jax.sharding import PartitionSpec as P

MESH = pl.DeviceIdType.MESH
BF16 = jnp.bfloat16
F32 = jnp.float32
I32 = jnp.int32

NX = 4
NY = 4
NZ = 8
HEADS = 7
D = 128
B = 128
QB = 4
KB = 32
SHARD = 8
SLICE = HEADS * D
ROWS = B // (NX * NY)
PART = NX * ROWS
KEYS = SHARD * B
PAIRS = 32
SUM_LANE = 64
NEG = -(2.0**100)
STEP = 4
FIRST = 64
FAR = (1, 3, 2)
CHUNKS = ((2, 1), (3, 0))
ORDER = (8, 9, 6, 7, 10, 11, 4, 5, 12, 13, 2, 3, 14, 15, 1, 0)
TO_LOG2 = math.log2(math.e) / math.sqrt(D)

DMA = pltpu.SemaphoreType.DMA
HBM = pl.BlockSpec(memory_space=pltpu.HBM)
VMEM = pl.BlockSpec(memory_space=pltpu.VMEM)
SMEM = pl.BlockSpec(memory_space=pltpu.SMEM)


def place():
    rep = lax.axis_index("replica")
    ctx = lax.axis_index("ctx")
    return rep, rep // 2, rep % 2, ctx // NY, ctx % NY


def greet(partners):
    barrier = pltpu.get_barrier_semaphore()
    for who in partners:
        pl.semaphore_signal(barrier, inc=1, device_id=who, device_id_type=MESH)
    pl.semaphore_wait(barrier, len(partners))


def remote(src, dst, send, recv, who):
    return pltpu.make_async_remote_copy(
        src_ref=src, dst_ref=dst, send_sem=send, recv_sem=recv, device_id=who, device_id_type=MESH
    )


def iota(shape, dim):
    return lax.broadcasted_iota(I32, shape, dim)


def block_lists(listed, blocks, y):
    shape = (PAIRS, 128)
    lane, row = iota(shape, 1), iota(shape, 0)
    block = (lane >> 3) * (SHARD * NY) + y * SHARD + (lane & 7)
    hits = jnp.zeros(shape, I32)
    own = jnp.zeros(shape, I32)
    column = iota(listed.shape[1:], 1)
    for s in range(QB):
        own = jnp.where(row >> 3 == s, blocks[s], own)
        for h in range(HEADS):
            entry = jnp.max(jnp.where(column == blocks[s], listed[h], -1), axis=1, keepdims=True)
            found = (jnp.broadcast_to(entry, shape) == block).astype(I32)
            found = jnp.max(found, axis=0, keepdims=True)
            hits = jnp.where(row == s * 8 + h, found, hits)
    below = FIRST + own - block
    hits = jnp.where(below == 0, 1, hits)
    hits = jnp.where((below >= 0) & (lane < KB) & ((row & 7) < HEADS), hits, 0)
    upto = hits
    for s in (1, 2, 4, 8, 16):
        upto = upto + jnp.where(lane >= s, pltpu.roll(upto, s, 1), 0)
    slot = jnp.where(hits > 0, upto - 1, -1)
    code = lane + KB * below
    packed = jnp.full(shape, -KB * 1024, I32)
    for b in range(KB):
        at = jnp.broadcast_to(slot[:, b : b + 1], shape) == lane
        packed = jnp.where(at, jnp.broadcast_to(code[:, b : b + 1], shape), packed)
    number = jnp.broadcast_to(upto[:, KB - 1 : KB], shape)
    return jnp.where(lane == KB, number, packed)


def spread_kernel(
    target, q, k, v, ks, vs, pattern,
    q_all, keys, values, factors, lists,
    q_loc, packed, first, second, chosen, k_land, v_land, scales, k_loc, v_loc, listed,
    z_send, z_recv, q_send, q_recv, y_send, y_recv, k_send, k_recv, v_send, v_recv, s_send, s_recv,
    kc_send, kc_recv, vc_send, vc_recv, own,
):
    rep, z, c, x, y = place()
    sib = (rep + 1 - 2 * c, x * NY + y)
    xs = [(x + d) % NX for d in range(NX)]
    back = [(x + NX - d) % NX for d in range(NX)]
    at_x = [(rep, xs[d] * NY + y) for d in range(NX)]
    at_y = [(rep, x * NY + (y + d) % NY) for d in range(NY)]
    half = pl.ds(pl.multiple_of(c * (KEYS // 2), KEYS // 2), KEYS // 2)
    groups = [((z + d) % NZ) * 2 + (c + e) % 2 for d in range(NZ) for e in range(2)]
    at_group = [(g, x * NY + y) for g in groups]

    arrived = (first, second)

    def cols(d, n):
        return pl.ds(pl.multiple_of(xs[d] * n, n), n)

    stay = [
        pltpu.make_async_copy(q, q_loc, own.at[0]),
        pltpu.make_async_copy(ks, k_loc, own.at[1]),
        pltpu.make_async_copy(vs, v_loc, own.at[2]),
        pltpu.make_async_copy(pattern.at[pl.ds(x * HEADS, HEADS)], listed, own.at[3]),
        pltpu.make_async_copy(k.at[:, cols(0, D)], k_land.at[0], own.at[4]),
        pltpu.make_async_copy(v.at[:, cols(0, D)], v_land.at[0], own.at[5]),
    ]
    for copy in stay:
        copy.start()
    greet(at_group[1:] + at_x[1:] + at_y[1:])

    qx, kx, vx, sx, kc, vc = ([None] * NX for _ in range(6))
    qy = [[None] * NY for _ in range(NX)]
    qz = [[None] * len(groups) for _ in CHUNKS]

    for d in FAR:
        kx[d] = remote(k.at[half, cols(d, D)], k_land.at[d, half], k_send.at[d], k_recv.at[d], at_x[d])
        vx[d] = remote(v.at[half, cols(d, D)], v_land.at[d, half], v_send.at[d], v_recv.at[d], at_x[d])
        kx[d].start()
        vx[d].start()

    goes_to = [target[rep * QB + b] for b in range(QB)]
    stay[0].wait()
    for i, chunk in enumerate(CHUNKS):
        for n in ORDER:
            b = jnp.int32(0)
            for other in range(1, QB):
                b = jnp.where(goes_to[other] == groups[n], other, b)
            for j, d in enumerate(chunk):
                block = q_loc[b, :, cols(d, SLICE)]
                if n == 0:
                    arrived[i][n, j] = block
                else:
                    packed[i, n, j] = block
            if n > 0:
                qz[i][n] = remote(
                    packed.at[i, n], arrived[i].at[n], z_send.at[i, n], z_recv.at[i, n], at_group[n]
                )
                qz[i][n].start()

    stay[1].wait()
    stay[2].wait()
    scales[0] = jnp.zeros((2 * NX, 128), F32)
    scales[0, 0:NX, 0:SHARD] = k_loc[...]
    scales[0, NX : 2 * NX, 0:SHARD] = v_loc[...]
    for d in FAR:
        sx[d] = remote(scales.at[0], scales.at[d], s_send.at[d], s_recv.at[d], at_x[d])
        sx[d].start()

    def look(j, state):
        found, *at = state
        hit = target[j] == rep
        at = [jnp.where(hit & (found == s), j, a) for s, a in enumerate(at)]
        return (found + hit.astype(I32), *at)

    _, *blocks = lax.fori_loop(0, 2 * NZ * QB, look, (jnp.int32(0),) * (1 + QB))
    stay[3].wait()
    lists[...] = block_lists(listed, blocks, y)

    scale_row = iota((2 * NX, 128), 0)

    def pick_row(tile, n):
        return jnp.sum(jnp.where(scale_row == n, tile, 0.0), axis=0, keepdims=True)

    def finish(d):
        tile = scales[d]
        for_keys = pick_row(tile, x) * TO_LOG2
        for_values = pick_row(tile, NX + x)
        for b in range(SHARD):
            at = back[d] * SHARD + b
            factors[at] = jnp.broadcast_to(for_keys[:, b : b + 1], (8, 128))
            rows = slice(b * B, (b + 1) * B)
            keys[at] = k_land[d, rows].T
            scaled = v_land[d, rows].astype(F32) * jnp.broadcast_to(for_values[:, b : b + 1], (B, D))
            values[at] = scaled.astype(BF16)

    def hand_over(d):
        kx[d].wait_recv()
        kc[d] = remote(k_land.at[d, half], k_land.at[d, half], kc_send.at[d], kc_recv.at[d], sib)
        kc[d].start()
        vx[d].wait_recv()
        vc[d] = remote(v_land.at[d, half], v_land.at[d, half], vc_send.at[d], vc_recv.at[d], sib)
        vc[d].start()
        sx[d].wait_recv()

    def whole(d):
        kc[d].wait_recv()
        vc[d].wait_recv()

    def over_y(d):
        for e in FAR:
            piece = q_all.at[y, back[d]]
            qy[d][e] = remote(piece, piece, y_send.at[d, e], y_recv.at[d, e], at_y[e])
            qy[d][e].start()

    def over_x(i):
        for n in range(1, len(groups)):
            qz[i][n].wait_recv()
        for j, d in enumerate(CHUNKS[i]):
            for s in range(QB):
                source = blocks[s] >> 2
                n = (((z + NZ - (source >> 1)) & (NZ - 1)) << 1) + ((source & 1) ^ c)
                block = arrived[i][n, j]
                if d == 0:
                    q_all[y, x, s] = block
                else:
                    chosen[d, s] = block
            if d == 0:
                over_y(0)
            else:
                qx[d] = remote(chosen.at[d], q_all.at[y, x], q_send.at[d], q_recv.at[d], at_x[d])
                qx[d].start()

    def from_x(i):
        for d in CHUNKS[i]:
            if d:
                qx[d].wait_recv()
                over_y(d)

    for copy in stay[4:]:
        copy.wait()
    finish(0)
    hand_over(1)
    hand_over(3)
    whole(1)
    finish(1)
    over_x(0)
    hand_over(2)
    from_x(0)
    whole(3)
    finish(3)
    whole(2)
    finish(2)
    over_x(1)
    from_x(1)
    for d in range(NX):
        for e in FAR:
            qy[d][e].wait_recv()
            qy[d][e].wait_send()
    for d in FAR:
        for copy in (qx[d], kx[d], vx[d], sx[d], kc[d], vc[d]):
            copy.wait_send()
    for copies in qz:
        for copy in copies[1:]:
            copy.wait_send()


def spread(target, q, k, v, ks, vs, pattern):
    pieces = (len(CHUNKS), 2 * NZ, len(CHUNKS[0]), ROWS, SLICE)
    return pl.pallas_call(
        spread_kernel,
        out_shape=[
            jax.ShapeDtypeStruct((NY, NX, QB, ROWS, SLICE), BF16),
            jax.ShapeDtypeStruct((KB, D, B), BF16),
            jax.ShapeDtypeStruct((KB, B, D), BF16),
            jax.ShapeDtypeStruct((KB, 8, 128), F32),
            jax.ShapeDtypeStruct((PAIRS, 128), I32),
        ],
        in_specs=[SMEM] + [HBM] * 6,
        out_specs=[VMEM] * 5,
        scratch_shapes=[
            pltpu.VMEM((QB, ROWS, NX * SLICE), BF16),
            pltpu.VMEM(pieces, BF16),
            pltpu.VMEM(pieces[1:], BF16),
            pltpu.VMEM(pieces[1:], BF16),
            pltpu.VMEM((NX, QB, ROWS, SLICE), BF16),
            pltpu.VMEM((NX, KEYS, D), BF16),
            pltpu.VMEM((NX, KEYS, D), BF16),
            pltpu.VMEM((NX, 2 * NX, 128), F32),
            pltpu.VMEM((NX, SHARD), F32),
            pltpu.VMEM((NX, SHARD), F32),
            pltpu.VMEM((HEADS, *pattern.shape[1:]), I32),
        ]
        + [DMA((len(CHUNKS), 2 * NZ))] * 2
        + [DMA((NX,))] * 2
        + [DMA((NX, NY))] * 2
        + [DMA((NX,))] * 10
        + [DMA((6,))],
        compiler_params=pltpu.CompilerParams(
            collective_id=0, has_side_effects=True, vmem_limit_bytes=50 << 20
        ),
        name="spread",
    )(target, q, k, v, ks, vs, pattern)


def attend_kernel(ints, q_ref, keys, values, factors, out, extra_out, qs, sc, mx, acc, su, extra):
    row = iota((B, B), 0)
    row = ((row >> 3) & 3) * PART + (row >> 5) * ROWS + (row & 7)
    lane = iota((B, B), 1)
    ahead = lane - row
    extra[...] = jnp.zeros((B, B), F32)

    @pl.loop(0, QB)
    def _(qb):
        qs[...] = q_ref[:, :, qb].astype(F32).reshape(B, SLICE).astype(BF16)
        mx[...] = jnp.full(mx.shape, NEG, F32)
        acc[...] = jnp.zeros(acc.shape, F32)
        su[...] = jnp.zeros(su.shape, F32)
        most = ints[qb * 8, KB]
        for h in range(1, HEADS):
            most = jnp.maximum(most, ints[qb * 8 + h, KB])
        count = (most + STEP - 1) // STEP

        @pl.loop(0, count)
        def _(t):
            for h in range(HEADS):
                head = qs[:, h * D : (h + 1) * D]
                top = mx[h]
                for u in range(STEP):
                    code = ints[qb * 8 + h, t * STEP + u]
                    kb = code & (KB - 1)
                    score = jnp.dot(head, keys[kb], preferred_element_type=F32)
                    factor = jnp.broadcast_to(factors[kb][None], (B // 8, 8, B)).reshape(B, B)
                    score = jnp.where(ahead <= (code >> 5) * B, score * factor, NEG)
                    sc[h, t * STEP + u] = score
                    top = jnp.maximum(top, score)
                mx[h] = top

        for h in range(HEADS):
            top = jnp.max(mx[h], axis=1, keepdims=True)
            mx[h] = jnp.broadcast_to(top, (B, B)).astype(BF16).astype(F32)

        @pl.loop(0, count)
        def _(t):
            for h in range(HEADS):
                top = mx[h]
                total = su[h]
                weights, columns = [], []
                for u in range(STEP):
                    code = ints[qb * 8 + h, t * STEP + u]
                    weight = jnp.exp2(sc[h, t * STEP + u] - top)
                    total = total + weight
                    weights.append(weight.astype(BF16))
                    columns.append(values[code & (KB - 1)])
                su[h] = total
                for u in range(0, STEP, 2):
                    acc[h] += jnp.dot(
                        jnp.concatenate(weights[u : u + 2], axis=1),
                        jnp.concatenate(columns[u : u + 2], axis=0),
                        preferred_element_type=F32,
                    )

        tile = extra[...]
        for h in range(HEADS):
            tile = jnp.where(lane == qb * 8 + h, mx[h], tile)
            total = jnp.broadcast_to(jnp.sum(su[h], axis=1, keepdims=True), (B, B))
            tile = jnp.where(lane == SUM_LANE + qb * 8 + h, total, tile)
            part = acc[h].astype(BF16)
            for d in range(NY):
                out[d, qb, :, h * D : (h + 1) * D] = part[d * PART : (d + 1) * PART]
        extra[...] = tile

    for d in range(NY):
        extra_out[d] = extra[d * PART : (d + 1) * PART].astype(BF16)


def attend(lists, q_all, keys, values, factors):
    return pl.pallas_call(
        attend_kernel,
        out_shape=[
            jax.ShapeDtypeStruct((NY, QB, PART, SLICE), BF16),
            jax.ShapeDtypeStruct((NY, PART, 128), BF16),
        ],
        in_specs=[SMEM] + [VMEM] * 4,
        out_specs=[VMEM] * 2,
        scratch_shapes=[
            pltpu.VMEM((B, SLICE), BF16),
            pltpu.VMEM((HEADS, KB, B, B), F32),
            pltpu.VMEM((HEADS, B, B), F32),
            pltpu.VMEM((HEADS, B, D), F32),
            pltpu.VMEM((HEADS, B, B), F32),
            pltpu.VMEM((B, B), F32),
        ],
        compiler_params=pltpu.CompilerParams(vmem_limit_bytes=36 << 20),
        name="attend",
    )(lists, q_all, keys, values, factors)


def gather_kernel(
    p, extra_in, out, parts, extra, att, e_send, e_recv, y_send, y_recv, x_send, x_recv, own
):
    rep, z, c, x, y = place()
    xs = [(x + d) % NX for d in range(NX)]
    ys = [(y + d) % NY for d in range(NY)]
    at_x = [(rep, xs[d] * NY + y) for d in range(NX)]
    at_y = [(rep, x * NY + ys[d]) for d in range(NY)]
    greet(at_x[1:] + at_y[1:])

    ex = [None] * NY
    py = [[None] * NY for _ in range(QB)]
    px = [[None] * NX for _ in range(QB)]
    for d in FAR:
        ex[d] = remote(extra_in.at[ys[d]], extra.at[d], e_send.at[d], e_recv.at[d], at_y[d])
        ex[d].start()
    for b in range(QB):
        for d in FAR:
            py[b][d] = remote(p.at[ys[d], b], parts.at[d, b], y_send.at[b, d], y_recv.at[b, d], at_y[d])
            py[b][d].start()
    for d in FAR:
        ex[d].wait_recv()
    marks = [extra_in[y].astype(F32)] + [extra[d].astype(F32) for d in range(1, NY)]
    top = functools.reduce(jnp.maximum, marks)
    shift = [jnp.exp2(e - top) for e in marks]
    total = sum(w * pltpu.roll(e, SUM_LANE, 1) for w, e in zip(shift, marks))
    lane = iota((PART, 128), 1)
    total = jnp.where((lane < QB * 8) & ((lane & 7) < HEADS), total, 1.0)
    ratio = [w / total for w in shift]
    mine = pl.ds(pl.multiple_of(x * SLICE, SLICE), SLICE)

    for b in range(QB):
        for d in FAR:
            py[b][d].wait_recv()
        for h in range(HEADS):
            cols = slice(h * D, (h + 1) * D)
            at = b * 8 + h
            value = sum(
                jnp.broadcast_to(ratio[d][:, at : at + 1], (PART, D))
                * (parts[d, b, :, cols] if d else p[y, b, :, cols]).astype(F32)
                for d in range(NY)
            )
            value = value.reshape(NX, ROWS, D).astype(BF16)
            for d in range(NX):
                att[b, d, :, cols] = value[d]
        for d in FAR:
            px[b][d] = remote(
                att.at[b, xs[d]], out.at[b, :, mine], x_send.at[b, d], x_recv.at[b, d], at_x[d]
            )
            px[b][d].start()
        px[b][0] = pltpu.make_async_copy(att.at[b, x], out.at[b, :, mine], own.at[b])
        px[b][0].start()

    for d in FAR:
        ex[d].wait_send()
    for b in range(QB):
        px[b][0].wait()
        for d in FAR:
            px[b][d].wait_recv()
            px[b][d].wait_send()
            py[b][d].wait_send()


def gather(p, extra):
    return pl.pallas_call(
        gather_kernel,
        out_shape=jax.ShapeDtypeStruct((QB, ROWS, NX * SLICE), BF16),
        in_specs=[VMEM, VMEM],
        out_specs=VMEM,
        scratch_shapes=[
            pltpu.VMEM((NY, QB, PART, SLICE), BF16),
            pltpu.VMEM((NY, PART, 128), BF16),
            pltpu.VMEM((QB, NX, ROWS, SLICE), BF16),
        ]
        + [DMA((NY,))] * 2
        + [DMA((QB, NY))] * 2
        + [DMA((QB, NX))] * 2
        + [DMA((QB,))],
        compiler_params=pltpu.CompilerParams(
            collective_id=1, has_side_effects=True, vmem_limit_bytes=16 << 20
        ),
        name="gather",
    )(p, extra)


def per_device(queries, key_cache, value_cache, key_scale, value_scale, pattern, target):
    q_all, keys, values, factors, lists = spread(
        target,
        queries,
        key_cache,
        value_cache,
        key_scale.T,
        value_scale.T,
        jnp.swapaxes(pattern, 1, 2),
    )
    part, extra = attend(lists, q_all, keys, values, factors)
    return gather(part, extra)


def solution(mesh):
    return jax.shard_map(
        per_device,
        mesh=mesh,
        in_specs=(
            P("replica", "ctx", None),
            P("ctx", None),
            P("ctx", None),
            P("ctx", None),
            P("ctx", None),
            P(),
            P(),
        ),
        out_specs=P("replica", "ctx", None),
        check_vma=False,
    )
```

time: 103 us -> 76.6 us (0.74)
  Pallas kernels: 97.5 us -> 72.9 us
  local copies, waits for them, and re-layouts: 5.03 us -> 3.34 us
    pallas_call x1, Pallas kernels: 62.2 us -> 18.4 us  [gather(): pl.pallas_call(gather_kernel, out_shape=jax.ShapeDtypeStruct((QB, ROWS, N...]
    pallas_call x1, Pallas kernels: 23.9 us -> 42.7 us  [spread(): pl.pallas_call(spread_kernel, out_shape=[jax.ShapeDtypeStruct((NY, NX, QB...]
    unnamed x17 -> x11, local copies, waits for them, and re-layouts: 4.81 us -> 3.34 us
where the time goes in v3:
time: 76.6 us; the launch traced here: 76.2 us
  Pallas kernels  72.9 us (95%)
  local copies, waits for them, and re-layouts  3.34 us (4%)
    pallas_call x1, Pallas kernels, spread(): pl.pallas_call(spread_kernel, out_shape=[jax.ShapeDtypeStruct((NY, NX, QB...  42.7 us
    pallas_call x1, Pallas kernels, gather(): pl.pallas_call(gather_kernel, out_shape=jax.ShapeDtypeStruct((QB, ROWS, N...  18.4 us
    pallas_call x1, Pallas kernels, attend(): pl.pallas_call(attend_kernel, out_shape=[jax.ShapeDtypeStruct((NY, QB, PA...  11.7 us
    unnamed x11, local copies, waits for them, and re-layouts  3.34 us

profile of v3, /device:TPU:1, one launch (start us, length us, event | category | flops | bytes accessed | tf_op | source)
XLA Modules:
  0.0 76.2 jit_solution(6381904247949925925)
XLA Ops:
  0.0 0.0 copy-start.3
  0.0 0.0 copy-start.2
  0.0 0.0 copy-start.4
  0.0 0.7 copy-done.3
  0.7 0.0 copy-done.2
  0.7 0.0 copy-done.4
  0.7 0.0 copy-start
  0.7 1.0 %copy-done = s32[28,64,32]{1,2,0:T(8,128)S(1)} copy-done((s32[28,64,32]{1,2,0:T(8,128)S(1)}, s32[28,64,32]{1,2,0:T(8,128)}, u32[]{:S(2)}) %copy-start) | copy-done | bytes 229400
  1.7 0.0 copy-start.1
  1.7 0.9 %copy-done.1 = bf16[4,8,3584]{2,1,0:T(8,128)(2,1)S(1)} copy-done((bf16[4,8,3584]{2,1,0:T(8,128)(2,1)S(1)}, bf16[4,8,3584]{2,1,0:T(8,128)(2,1)}, u32[]{:S(2)}) %copy-start.1) | copy-done | bytes 229400
  2.7 42.7 %spread.1 = (bf16[4,4,4,8,896]{4,3,2,1,0:T(8,128)(2,1)S(1)}, bf16[32,128,128]{2,1,0:T(8,128)(2,1)S(1)}, bf16[32,128,128]{2,1,0:T(8,128)(2,1)S(1)}, f32[32,8,128]{2,1,0:T(8,128)S(1)}, s32[32,128]{1,0:T(8,128)S(1)}) custom-call(s32[64]{0:T(128)S(1)} %copy-done.4, bf16[4,8,3584]{2,1,0:T(8,128)(2,1)S(1)} %copy-done.1, bf16[1024,512]{1,0:T(8,128)(2,1)} %k.1, ...), custom_call_target="tpu_custom_call" | custom-call | tf_op jit(solution)/shard_map/spread/pallas_call | solution.py:270
  45.4 11.7 %attend.1 = (bf16[4,4,32,896]{3,2,1,0:T(8,128)(2,1)S(1)}, bf16[4,32,128]{2,1,0:T(8,128)(2,1)S(1)}) custom-call(s32[32,128]{1,0:T(8,128)S(1)} %get-tuple-element.12.ints, bf16[4,4,4,8,896]{4,3,2,1,0:T(8,128)(2,1)S(1)} %get-tuple-element.13.q_ref, bf16[32,128,128]{2,1,0:T(8,128)(2,1)S(1)} %get-tuple-element.14.keys, ...), custom_call_target="tpu_custom_call" | custom-call | tf_op jit(solution)/shard_map/attend/pallas_call | solution.py:378
  57.1 18.4 %gather.1 = bf16[4,8,3584]{2,1,0:T(8,128)(2,1)S(1)} custom-call(bf16[4,4,32,896]{3,2,1,0:T(8,128)(2,1)S(1)} %get-tuple-element.17.p, bf16[4,32,128]{2,1,0:T(8,128)(2,1)S(1)} %get-tuple-element.18.extra_in), custom_call_target="tpu_custom_call" | custom-call | tf_op jit(solution)/shard_map/gather/pallas_call | solution.py:463
  75.5 0.7 copy.9
Async XLA Ops:
  0.0 0.7 copy-start.3
  0.0 0.7 copy-start.2
  0.0 0.7 copy-start.4
  0.7 1.0 %copy-start = (s32[28,64,32]{1,2,0:T(8,128)S(1)}, s32[28,64,32]{1,2,0:T(8,128)}, u32[]{:S(2)}) copy-start(s32[28,64,32]{1,2,0:T(8,128)} %param.12) | copy-start | bytes 688132
  1.7 0.9 %copy-start.1 = (bf16[4,8,3584]{2,1,0:T(8,128)(2,1)S(1)}, bf16[4,8,3584]{2,1,0:T(8,128)(2,1)}, u32[]{:S(2)}) copy-start(bf16[4,8,3584]{2,1,0:T(8,128)(2,1)} %q.1) | copy-start | bytes 688132

commit v4 on v3

--- a/solution.py
+++ b/solution.py
@@ -32,7 +32,6 @@
 STEP = 4
 FIRST = 64
 FAR = (1, 3, 2)
-CHUNKS = ((2, 1), (3, 0))
 ORDER = (8, 9, 6, 7, 10, 11, 4, 5, 12, 13, 2, 3, 14, 15, 1, 0)
 TO_LOG2 = math.log2(math.e) / math.sqrt(D)
 
@@ -98,7 +97,8 @@
 def spread_kernel(
     target, q, k, v, ks, vs, pattern,
     q_all, keys, values, factors, lists,
-    q_loc, packed, first, second, chosen, k_land, v_land, scales, k_loc, v_loc, listed,
+    held0, held1, held2, held3, packed, came0, came1, came2, came3,
+    k_land, v_land, scales, k_loc, v_loc, listed, goes,
     z_send, z_recv, q_send, q_recv, y_send, y_recv, k_send, k_recv, v_send, v_recv, s_send, s_recv,
     kc_send, kc_recv, vc_send, vc_recv, own,
 ):
@@ -111,70 +111,90 @@
     half = pl.ds(pl.multiple_of(c * (KEYS // 2), KEYS // 2), KEYS // 2)
     groups = [((z + d) % NZ) * 2 + (c + e) % 2 for d in range(NZ) for e in range(2)]
     at_group = [(g, x * NY + y) for g in groups]
-
-    arrived = (first, second)
+    held = (held0, held1, held2, held3)
+    came = (came0, came1, came2, came3)
 
     def cols(d, n):
         return pl.ds(pl.multiple_of(xs[d] * n, n), n)
 
+    partners = at_group[1:] + at_x[1:] + at_y[1:]
+    barrier = pltpu.get_barrier_semaphore()
+    for who in partners:
+        pl.semaphore_signal(barrier, inc=1, device_id=who, device_id_type=MESH)
     stay = [
-        pltpu.make_async_copy(q, q_loc, own.at[0]),
-        pltpu.make_async_copy(ks, k_loc, own.at[1]),
-        pltpu.make_async_copy(vs, v_loc, own.at[2]),
-        pltpu.make_async_copy(pattern.at[pl.ds(x * HEADS, HEADS)], listed, own.at[3]),
-        pltpu.make_async_copy(k.at[:, cols(0, D)], k_land.at[0], own.at[4]),
-        pltpu.make_async_copy(v.at[:, cols(0, D)], v_land.at[0], own.at[5]),
+        pltpu.make_async_copy(target, goes, own.at[0]),
+        pltpu.make_async_copy(q.at[:, :, cols(0, SLICE)], held[0], own.at[1]),
+        pltpu.make_async_copy(ks, k_loc, own.at[2]),
+        pltpu.make_async_copy(vs, v_loc, own.at[3]),
+        pltpu.make_async_copy(pattern.at[pl.ds(x * HEADS, HEADS)], listed, own.at[4]),
+        pltpu.make_async_copy(k.at[:, cols(0, D)], k_land.at[0], own.at[5]),
+        pltpu.make_async_copy(v.at[:, cols(0, D)], v_land.at[0], own.at[6]),
     ]
     for copy in stay:
         copy.start()
-    greet(at_group[1:] + at_x[1:] + at_y[1:])
 
     qx, kx, vx, sx, kc, vc = ([None] * NX for _ in range(6))
     qy = [[None] * NY for _ in range(NX)]
-    qz = [[None] * len(groups) for _ in CHUNKS]
-
+    qz = [[None] * len(groups) for _ in range(NX)]
+
+    stay[0].wait()
+    goes_to = [goes[rep * QB + b] for b in range(QB)]
+    leaving = []
+    for group in groups:
+        b = jnp.int32(0)
+        for other in range(1, QB):
+            b = jnp.where(goes_to[other] == group, other, b)
+        leaving.append(b)
+
+    def pack(d):
+        for n in ORDER:
+            block = held[d][leaving[n]]
+            if n == 0:
+                came[d][n] = block
+            else:
+                packed[d, n] = block
+
+    def over_z(d):
+        for n in ORDER[:-1]:
+            qz[d][n] = remote(packed.at[d, n], came[d].at[n], z_send.at[d, n], z_recv.at[d, n], at_group[n])
+            qz[d][n].start()
+
+    stay[1].wait()
+    pack(0)
+    scales[0] = jnp.zeros((2 * NX, 128), F32)
+    stay[2].wait()
+    stay[3].wait()
+    scales[0, 0:NX, 0:SHARD] = k_loc[...]
+    scales[0, NX : 2 * NX, 0:SHARD] = v_loc[...]
+
+    pl.semaphore_wait(barrier, len(partners))
+    for d in FAR:
+        qx[d] = remote(q.at[:, :, cols(d, SLICE)], held[d], q_send.at[d], q_recv.at[d], at_x[d])
+        qx[d].start()
+    over_z(0)
+    for d in FAR:
+        sx[d] = remote(scales.at[0], scales.at[d], s_send.at[d], s_recv.at[d], at_x[d])
+        sx[d].start()
     for d in FAR:
         kx[d] = remote(k.at[half, cols(d, D)], k_land.at[d, half], k_send.at[d], k_recv.at[d], at_x[d])
         vx[d] = remote(v.at[half, cols(d, D)], v_land.at[d, half], v_send.at[d], v_recv.at[d], at_x[d])
         kx[d].start()
         vx[d].start()
 
-    goes_to = [target[rep * QB + b] for b in range(QB)]
-    stay[0].wait()
-    for i, chunk in enumerate(CHUNKS):
-        for n in ORDER:
-            b = jnp.int32(0)
-            for other in range(1, QB):
-                b = jnp.where(goes_to[other] == groups[n], other, b)
-            for j, d in enumerate(chunk):
-                block = q_loc[b, :, cols(d, SLICE)]
-                if n == 0:
-                    arrived[i][n, j] = block
-                else:
-                    packed[i, n, j] = block
-            if n > 0:
-                qz[i][n] = remote(
-                    packed.at[i, n], arrived[i].at[n], z_send.at[i, n], z_recv.at[i, n], at_group[n]
-                )
-                qz[i][n].start()
-
-    stay[1].wait()
-    stay[2].wait()
-    scales[0] = jnp.zeros((2 * NX, 128), F32)
-    scales[0, 0:NX, 0:SHARD] = k_loc[...]
-    scales[0, NX : 2 * NX, 0:SHARD] = v_loc[...]
-    for d in FAR:
-        sx[d] = remote(scales.at[0], scales.at[d], s_send.at[d], s_recv.at[d], at_x[d])
-        sx[d].start()
-
     def look(j, state):
         found, *at = state
-        hit = target[j] == rep
+        hit = goes[j] == rep
         at = [jnp.where(hit & (found == s), j, a) for s, a in enumerate(at)]
         return (found + hit.astype(I32), *at)
 
     _, *blocks = lax.fori_loop(0, 2 * NZ * QB, look, (jnp.int32(0),) * (1 + QB))
-    stay[3].wait()
+
+    for d in FAR:
+        qx[d].wait_recv()
+        pack(d)
+        over_z(d)
+
+    stay[4].wait()
     lists[...] = block_lists(listed, blocks, y)
 
     scale_row = iota((2 * NX, 128), 0)
@@ -206,53 +226,33 @@
     def whole(d):
         kc[d].wait_recv()
         vc[d].wait_recv()
+        finish(d)
 
     def over_y(d):
+        for n in range(1, len(groups)):
+            qz[d][n].wait_recv()
+        for s in range(QB):
+            source = blocks[s] >> 2
+            n = (((z + NZ - (source >> 1)) & (NZ - 1)) << 1) + ((source & 1) ^ c)
+            q_all[y, back[d], s] = came[d][n]
         for e in FAR:
             piece = q_all.at[y, back[d]]
             qy[d][e] = remote(piece, piece, y_send.at[d, e], y_recv.at[d, e], at_y[e])
             qy[d][e].start()
 
-    def over_x(i):
-        for n in range(1, len(groups)):
-            qz[i][n].wait_recv()
-        for j, d in enumerate(CHUNKS[i]):
-            for s in range(QB):
-                source = blocks[s] >> 2
-                n = (((z + NZ - (source >> 1)) & (NZ - 1)) << 1) + ((source & 1) ^ c)
-                block = arrived[i][n, j]
-                if d == 0:
-                    q_all[y, x, s] = block
-                else:
-                    chosen[d, s] = block
-            if d == 0:
-                over_y(0)
-            else:
-                qx[d] = remote(chosen.at[d], q_all.at[y, x], q_send.at[d], q_recv.at[d], at_x[d])
-                qx[d].start()
-
-    def from_x(i):
-        for d in CHUNKS[i]:
-            if d:
-                qx[d].wait_recv()
-                over_y(d)
-
-    for copy in stay[4:]:
+    for copy in stay[5:]:
         copy.wait()
     finish(0)
     hand_over(1)
     hand_over(3)
+    over_y(0)
     whole(1)
-    finish(1)
-    over_x(0)
+    whole(3)
+    over_y(1)
     hand_over(2)
-    from_x(0)
-    whole(3)
-    finish(3)
     whole(2)
-    finish(2)
-    over_x(1)
-    from_x(1)
+    over_y(3)
+    over_y(2)
     for d in range(NX):
         for e in FAR:
             qy[d][e].wait_recv()
@@ -266,7 +266,7 @@
 
 
 def spread(target, q, k, v, ks, vs, pattern):
-    pieces = (len(CHUNKS), 2 * NZ, len(CHUNKS[0]), ROWS, SLICE)
+    slots = pltpu.VMEM((2 * NZ, ROWS, SLICE), BF16)
     return pl.pallas_call(
         spread_kernel,
         out_shape=[
@@ -276,28 +276,27 @@
             jax.ShapeDtypeStruct((KB, 8, 128), F32),
             jax.ShapeDtypeStruct((PAIRS, 128), I32),
         ],
-        in_specs=[SMEM] + [HBM] * 6,
+        in_specs=[HBM] * 7,
         out_specs=[VMEM] * 5,
-        scratch_shapes=[
-            pltpu.VMEM((QB, ROWS, NX * SLICE), BF16),
-            pltpu.VMEM(pieces, BF16),
-            pltpu.VMEM(pieces[1:], BF16),
-            pltpu.VMEM(pieces[1:], BF16),
-            pltpu.VMEM((NX, QB, ROWS, SLICE), BF16),
+        scratch_shapes=[pltpu.VMEM((QB, ROWS, SLICE), BF16)] * NX
+        + [pltpu.VMEM((NX, 2 * NZ, ROWS, SLICE), BF16)]
+        + [slots] * NX
+        + [
             pltpu.VMEM((NX, KEYS, D), BF16),
             pltpu.VMEM((NX, KEYS, D), BF16),
             pltpu.VMEM((NX, 2 * NX, 128), F32),
             pltpu.VMEM((NX, SHARD), F32),
             pltpu.VMEM((NX, SHARD), F32),
             pltpu.VMEM((HEADS, *pattern.shape[1:]), I32),
+            pltpu.SMEM(target.shape, I32),
         ]
-        + [DMA((len(CHUNKS), 2 * NZ))] * 2
+        + [DMA((NX, 2 * NZ))] * 2
         + [DMA((NX,))] * 2
         + [DMA((NX, NY))] * 2
         + [DMA((NX,))] * 10
-        + [DMA((6,))],
+        + [DMA((7,))],
         compiler_params=pltpu.CompilerParams(
-            collective_id=0, has_side_effects=True, vmem_limit_bytes=50 << 20
+            collective_id=0, has_side_effects=True, vmem_limit_bytes=24 << 20
         ),
         name="spread",
     )(target, q, k, v, ks, vs, pattern)
@@ -481,15 +480,19 @@
     )(p, extra)
 
 
+def hbm(array):
+    return pltpu.with_memory_space_constraint(array, pltpu.HBM)
+
+
 def per_device(queries, key_cache, value_cache, key_scale, value_scale, pattern, target):
     q_all, keys, values, factors, lists = spread(
-        target,
-        queries,
-        key_cache,
-        value_cache,
-        key_scale.T,
-        value_scale.T,
-        jnp.swapaxes(pattern, 1, 2),
+        hbm(target),
+        hbm(queries),
+        hbm(key_cache),
+        hbm(value_cache),
+        hbm(key_scale.T),
+        hbm(value_scale.T),
+        hbm(jnp.swapaxes(pattern, 1, 2)),
     )
     part, extra = attend(lists, q_all, keys, values, factors)
     return gather(part, extra)

time: 76.6 us -> 69.7 us (0.910)
  Pallas kernels: 72.9 us -> 68.9 us
  local copies, waits for them, and re-layouts: 3.34 us -> 0.69 us
    pallas_call x1, Pallas kernels: 42.7 us -> 38.7 us  [spread(): pl.pallas_call(spread_kernel, out_shape=[jax.ShapeDtypeStruct((NY, NX, QB...]
    unnamed x11 -> x1, local copies, waits for them, and re-layouts: 3.34 us -> 0.69 us
where the time goes in v4:
time: 69.7 us; the launch traced here: 69.6 us
  Pallas kernels  68.9 us (99%)
    pallas_call x1, Pallas kernels, spread(): pl.pallas_call(spread_kernel, out_shape=[jax.ShapeDtypeStruct((NY, NX, QB...  38.7 us
    pallas_call x1, Pallas kernels, gather(): pl.pallas_call(gather_kernel, out_shape=jax.ShapeDtypeStruct((QB, ROWS, N...  18.9 us
    pallas_call x1, Pallas kernels, attend(): pl.pallas_call(attend_kernel, out_shape=[jax.ShapeDtypeStruct((NY, QB, PA...  11.3 us

profile of v4, /device:TPU:1, one launch (start us, length us, event | category | flops | bytes accessed | tf_op | source)
XLA Modules:
  0.0 69.6 jit_solution(3794113730441143942)
XLA Ops:
  0.0 38.7 %spread.1 = (bf16[4,4,4,8,896]{4,3,2,1,0:T(8,128)(2,1)S(1)}, bf16[32,128,128]{2,1,0:T(8,128)(2,1)S(1)}, bf16[32,128,128]{2,1,0:T(8,128)(2,1)S(1)}, f32[32,8,128]{2,1,0:T(8,128)S(1)}, s32[32,128]{1,0:T(8,128)S(1)}) custom-call(s32[64]{0:T(128)} %target.1, bf16[4,8,3584]{2,1,0:T(8,128)(2,1)} %q.1, bf16[1024,512]{1,0:T(8,128)(2,1)} %k.1, bf16[1024,512]{1,0:T(8,128)(2,1)} %v.1, ...), custom_call_target="tpu_custom_call" | custom-call | tf_op jit(solution)/shard_map/spread/pallas_call | solution.py:270
  38.7 11.3 %attend.1 = (bf16[4,4,32,896]{3,2,1,0:T(8,128)(2,1)S(1)}, bf16[4,32,128]{2,1,0:T(8,128)(2,1)S(1)}) custom-call(s32[32,128]{1,0:T(8,128)S(1)} %get-tuple-element.12.ints, bf16[4,4,4,8,896]{4,3,2,1,0:T(8,128)(2,1)S(1)} %get-tuple-element.13.q_ref, bf16[32,128,128]{2,1,0:T(8,128)(2,1)S(1)} %get-tuple-element.14.keys, ...), custom_call_target="tpu_custom_call" | custom-call | tf_op jit(solution)/shard_map/attend/pallas_call | solution.py:377
  50.0 18.9 %gather.1 = bf16[4,8,3584]{2,1,0:T(8,128)(2,1)S(1)} custom-call(bf16[4,4,32,896]{3,2,1,0:T(8,128)(2,1)S(1)} %get-tuple-element.17.p, bf16[4,32,128]{2,1,0:T(8,128)(2,1)S(1)} %get-tuple-element.18.extra_in), custom_call_target="tpu_custom_call" | custom-call | tf_op jit(solution)/shard_map/gather/pallas_call | solution.py:462
  68.9 0.7 copy.9

commit v5 on v4

--- a/solution.py
+++ b/solution.py
@@ -32,7 +32,6 @@
 STEP = 4
 FIRST = 64
 FAR = (1, 3, 2)
-ORDER = (8, 9, 6, 7, 10, 11, 4, 5, 12, 13, 2, 3, 14, 15, 1, 0)
 TO_LOG2 = math.log2(math.e) / math.sqrt(D)
 
 DMA = pltpu.SemaphoreType.DMA
@@ -97,33 +96,35 @@
 def spread_kernel(
     target, q, k, v, ks, vs, pattern,
     q_all, keys, values, factors, lists,
-    held0, held1, held2, held3, packed, came0, came1, came2, came3,
+    ring0, ring1, ring2, ring3, give, take,
     k_land, v_land, scales, k_loc, v_loc, listed, goes,
-    z_send, z_recv, q_send, q_recv, y_send, y_recv, k_send, k_recv, v_send, v_recv, s_send, s_recv,
+    up_send, up_recv, dn_send, dn_recv, g_send, g_recv,
+    q_send, q_recv, y_send, y_recv, k_send, k_recv, v_send, v_recv, s_send, s_recv,
     kc_send, kc_recv, vc_send, vc_recv, own,
 ):
     rep, z, c, x, y = place()
-    sib = (rep + 1 - 2 * c, x * NY + y)
+    other = rep + 1 - 2 * c
+    here = x * NY + y
+    sib = (other, here)
     xs = [(x + d) % NX for d in range(NX)]
     back = [(x + NX - d) % NX for d in range(NX)]
     at_x = [(rep, xs[d] * NY + y) for d in range(NX)]
     at_y = [(rep, x * NY + (y + d) % NY) for d in range(NY)]
     half = pl.ds(pl.multiple_of(c * (KEYS // 2), KEYS // 2), KEYS // 2)
-    groups = [((z + d) % NZ) * 2 + (c + e) % 2 for d in range(NZ) for e in range(2)]
-    at_group = [(g, x * NY + y) for g in groups]
-    held = (held0, held1, held2, held3)
-    came = (came0, came1, came2, came3)
+    at_zup = (((z + 1) % NZ) * 2 + c, here)
+    at_zdn = (((z + NZ - 1) % NZ) * 2 + c, here)
+    ring = (ring0, ring1, ring2, ring3)
 
     def cols(d, n):
         return pl.ds(pl.multiple_of(xs[d] * n, n), n)
 
-    partners = at_group[1:] + at_x[1:] + at_y[1:]
+    partners = [at_zup, at_zdn, sib] + at_x[1:] + at_y[1:]
     barrier = pltpu.get_barrier_semaphore()
     for who in partners:
         pl.semaphore_signal(barrier, inc=1, device_id=who, device_id_type=MESH)
     stay = [
         pltpu.make_async_copy(target, goes, own.at[0]),
-        pltpu.make_async_copy(q.at[:, :, cols(0, SLICE)], held[0], own.at[1]),
+        pltpu.make_async_copy(q.at[:, :, cols(0, SLICE)], ring[0].at[0], own.at[1]),
         pltpu.make_async_copy(ks, k_loc, own.at[2]),
         pltpu.make_async_copy(vs, v_loc, own.at[3]),
         pltpu.make_async_copy(pattern.at[pl.ds(x * HEADS, HEADS)], listed, own.at[4]),
@@ -135,43 +136,57 @@
 
     qx, kx, vx, sx, kc, vc = ([None] * NX for _ in range(6))
     qy = [[None] * NY for _ in range(NX)]
-    qz = [[None] * len(groups) for _ in range(NX)]
-
-    stay[0].wait()
-    goes_to = [goes[rep * QB + b] for b in range(QB)]
-    leaving = []
-    for group in groups:
-        b = jnp.int32(0)
-        for other in range(1, QB):
-            b = jnp.where(goes_to[other] == group, other, b)
-        leaving.append(b)
-
-    def pack(d):
-        for n in ORDER:
-            block = held[d][leaving[n]]
-            if n == 0:
-                came[d][n] = block
-            else:
-                packed[d, n] = block
-
-    def over_z(d):
-        for n in ORDER[:-1]:
-            qz[d][n] = remote(packed.at[d, n], came[d].at[n], z_send.at[d, n], z_recv.at[d, n], at_group[n])
-            qz[d][n].start()
-
-    stay[1].wait()
-    pack(0)
+    zu, zd = ([[None] * 5 for _ in range(NX)] for _ in range(2))
+    handed = [None] * NX
+
     scales[0] = jnp.zeros((2 * NX, 128), F32)
     stay[2].wait()
     stay[3].wait()
     scales[0, 0:NX, 0:SHARD] = k_loc[...]
     scales[0, NX : 2 * NX, 0:SHARD] = v_loc[...]
 
+    stay[0].wait()
+
+    def look(j, state):
+        mine = goes[j] == rep
+        theirs = goes[j] == other
+        found, passed, *at = state
+        tests = [(mine, found, s) for s in range(QB)] + [(theirs, passed, s) for s in range(QB)]
+        at = [jnp.where(hit & (n == s), j, old) for old, (hit, n, s) in zip(at, tests)]
+        return (found + mine.astype(I32), passed + theirs.astype(I32), *at)
+
+    _, _, *at = lax.fori_loop(0, 2 * NZ * QB, look, (jnp.int32(0),) * (2 + 2 * QB))
+    blocks, to_give = at[:QB], at[QB:]
+
+    def over_z(d, k):
+        low, high = (pl.ds(0, QB // 2), pl.ds(QB // 2, QB // 2)) if k == 4 else (pl.ds(0, QB),) * 2
+        zu[d][k] = remote(
+            ring[d].at[k - 1, low], ring[d].at[k, low], up_send.at[d, k], up_recv.at[d, k], at_zup
+        )
+        zd[d][k] = remote(
+            ring[d].at[(NZ + 1 - k) % NZ, high], ring[d].at[NZ - k, high],
+            dn_send.at[d, k], dn_recv.at[d, k], at_zdn,
+        )
+        zu[d][k].start()
+        zd[d][k].start()
+
+    def onward(d, k):
+        zu[d][k].wait_recv()
+        zd[d][k].wait_recv()
+        if k < 4:
+            over_z(d, k + 1)
+        else:
+            for s in range(QB):
+                give[d, s] = ring[d][(z + NZ - (to_give[s] >> 3)) & (NZ - 1), to_give[s] & (QB - 1)]
+            handed[d] = remote(give.at[d], take.at[d], g_send.at[d], g_recv.at[d], sib)
+            handed[d].start()
+
+    stay[1].wait()
     pl.semaphore_wait(barrier, len(partners))
     for d in FAR:
-        qx[d] = remote(q.at[:, :, cols(d, SLICE)], held[d], q_send.at[d], q_recv.at[d], at_x[d])
+        qx[d] = remote(q.at[:, :, cols(d, SLICE)], ring[d].at[0], q_send.at[d], q_recv.at[d], at_x[d])
         qx[d].start()
-    over_z(0)
+    over_z(0, 1)
     for d in FAR:
         sx[d] = remote(scales.at[0], scales.at[d], s_send.at[d], s_recv.at[d], at_x[d])
         sx[d].start()
@@ -181,21 +196,9 @@
         kx[d].start()
         vx[d].start()
 
-    def look(j, state):
-        found, *at = state
-        hit = goes[j] == rep
-        at = [jnp.where(hit & (found == s), j, a) for s, a in enumerate(at)]
-        return (found + hit.astype(I32), *at)
-
-    _, *blocks = lax.fori_loop(0, 2 * NZ * QB, look, (jnp.int32(0),) * (1 + QB))
-
-    for d in FAR:
+    def from_x(d):
         qx[d].wait_recv()
-        pack(d)
-        over_z(d)
-
-    stay[4].wait()
-    lists[...] = block_lists(listed, blocks, y)
+        over_z(d, 1)
 
     scale_row = iota((2 * NX, 128), 0)
 
@@ -229,29 +232,48 @@
         finish(d)
 
     def over_y(d):
-        for n in range(1, len(groups)):
-            qz[d][n].wait_recv()
+        handed[d].wait_recv()
         for s in range(QB):
-            source = blocks[s] >> 2
-            n = (((z + NZ - (source >> 1)) & (NZ - 1)) << 1) + ((source & 1) ^ c)
-            q_all[y, back[d], s] = came[d][n]
+            near = ring[d][(z + NZ - (blocks[s] >> 3)) & (NZ - 1), blocks[s] & (QB - 1)]
+            q_all[y, back[d], s] = jnp.where(((blocks[s] >> 2) & 1) == c, near, take[d, s])
         for e in FAR:
             piece = q_all.at[y, back[d]]
             qy[d][e] = remote(piece, piece, y_send.at[d, e], y_recv.at[d, e], at_y[e])
             qy[d][e].start()
 
+    from_x(1)
+    onward(0, 1)
+    from_x(3)
+    onward(1, 1)
+    onward(0, 2)
+    from_x(2)
+    stay[4].wait()
+    lists[...] = block_lists(listed, blocks, y)
+    onward(3, 1)
+    onward(1, 2)
+    onward(0, 3)
+    onward(2, 1)
     for copy in stay[5:]:
         copy.wait()
     finish(0)
+    onward(3, 2)
+    onward(1, 3)
+    onward(0, 4)
     hand_over(1)
+    onward(2, 2)
+    onward(3, 3)
+    over_y(0)
     hand_over(3)
-    over_y(0)
     whole(1)
-    whole(3)
+    onward(1, 4)
+    onward(2, 3)
     over_y(1)
     hand_over(2)
+    onward(3, 4)
+    whole(3)
+    over_y(3)
+    onward(2, 4)
     whole(2)
-    over_y(3)
     over_y(2)
     for d in range(NX):
         for e in FAR:
@@ -260,13 +282,14 @@
     for d in FAR:
         for copy in (qx[d], kx[d], vx[d], sx[d], kc[d], vc[d]):
             copy.wait_send()
-    for copies in qz:
-        for copy in copies[1:]:
-            copy.wait_send()
+    for d in range(NX):
+        handed[d].wait_send()
+        for k in range(1, 5):
+            zu[d][k].wait_send()
+            zd[d][k].wait_send()
 
 
 def spread(target, q, k, v, ks, vs, pattern):
-    slots = pltpu.VMEM((2 * NZ, ROWS, SLICE), BF16)
     return pl.pallas_call(
         spread_kernel,
         out_shape=[
@@ -278,9 +301,8 @@
         ],
         in_specs=[HBM] * 7,
         out_specs=[VMEM] * 5,
-        scratch_shapes=[pltpu.VMEM((QB, ROWS, SLICE), BF16)] * NX
-        + [pltpu.VMEM((NX, 2 * NZ, ROWS, SLICE), BF16)]
-        + [slots] * NX
+        scratch_shapes=[pltpu.VMEM((NZ, QB, ROWS, SLICE), BF16)] * NX
+        + [pltpu.VMEM((NX, QB, ROWS, SLICE), BF16)] * 2
         + [
             pltpu.VMEM((NX, KEYS, D), BF16),
             pltpu.VMEM((NX, KEYS, D), BF16),
@@ -290,8 +312,8 @@
             pltpu.VMEM((HEADS, *pattern.shape[1:]), I32),
             pltpu.SMEM(target.shape, I32),
         ]
-        + [DMA((NX, 2 * NZ))] * 2
-        + [DMA((NX,))] * 2
+        + [DMA((NX, 5))] * 4
+        + [DMA((NX,))] * 4
         + [DMA((NX, NY))] * 2
         + [DMA((NX,))] * 10
         + [DMA((7,))],

time: 69.7 us -> 74.2 us (1.065)
  Pallas kernels: 68.9 us -> 73.1 us
    pallas_call x1, Pallas kernels: 38.7 us -> 45.1 us  [spread(): pl.pallas_call(spread_kernel, out_shape=[jax.ShapeDtypeStruct((NY, NX, QB...]
    pallas_call x1, Pallas kernels: 18.9 us -> 16.6 us  [gather(): pl.pallas_call(gather_kernel, out_shape=jax.ShapeDtypeStruct((QB, ROWS, N...]
where the time goes in v5:
time: 74.2 us; the launch traced here: 73.8 us
  Pallas kernels  73.1 us (99%)
    pallas_call x1, Pallas kernels, spread(): pl.pallas_call(spread_kernel, out_shape=[jax.ShapeDtypeStruct((NY, NX, QB...  45.1 us
    pallas_call x1, Pallas kernels, gather(): pl.pallas_call(gather_kernel, out_shape=jax.ShapeDtypeStruct((QB, ROWS, N...  16.6 us
    pallas_call x1, Pallas kernels, attend(): pl.pallas_call(attend_kernel, out_shape=[jax.ShapeDtypeStruct((NY, QB, PA...  11.4 us

profile of v5, /device:TPU:1, one launch (start us, length us, event | category | flops | bytes accessed | tf_op | source)
XLA Modules:
  0.0 73.8 jit_solution(11154171598277990222)
XLA Ops:
  0.0 45.1 %spread.1 = (bf16[4,4,4,8,896]{4,3,2,1,0:T(8,128)(2,1)S(1)}, bf16[32,128,128]{2,1,0:T(8,128)(2,1)S(1)}, bf16[32,128,128]{2,1,0:T(8,128)(2,1)S(1)}, f32[32,8,128]{2,1,0:T(8,128)S(1)}, s32[32,128]{1,0:T(8,128)S(1)}) custom-call(s32[64]{0:T(128)} %target.1, bf16[4,8,3584]{2,1,0:T(8,128)(2,1)} %q.1, bf16[1024,512]{1,0:T(8,128)(2,1)} %k.1, bf16[1024,512]{1,0:T(8,128)(2,1)} %v.1, ...), custom_call_target="tpu_custom_call" | custom-call | tf_op jit(solution)/shard_map/spread/pallas_call | solution.py:293
  45.1 11.4 %attend.1 = (bf16[4,4,32,896]{3,2,1,0:T(8,128)(2,1)S(1)}, bf16[4,32,128]{2,1,0:T(8,128)(2,1)S(1)}) custom-call(s32[32,128]{1,0:T(8,128)S(1)} %get-tuple-element.12.ints, bf16[4,4,4,8,896]{4,3,2,1,0:T(8,128)(2,1)S(1)} %get-tuple-element.13.q_ref, bf16[32,128,128]{2,1,0:T(8,128)(2,1)S(1)} %get-tuple-element.14.keys, ...), custom_call_target="tpu_custom_call" | custom-call | tf_op jit(solution)/shard_map/attend/pallas_call | solution.py:399
  56.5 16.6 %gather.1 = bf16[4,8,3584]{2,1,0:T(8,128)(2,1)S(1)} custom-call(bf16[4,4,32,896]{3,2,1,0:T(8,128)(2,1)S(1)} %get-tuple-element.17.p, bf16[4,32,128]{2,1,0:T(8,128)(2,1)S(1)} %get-tuple-element.18.extra_in), custom_call_target="tpu_custom_call" | custom-call | tf_op jit(solution)/shard_map/gather/pallas_call | solution.py:484
  73.1 0.7 copy.9

commit v6 on v4

--- a/solution.py
+++ b/solution.py
@@ -29,7 +29,9 @@
 PAIRS = 32
 SUM_LANE = 64
 NEG = -(2.0**100)
-STEP = 4
+STEP = 24
+TOGETHER = 2
+LANES = 8 * TOGETHER
 FIRST = 64
 FAR = (1, 3, 2)
 ORDER = (8, 9, 6, 7, 10, 11, 4, 5, 12, 13, 2, 3, 14, 15, 1, 0)
@@ -98,7 +100,7 @@
     target, q, k, v, ks, vs, pattern,
     q_all, keys, values, factors, lists,
     held0, held1, held2, held3, packed, came0, came1, came2, came3,
-    k_land, v_land, scales, k_loc, v_loc, listed, goes,
+    v_land, scales, k_loc, v_loc, listed, goes,
     z_send, z_recv, q_send, q_recv, y_send, y_recv, k_send, k_recv, v_send, v_recv, s_send, s_recv,
     kc_send, kc_recv, vc_send, vc_recv, own,
 ):
@@ -127,7 +129,7 @@
         pltpu.make_async_copy(ks, k_loc, own.at[2]),
         pltpu.make_async_copy(vs, v_loc, own.at[3]),
         pltpu.make_async_copy(pattern.at[pl.ds(x * HEADS, HEADS)], listed, own.at[4]),
-        pltpu.make_async_copy(k.at[:, cols(0, D)], k_land.at[0], own.at[5]),
+        pltpu.make_async_copy(k.at[:, cols(0, D)], keys.at[x], own.at[5]),
         pltpu.make_async_copy(v.at[:, cols(0, D)], v_land.at[0], own.at[6]),
     ]
     for copy in stay:
@@ -176,7 +178,7 @@
         sx[d] = remote(scales.at[0], scales.at[d], s_send.at[d], s_recv.at[d], at_x[d])
         sx[d].start()
     for d in FAR:
-        kx[d] = remote(k.at[half, cols(d, D)], k_land.at[d, half], k_send.at[d], k_recv.at[d], at_x[d])
+        kx[d] = remote(k.at[half, cols(d, D)], keys.at[x, half], k_send.at[d], k_recv.at[d], at_x[d])
         vx[d] = remote(v.at[half, cols(d, D)], v_land.at[d, half], v_send.at[d], v_recv.at[d], at_x[d])
         kx[d].start()
         vx[d].start()
@@ -210,13 +212,13 @@
             at = back[d] * SHARD + b
             factors[at] = jnp.broadcast_to(for_keys[:, b : b + 1], (8, 128))
             rows = slice(b * B, (b + 1) * B)
-            keys[at] = k_land[d, rows].T
             scaled = v_land[d, rows].astype(F32) * jnp.broadcast_to(for_values[:, b : b + 1], (B, D))
-            values[at] = scaled.astype(BF16)
+            values[at] = scaled.astype(BF16).T
 
     def hand_over(d):
         kx[d].wait_recv()
-        kc[d] = remote(k_land.at[d, half], k_land.at[d, half], kc_send.at[d], kc_recv.at[d], sib)
+        piece = keys.at[back[d], half]
+        kc[d] = remote(piece, piece, kc_send.at[d], kc_recv.at[d], sib)
         kc[d].start()
         vx[d].wait_recv()
         vc[d] = remote(v_land.at[d, half], v_land.at[d, half], vc_send.at[d], vc_recv.at[d], sib)
@@ -271,8 +273,8 @@
         spread_kernel,
         out_shape=[
             jax.ShapeDtypeStruct((NY, NX, QB, ROWS, SLICE), BF16),
+            jax.ShapeDtypeStruct((NX, KEYS, D), BF16),
             jax.ShapeDtypeStruct((KB, D, B), BF16),
-            jax.ShapeDtypeStruct((KB, B, D), BF16),
             jax.ShapeDtypeStruct((KB, 8, 128), F32),
             jax.ShapeDtypeStruct((PAIRS, 128), I32),
         ],
@@ -282,7 +284,6 @@
         + [pltpu.VMEM((NX, 2 * NZ, ROWS, SLICE), BF16)]
         + [slots] * NX
         + [
-            pltpu.VMEM((NX, KEYS, D), BF16),
             pltpu.VMEM((NX, KEYS, D), BF16),
             pltpu.VMEM((NX, 2 * NX, 128), F32),
             pltpu.VMEM((NX, SHARD), F32),
@@ -302,78 +303,93 @@
     )(target, q, k, v, ks, vs, pattern)
 
 
-def attend_kernel(ints, q_ref, keys, values, factors, out, extra_out, qs, sc, mx, acc, su, extra):
-    row = iota((B, B), 0)
+def attend_kernel(ints, q_ref, keys, values, factors, out, extra_out, qs, sc, mx, acc, su, extra, items):
+    row = iota((B, B), 1)
     row = ((row >> 3) & 3) * PART + (row >> 5) * ROWS + (row & 7)
-    lane = iota((B, B), 1)
-    ahead = lane - row
+    ahead = iota((B, B), 0) - row
     extra[...] = jnp.zeros((B, B), F32)
-
-    @pl.loop(0, QB)
-    def _(qb):
-        qs[...] = q_ref[:, :, qb].astype(F32).reshape(B, SLICE).astype(BF16)
+    qs[HEADS] = jnp.zeros((D, B), BF16)
+
+    def tall(tile):
+        return jnp.broadcast_to(tile[None], (B // 8, 8, B)).reshape(B, B)
+
+    @pl.loop(0, QB // TOGETHER)
+    def _(part_of):
+        def add_pair(r, n):
+            def add(t, n):
+                items[n] = r * 16 + t
+                return n + 1
+
+            return lax.fori_loop(0, (ints[part_of * LANES + r, KB] + 1) // 2, add, n)
+
+        n = lax.fori_loop(0, LANES, add_pair, jnp.int32(0))
+        for g in range(STEP):
+            items[n + g] = HEADS * 16
+        count = (n + STEP - 1) // STEP
+        for j in range(TOGETHER):
+            rows = q_ref[:, :, part_of * TOGETHER + j].astype(F32).reshape(B, SLICE).astype(BF16)
+            for h in range(HEADS):
+                qs[j * 8 + h] = rows[:, h * D : (h + 1) * D].T
         mx[...] = jnp.full(mx.shape, NEG, F32)
         acc[...] = jnp.zeros(acc.shape, F32)
         su[...] = jnp.zeros(su.shape, F32)
-        most = ints[qb * 8, KB]
-        for h in range(1, HEADS):
-            most = jnp.maximum(most, ints[qb * 8 + h, KB])
-        count = (most + STEP - 1) // STEP
+
+        def item_at(i, g):
+            item = items[i * STEP + g]
+            r, t = item >> 4, item & 15
+            codes = [ints[part_of * LANES + r, t * 2 + u] for u in range(2)]
+            return r, codes, [code & (KB - 1) for code in codes]
 
         @pl.loop(0, count)
-        def _(t):
+        def _(i):
+            for g in range(STEP):
+                r, codes, kbs = item_at(i, g)
+                both = jnp.dot(
+                    jnp.concatenate([keys[kb] for kb in kbs], axis=0), qs[r], preferred_element_type=F32
+                )
+                top = mx[r]
+                for u in range(2):
+                    score = both[u * B : (u + 1) * B] * tall(factors[kbs[u]])
+                    score = jnp.where(ahead <= (codes[u] >> 5) * B, score, NEG)
+                    sc[(i * STEP + g) * 2 + u] = score
+                    top = jnp.maximum(top, jnp.max(score.reshape(B // 8, 8, B), axis=0))
+                mx[r] = top
+
+        for j in range(TOGETHER):
             for h in range(HEADS):
-                head = qs[:, h * D : (h + 1) * D]
-                top = mx[h]
-                for u in range(STEP):
-                    code = ints[qb * 8 + h, t * STEP + u]
-                    kb = code & (KB - 1)
-                    score = jnp.dot(head, keys[kb], preferred_element_type=F32)
-                    factor = jnp.broadcast_to(factors[kb][None], (B // 8, 8, B)).reshape(B, B)
-                    score = jnp.where(ahead <= (code >> 5) * B, score * factor, NEG)
-                    sc[h, t * STEP + u] = score
-                    top = jnp.maximum(top, score)
-                mx[h] = top
-
-        for h in range(HEADS):
-            top = jnp.max(mx[h], axis=1, keepdims=True)
-            mx[h] = jnp.broadcast_to(top, (B, B)).astype(BF16).astype(F32)
+                top = jnp.max(mx[j * 8 + h], axis=0, keepdims=True)
+                mx[j * 8 + h] = jnp.broadcast_to(top, (8, B)).astype(BF16).astype(F32)
 
         @pl.loop(0, count)
-        def _(t):
+        def _(i):
+            for g in range(STEP):
+                r, codes, kbs = item_at(i, g)
+                top = tall(mx[r])
+                weights = [jnp.exp2(sc[(i * STEP + g) * 2 + u] - top) for u in range(2)]
+                su[r] += jnp.sum((weights[0] + weights[1]).reshape(B // 8, 8, B), axis=0)
+                acc[r] += jnp.dot(
+                    jnp.concatenate([values[kb] for kb in kbs], axis=1),
+                    jnp.concatenate([w.astype(BF16) for w in weights], axis=0),
+                    preferred_element_type=F32,
+                )
+
+        for j in range(TOGETHER):
             for h in range(HEADS):
-                top = mx[h]
-                total = su[h]
-                weights, columns = [], []
-                for u in range(STEP):
-                    code = ints[qb * 8 + h, t * STEP + u]
-                    weight = jnp.exp2(sc[h, t * STEP + u] - top)
-                    total = total + weight
-                    weights.append(weight.astype(BF16))
-                    columns.append(values[code & (KB - 1)])
-                su[h] = total
-                for u in range(0, STEP, 2):
-                    acc[h] += jnp.dot(
-                        jnp.concatenate(weights[u : u + 2], axis=1),
-                        jnp.concatenate(columns[u : u + 2], axis=0),
-                        preferred_element_type=F32,
-                    )
-
-        tile = extra[...]
-        for h in range(HEADS):
-            tile = jnp.where(lane == qb * 8 + h, mx[h], tile)
-            total = jnp.broadcast_to(jnp.sum(su[h], axis=1, keepdims=True), (B, B))
-            tile = jnp.where(lane == SUM_LANE + qb * 8 + h, total, tile)
-            part = acc[h].astype(BF16)
-            for d in range(NY):
-                out[d, qb, :, h * D : (h + 1) * D] = part[d * PART : (d + 1) * PART]
-        extra[...] = tile
-
+                r = j * 8 + h
+                at = part_of * LANES + r
+                extra[pl.ds(at, 1), :] = mx[r][0:1]
+                extra[pl.ds(SUM_LANE + at, 1), :] = jnp.sum(su[r], axis=0, keepdims=True)
+                part = acc[r].astype(BF16).T
+                for d in range(NY):
+                    out[d, part_of * TOGETHER + j, :, h * D : (h + 1) * D] = part[d * PART : (d + 1) * PART]
+
+    turned = extra[...].T
     for d in range(NY):
-        extra_out[d] = extra[d * PART : (d + 1) * PART].astype(BF16)
+        extra_out[d] = turned[d * PART : (d + 1) * PART].astype(BF16)
 
 
 def attend(lists, q_all, keys, values, factors):
+    most = TOGETHER * HEADS * KB // 2 + STEP
     return pl.pallas_call(
         attend_kernel,
         out_shape=[
@@ -383,16 +399,17 @@
         in_specs=[SMEM] + [VMEM] * 4,
         out_specs=[VMEM] * 2,
         scratch_shapes=[
-            pltpu.VMEM((B, SLICE), BF16),
-            pltpu.VMEM((HEADS, KB, B, B), F32),
-            pltpu.VMEM((HEADS, B, B), F32),
-            pltpu.VMEM((HEADS, B, D), F32),
-            pltpu.VMEM((HEADS, B, B), F32),
+            pltpu.VMEM((LANES, D, B), BF16),
+            pltpu.VMEM((2 * most, B, B), F32),
+            pltpu.VMEM((LANES, 8, B), F32),
+            pltpu.VMEM((LANES, D, B), F32),
+            pltpu.VMEM((LANES, 8, B), F32),
             pltpu.VMEM((B, B), F32),
+            pltpu.SMEM((most,), I32),
         ],
-        compiler_params=pltpu.CompilerParams(vmem_limit_bytes=36 << 20),
+        compiler_params=pltpu.CompilerParams(vmem_limit_bytes=46 << 20),
         name="attend",
-    )(lists, q_all, keys, values, factors)
+    )(lists, q_all, keys.reshape(KB, B, D), values, factors)
 
 
 def gather_kernel(

time: 69.7 us -> 68.8 us (0.987)
  Pallas kernels: 68.9 us -> 68 us
    pallas_call x1, Pallas kernels: 11.3 us -> 8 us  [attend(): pl.pallas_call(attend_kernel, out_shape=[jax.ShapeDtypeStruct((NY, QB, PA...]
    pallas_call x1, Pallas kernels: 18.9 us -> 21.3 us  [gather(): pl.pallas_call(gather_kernel, out_shape=jax.ShapeDtypeStruct((QB, ROWS, N...]
where the time goes in v6:
time: 68.8 us; the launch traced here: 68.7 us
  Pallas kernels  68 us (99%)
  local copies, waits for them, and re-layouts  0.69 us (1%)
    pallas_call x1, Pallas kernels, spread(): pl.pallas_call(spread_kernel, out_shape=[jax.ShapeDtypeStruct((NY, NX, QB...  38.7 us
    pallas_call x1, Pallas kernels, gather(): pl.pallas_call(gather_kernel, out_shape=jax.ShapeDtypeStruct((QB, ROWS, N...  21.3 us
    pallas_call x1, Pallas kernels, attend(): pl.pallas_call(attend_kernel, out_shape=[jax.ShapeDtypeStruct((NY, QB, PA...  8 us

profile of v6, /device:TPU:1, one launch (start us, length us, event | category | flops | bytes accessed | tf_op | source)
XLA Modules:
  0.0 68.7 jit_solution(12278063055918554425)
XLA Ops:
  0.0 38.7 %spread.1 = (bf16[4,4,4,8,896]{4,3,2,1,0:T(8,128)(2,1)S(1)}, bf16[4,1024,128]{2,1,0:T(8,128)(2,1)S(1)}, bf16[32,128,128]{2,1,0:T(8,128)(2,1)S(1)}, f32[32,8,128]{2,1,0:T(8,128)S(1)}, s32[32,128]{1,0:T(8,128)S(1)}) custom-call(s32[64]{0:T(128)} %target.1, bf16[4,8,3584]{2,1,0:T(8,128)(2,1)} %q.1, bf16[1024,512]{1,0:T(8,128)(2,1)} %k.1, bf16[1024,512]{1,0:T(8,128)(2,1)} %v.1, ...), custom_call_target="tpu_custom_call" | custom-call | tf_op jit(solution)/shard_map/spread/pallas_call | solution.py:272
  38.7 8.0 %attend.1 = (bf16[4,4,32,896]{3,2,1,0:T(8,128)(2,1)S(1)}, bf16[4,32,128]{2,1,0:T(8,128)(2,1)S(1)}) custom-call(s32[32,128]{1,0:T(8,128)S(1)} %get-tuple-element.12.ints, bf16[4,4,4,8,896]{4,3,2,1,0:T(8,128)(2,1)S(1)} %get-tuple-element.13.q_ref, bf16[32,128,128]{2,1,0:T(8,128)(2,1)S(1)} %bitcast.4, bf16[32,128,128]{2,1,0:T(8,128)(2,1)S(1)} %get-tuple-element.15.values, ...), custom_call_target="tpu_custom_call" | custom-call | tf_op jit(solution)/shard_map/attend/pallas_call | solution.py:393
  46.7 21.3 %gather.1 = bf16[4,8,3584]{2,1,0:T(8,128)(2,1)S(1)} custom-call(bf16[4,4,32,896]{3,2,1,0:T(8,128)(2,1)S(1)} %get-tuple-element.17.p, bf16[4,32,128]{2,1,0:T(8,128)(2,1)S(1)} %get-tuple-element.18.extra_in), custom_call_target="tpu_custom_call" | custom-call | tf_op jit(solution)/shard_map/gather/pallas_call | solution.py:479
  68.0 0.7 %copy.9 = bf16[4,8,3584]{2,1,0:T(8,128)(2,1)} copy(bf16[4,8,3584]{2,1,0:T(8,128)(2,1)S(1)} %gather.1) | data formatting | bytes 458752

commit v7 on v6

--- a/solution.py
+++ b/solution.py
@@ -23,6 +23,9 @@
 KB = 32
 SHARD = 8
 SLICE = HEADS * D
+EARLY = 5
+FORE = EARLY * D
+REST = SLICE - FORE
 ROWS = B // (NX * NY)
 PART = NX * ROWS
 KEYS = SHARD * B
@@ -49,13 +52,6 @@
     return rep, rep // 2, rep % 2, ctx // NY, ctx % NY
 
 
-def greet(partners):
-    barrier = pltpu.get_barrier_semaphore()
-    for who in partners:
-        pl.semaphore_signal(barrier, inc=1, device_id=who, device_id_type=MESH)
-    pl.semaphore_wait(barrier, len(partners))
-
-
 def remote(src, dst, send, recv, who):
     return pltpu.make_async_remote_copy(
         src_ref=src, dst_ref=dst, send_sem=send, recv_sem=recv, device_id=who, device_id_type=MESH
@@ -66,7 +62,7 @@
     return lax.broadcasted_iota(I32, shape, dim)
 
 
-def block_lists(listed, blocks, y):
+def block_lists(listed, blocks, rep, y):
     shape = (PAIRS, 128)
     lane, row = iota(shape, 1), iota(shape, 0)
     block = (lane >> 3) * (SHARD * NY) + y * SHARD + (lane & 7)
@@ -74,9 +70,10 @@
     own = jnp.zeros(shape, I32)
     column = iota(listed.shape[1:], 1)
     for s in range(QB):
-        own = jnp.where(row >> 3 == s, blocks[s], own)
+        own = jnp.where(row >> 3 == s, jnp.where((row & 7) < EARLY, blocks[s], rep * QB + s), own)
         for h in range(HEADS):
-            entry = jnp.max(jnp.where(column == blocks[s], listed[h], -1), axis=1, keepdims=True)
+            of = blocks[s] if h < EARLY else rep * QB + s
+            entry = jnp.max(jnp.where(column == of, listed[h], -1), axis=1, keepdims=True)
             found = (jnp.broadcast_to(entry, shape) == block).astype(I32)
             found = jnp.max(found, axis=0, keepdims=True)
             hits = jnp.where(row == s * 8 + h, found, hits)
@@ -96,12 +93,40 @@
     return jnp.where(lane == KB, number, packed)
 
 
+def near_groups(z, c):
+    return [((z + d) % NZ) * 2 + (c + e) % 2 for d in range(NZ) for e in range(2)]
+
+
+def slot_of(block, z, c):
+    source = block >> 2
+    return (((z + NZ - (source >> 1)) & (NZ - 1)) << 1) + ((source & 1) ^ c)
+
+
+def routes(goes, rep, groups):
+    goes_to = [goes[rep * QB + b] for b in range(QB)]
+    leaving = []
+    for group in groups:
+        b = jnp.int32(0)
+        for other in range(1, QB):
+            b = jnp.where(goes_to[other] == group, other, b)
+        leaving.append(b)
+
+    def look(j, state):
+        found, *at = state
+        hit = goes[j] == rep
+        at = [jnp.where(hit & (found == s), j, a) for s, a in enumerate(at)]
+        return (found + hit.astype(I32), *at)
+
+    _, *blocks = lax.fori_loop(0, 2 * NZ * QB, look, (jnp.int32(0),) * (1 + QB))
+    return leaving, blocks
+
+
 def spread_kernel(
     target, q, k, v, ks, vs, pattern,
-    q_all, keys, values, factors, lists,
+    q_fore, q_rest, keys, values, factors, lists,
     held0, held1, held2, held3, packed, came0, came1, came2, came3,
     v_land, scales, k_loc, v_loc, listed, goes,
-    z_send, z_recv, q_send, q_recv, y_send, y_recv, k_send, k_recv, v_send, v_recv, s_send, s_recv,
+    z_send, z_recv, q_send, q_recv, r_send, r_recv, y_send, y_recv, t_send, t_recv, k_send, k_recv, v_send, v_recv, s_send, s_recv,
     kc_send, kc_recv, vc_send, vc_recv, own,
 ):
     rep, z, c, x, y = place()
@@ -111,13 +136,19 @@
     at_x = [(rep, xs[d] * NY + y) for d in range(NX)]
     at_y = [(rep, x * NY + (y + d) % NY) for d in range(NY)]
     half = pl.ds(pl.multiple_of(c * (KEYS // 2), KEYS // 2), KEYS // 2)
-    groups = [((z + d) % NZ) * 2 + (c + e) % 2 for d in range(NZ) for e in range(2)]
+    groups = near_groups(z, c)
     at_group = [(g, x * NY + y) for g in groups]
     held = (held0, held1, held2, held3)
     came = (came0, came1, came2, came3)
 
     def cols(d, n):
         return pl.ds(pl.multiple_of(xs[d] * n, n), n)
+
+    def fore(d):
+        return q.at[:, :, pl.ds(pl.multiple_of(xs[d] * SLICE, D), FORE)]
+
+    def rest(d):
+        return q.at[:, :, pl.ds(pl.multiple_of(xs[d] * SLICE + FORE, D), REST)]
 
     partners = at_group[1:] + at_x[1:] + at_y[1:]
     barrier = pltpu.get_barrier_semaphore()
@@ -125,28 +156,23 @@
         pl.semaphore_signal(barrier, inc=1, device_id=who, device_id_type=MESH)
     stay = [
         pltpu.make_async_copy(target, goes, own.at[0]),
-        pltpu.make_async_copy(q.at[:, :, cols(0, SLICE)], held[0], own.at[1]),
+        pltpu.make_async_copy(fore(0), held[0], own.at[1]),
         pltpu.make_async_copy(ks, k_loc, own.at[2]),
         pltpu.make_async_copy(vs, v_loc, own.at[3]),
         pltpu.make_async_copy(pattern.at[pl.ds(x * HEADS, HEADS)], listed, own.at[4]),
         pltpu.make_async_copy(k.at[:, cols(0, D)], keys.at[x], own.at[5]),
         pltpu.make_async_copy(v.at[:, cols(0, D)], v_land.at[0], own.at[6]),
+        pltpu.make_async_copy(rest(0), q_rest.at[y, x], own.at[7]),
     ]
     for copy in stay:
         copy.start()
 
-    qx, kx, vx, sx, kc, vc = ([None] * NX for _ in range(6))
-    qy = [[None] * NY for _ in range(NX)]
+    qx, rx, kx, vx, sx, kc, vc = ([None] * NX for _ in range(7))
+    qy, ry = ([[None] * NY for _ in range(NX)] for _ in range(2))
     qz = [[None] * len(groups) for _ in range(NX)]
 
     stay[0].wait()
-    goes_to = [goes[rep * QB + b] for b in range(QB)]
-    leaving = []
-    for group in groups:
-        b = jnp.int32(0)
-        for other in range(1, QB):
-            b = jnp.where(goes_to[other] == group, other, b)
-        leaving.append(b)
+    leaving, blocks = routes(goes, rep, groups)
 
     def pack(d):
         for n in ORDER:
@@ -171,9 +197,12 @@
 
     pl.semaphore_wait(barrier, len(partners))
     for d in FAR:
-        qx[d] = remote(q.at[:, :, cols(d, SLICE)], held[d], q_send.at[d], q_recv.at[d], at_x[d])
+        qx[d] = remote(fore(d), held[d], q_send.at[d], q_recv.at[d], at_x[d])
         qx[d].start()
     over_z(0)
+    for d in FAR:
+        rx[d] = remote(rest(d), q_rest.at[y, x], r_send.at[d], r_recv.at[d], at_x[d])
+        rx[d].start()
     for d in FAR:
         sx[d] = remote(scales.at[0], scales.at[d], s_send.at[d], s_recv.at[d], at_x[d])
         sx[d].start()
@@ -183,21 +212,13 @@
         kx[d].start()
         vx[d].start()
 
-    def look(j, state):
-        found, *at = state
-        hit = goes[j] == rep
-        at = [jnp.where(hit & (found == s), j, a) for s, a in enumerate(at)]
-        return (found + hit.astype(I32), *at)
-
-    _, *blocks = lax.fori_loop(0, 2 * NZ * QB, look, (jnp.int32(0),) * (1 + QB))
-
     for d in FAR:
         qx[d].wait_recv()
         pack(d)
         over_z(d)
 
     stay[4].wait()
-    lists[...] = block_lists(listed, blocks, y)
+    lists[...] = block_lists(listed, blocks, rep, y)
 
     scale_row = iota((2 * NX, 128), 0)
 
@@ -234,15 +255,21 @@
         for n in range(1, len(groups)):
             qz[d][n].wait_recv()
         for s in range(QB):
-            source = blocks[s] >> 2
-            n = (((z + NZ - (source >> 1)) & (NZ - 1)) << 1) + ((source & 1) ^ c)
-            q_all[y, back[d], s] = came[d][n]
+            q_fore[y, back[d], s] = came[d][slot_of(blocks[s], z, c)]
         for e in FAR:
-            piece = q_all.at[y, back[d]]
+            piece = q_fore.at[y, back[d]]
             qy[d][e] = remote(piece, piece, y_send.at[d, e], y_recv.at[d, e], at_y[e])
             qy[d][e].start()
 
-    for copy in stay[5:]:
+    stay[7].wait()
+    for d in (0, *FAR):
+        if d:
+            rx[d].wait_recv()
+        for e in FAR:
+            piece = q_rest.at[y, back[d]]
+            ry[d][e] = remote(piece, piece, t_send.at[d, e], t_recv.at[d, e], at_y[e])
+            ry[d][e].start()
+    for copy in stay[5:7]:
         copy.wait()
     finish(0)
     hand_over(1)
@@ -257,10 +284,11 @@
     over_y(2)
     for d in range(NX):
         for e in FAR:
-            qy[d][e].wait_recv()
-            qy[d][e].wait_send()
-    for d in FAR:
-        for copy in (qx[d], kx[d], vx[d], sx[d], kc[d], vc[d]):
+            for copy in (qy[d][e], ry[d][e]):
+                copy.wait_recv()
+                copy.wait_send()
+    for d in FAR:
+        for copy in (qx[d], rx[d], kx[d], vx[d], sx[d], kc[d], vc[d]):
             copy.wait_send()
     for copies in qz:
         for copy in copies[1:]:
@@ -268,20 +296,21 @@
 
 
 def spread(target, q, k, v, ks, vs, pattern):
-    slots = pltpu.VMEM((2 * NZ, ROWS, SLICE), BF16)
+    slots = pltpu.VMEM((2 * NZ, ROWS, FORE), BF16)
     return pl.pallas_call(
         spread_kernel,
         out_shape=[
-            jax.ShapeDtypeStruct((NY, NX, QB, ROWS, SLICE), BF16),
+            jax.ShapeDtypeStruct((NY, NX, QB, ROWS, FORE), BF16),
+            jax.ShapeDtypeStruct((NY, NX, QB, ROWS, REST), BF16),
             jax.ShapeDtypeStruct((NX, KEYS, D), BF16),
             jax.ShapeDtypeStruct((KB, D, B), BF16),
             jax.ShapeDtypeStruct((KB, 8, 128), F32),
             jax.ShapeDtypeStruct((PAIRS, 128), I32),
         ],
         in_specs=[HBM] * 7,
-        out_specs=[VMEM] * 5,
-        scratch_shapes=[pltpu.VMEM((QB, ROWS, SLICE), BF16)] * NX
-        + [pltpu.VMEM((NX, 2 * NZ, ROWS, SLICE), BF16)]
+        out_specs=[VMEM] * 6,
+        scratch_shapes=[pltpu.VMEM((QB, ROWS, FORE), BF16)] * NX
+        + [pltpu.VMEM((NX, 2 * NZ, ROWS, FORE), BF16)]
         + [slots] * NX
         + [
             pltpu.VMEM((NX, KEYS, D), BF16),
@@ -292,10 +321,10 @@
             pltpu.SMEM(target.shape, I32),
         ]
         + [DMA((NX, 2 * NZ))] * 2
-        + [DMA((NX,))] * 2
-        + [DMA((NX, NY))] * 2
+        + [DMA((NX,))] * 4
+        + [DMA((NX, NY))] * 4
         + [DMA((NX,))] * 10
-        + [DMA((7,))],
+        + [DMA((8,))],
         compiler_params=pltpu.CompilerParams(
             collective_id=0, has_side_effects=True, vmem_limit_bytes=24 << 20
         ),
@@ -303,7 +332,10 @@
     )(target, q, k, v, ks, vs, pattern)
 
 
-def attend_kernel(ints, q_ref, keys, values, factors, out, extra_out, qs, sc, mx, acc, su, extra, items):
+def attend_kernel(
+    ints, q_fore, q_rest, keys, values, factors, out_fore, out_rest, extra_out,
+    qs, sc, mx, acc, su, extra, items,
+):
     row = iota((B, B), 1)
     row = ((row >> 3) & 3) * PART + (row >> 5) * ROWS + (row & 7)
     ahead = iota((B, B), 0) - row
@@ -327,9 +359,11 @@
             items[n + g] = HEADS * 16
         count = (n + STEP - 1) // STEP
         for j in range(TOGETHER):
-            rows = q_ref[:, :, part_of * TOGETHER + j].astype(F32).reshape(B, SLICE).astype(BF16)
-            for h in range(HEADS):
-                qs[j * 8 + h] = rows[:, h * D : (h + 1) * D].T
+            for q_ref, low, high in ((q_fore, 0, EARLY), (q_rest, EARLY, HEADS)):
+                rows = q_ref[:, :, part_of * TOGETHER + j].astype(F32).reshape(B, (high - low) * D)
+                rows = rows.astype(BF16)
+                for h in range(low, high):
+                    qs[j * 8 + h] = rows[:, (h - low) * D : (h - low + 1) * D].T
         mx[...] = jnp.full(mx.shape, NEG, F32)
         acc[...] = jnp.zeros(acc.shape, F32)
         su[...] = jnp.zeros(su.shape, F32)
@@ -380,24 +414,26 @@
                 extra[pl.ds(at, 1), :] = mx[r][0:1]
                 extra[pl.ds(SUM_LANE + at, 1), :] = jnp.sum(su[r], axis=0, keepdims=True)
                 part = acc[r].astype(BF16).T
+                out, i = (out_fore, h) if h < EARLY else (out_rest, h - EARLY)
                 for d in range(NY):
-                    out[d, part_of * TOGETHER + j, :, h * D : (h + 1) * D] = part[d * PART : (d + 1) * PART]
+                    out[d, part_of * TOGETHER + j, :, i * D : (i + 1) * D] = part[d * PART : (d + 1) * PART]
 
     turned = extra[...].T
     for d in range(NY):
         extra_out[d] = turned[d * PART : (d + 1) * PART].astype(BF16)
 
 
-def attend(lists, q_all, keys, values, factors):
+def attend(lists, q_fore, q_rest, keys, values, factors):
     most = TOGETHER * HEADS * KB // 2 + STEP
     return pl.pallas_call(
         attend_kernel,
         out_shape=[
-            jax.ShapeDtypeStruct((NY, QB, PART, SLICE), BF16),
+            jax.ShapeDtypeStruct((NY, QB, PART, FORE), BF16),
+            jax.ShapeDtypeStruct((NY, QB, PART, REST), BF16),
             jax.ShapeDtypeStruct((NY, PART, 128), BF16),
         ],
-        in_specs=[SMEM] + [VMEM] * 4,
-        out_specs=[VMEM] * 2,
+        in_specs=[SMEM] + [VMEM] * 5,
+        out_specs=[VMEM] * 3,
         scratch_shapes=[
             pltpu.VMEM((LANES, D, B), BF16),
             pltpu.VMEM((2 * most, B, B), F32),
@@ -409,25 +445,41 @@
         ],
         compiler_params=pltpu.CompilerParams(vmem_limit_bytes=46 << 20),
         name="attend",
-    )(lists, q_all, keys.reshape(KB, B, D), values, factors)
+    )(lists, q_fore, q_rest, keys.reshape(KB, B, D), values, factors)
 
 
 def gather_kernel(
-    p, extra_in, out, parts, extra, att, e_send, e_recv, y_send, y_recv, x_send, x_recv, own
+    target, p, p_rest, extra_in, out,
+    parts, parts_rest, extra, att, att_rest, held, packed, came, goes,
+    e_send, e_recv, y_send, y_recv, t_send, t_recv, x_send, x_recv, r_send, r_recv, z_send, z_recv, own,
 ):
     rep, z, c, x, y = place()
     xs = [(x + d) % NX for d in range(NX)]
+    back = [(x + NX - d) % NX for d in range(NX)]
     ys = [(y + d) % NY for d in range(NY)]
     at_x = [(rep, xs[d] * NY + y) for d in range(NX)]
     at_y = [(rep, x * NY + ys[d]) for d in range(NY)]
-    greet(at_x[1:] + at_y[1:])
-
-    ex = [None] * NY
+    groups = near_groups(z, c)
+    at_group = [(g, x * NY + y) for g in groups]
+    partners = at_group[1:] + at_x[1:] + at_y[1:]
+    barrier = pltpu.get_barrier_semaphore()
+    for who in partners:
+        pl.semaphore_signal(barrier, inc=1, device_id=who, device_id_type=MESH)
+    told = pltpu.make_async_copy(target, goes, own.at[QB])
+    told.start()
+    told.wait()
+    leaving, blocks = routes(goes, rep, groups)
+    pl.semaphore_wait(barrier, len(partners))
+
+    ex, ty, rx = ([None] * NY for _ in range(3))
     py = [[None] * NY for _ in range(QB)]
     px = [[None] * NX for _ in range(QB)]
+    pz = [None] * len(groups)
     for d in FAR:
         ex[d] = remote(extra_in.at[ys[d]], extra.at[d], e_send.at[d], e_recv.at[d], at_y[d])
         ex[d].start()
+        ty[d] = remote(p_rest.at[ys[d]], parts_rest.at[d], t_send.at[d], t_recv.at[d], at_y[d])
+        ty[d].start()
     for b in range(QB):
         for d in FAR:
             py[b][d] = remote(p.at[ys[d], b], parts.at[d, b], y_send.at[b, d], y_recv.at[b, d], at_y[d])
@@ -441,20 +493,48 @@
     lane = iota((PART, 128), 1)
     total = jnp.where((lane < QB * 8) & ((lane & 7) < HEADS), total, 1.0)
     ratio = [w / total for w in shift]
-    mine = pl.ds(pl.multiple_of(x * SLICE, SLICE), SLICE)
-
+
+    def quotient(b, h, mine, theirs, cols):
+        at = b * 8 + h
+        value = sum(
+            jnp.broadcast_to(ratio[d][:, at : at + 1], (PART, D))
+            * (theirs[d, b, :, cols] if d else mine[y, b, :, cols]).astype(F32)
+            for d in range(NY)
+        )
+        return value.reshape(NX, ROWS, D).astype(BF16)
+
+    for d in FAR:
+        ty[d].wait_recv()
+    for b in range(QB):
+        for h in range(EARLY, HEADS):
+            cols = slice((h - EARLY) * D, (h - EARLY + 1) * D)
+            value = quotient(b, h, p_rest, parts_rest, cols)
+            for d in range(NX):
+                att_rest[d, b, :, cols] = value[d]
+    for d in FAR:
+        rx[d] = remote(att_rest.at[xs[d]], held.at[d], r_send.at[d], r_recv.at[d], at_x[d])
+        rx[d].start()
+    held[0] = att_rest[x]
+    for d in FAR:
+        rx[d].wait_recv()
+    for n in ORDER:
+        for d in range(NX):
+            block = held[d, leaving[n]]
+            if n == 0:
+                came[n, d] = block
+            else:
+                packed[n, d] = block
+        if n > 0:
+            pz[n] = remote(packed.at[n], came.at[n], z_send.at[n], z_recv.at[n], at_group[n])
+            pz[n].start()
+
+    mine = pl.ds(pl.multiple_of(x * SLICE, D), FORE)
     for b in range(QB):
         for d in FAR:
             py[b][d].wait_recv()
-        for h in range(HEADS):
+        for h in range(EARLY):
             cols = slice(h * D, (h + 1) * D)
-            at = b * 8 + h
-            value = sum(
-                jnp.broadcast_to(ratio[d][:, at : at + 1], (PART, D))
-                * (parts[d, b, :, cols] if d else p[y, b, :, cols]).astype(F32)
-                for d in range(NY)
-            )
-            value = value.reshape(NX, ROWS, D).astype(BF16)
+            value = quotient(b, h, p, parts, cols)
             for d in range(NX):
                 att[b, d, :, cols] = value[d]
         for d in FAR:
@@ -465,36 +545,57 @@
         px[b][0] = pltpu.make_async_copy(att.at[b, x], out.at[b, :, mine], own.at[b])
         px[b][0].start()
 
-    for d in FAR:
-        ex[d].wait_send()
+    for n in range(1, len(groups)):
+        pz[n].wait_recv()
     for b in range(QB):
         px[b][0].wait()
         for d in FAR:
             px[b][d].wait_recv()
+    for s in range(QB):
+        n = slot_of(blocks[s], z, c)
+        for d in range(NX):
+            out[s, :, pl.ds(pl.multiple_of(back[d] * SLICE + FORE, D), REST)] = came[n, d]
+
+    for n in range(1, len(groups)):
+        pz[n].wait_send()
+    for d in FAR:
+        for copy in (ex[d], ty[d], rx[d]):
+            copy.wait_send()
+        for b in range(QB):
             px[b][d].wait_send()
             py[b][d].wait_send()
 
 
-def gather(p, extra):
+def gather(target, p, p_rest, extra):
+    slots = pltpu.VMEM((2 * NZ, NX, ROWS, REST), BF16)
     return pl.pallas_call(
         gather_kernel,
         out_shape=jax.ShapeDtypeStruct((QB, ROWS, NX * SLICE), BF16),
-        in_specs=[VMEM, VMEM],
+        in_specs=[HBM, VMEM, VMEM, VMEM],
         out_specs=VMEM,
         scratch_shapes=[
-            pltpu.VMEM((NY, QB, PART, SLICE), BF16),
+            pltpu.VMEM((NY, QB, PART, FORE), BF16),
+            pltpu.VMEM((NY, QB, PART, REST), BF16),
             pltpu.VMEM((NY, PART, 128), BF16),
-            pltpu.VMEM((QB, NX, ROWS, SLICE), BF16),
+            pltpu.VMEM((QB, NX, ROWS, FORE), BF16),
+            pltpu.VMEM((NX, QB, ROWS, REST), BF16),
+            pltpu.VMEM((NX, QB, ROWS, REST), BF16),
+            slots,
+            slots,
+            pltpu.SMEM(target.shape, I32),
         ]
         + [DMA((NY,))] * 2
         + [DMA((QB, NY))] * 2
+        + [DMA((NY,))] * 2
         + [DMA((QB, NX))] * 2
-        + [DMA((QB,))],
+        + [DMA((NX,))] * 2
+        + [DMA((2 * NZ,))] * 2
+        + [DMA((QB + 1,))],
         compiler_params=pltpu.CompilerParams(
             collective_id=1, has_side_effects=True, vmem_limit_bytes=16 << 20
         ),
         name="gather",
-    )(p, extra)
+    )(target, p, p_rest, extra)
 
 
 def hbm(array):
@@ -502,8 +603,9 @@
 
 
 def per_device(queries, key_cache, value_cache, key_scale, value_scale, pattern, target):
-    q_all, keys, values, factors, lists = spread(
-        hbm(target),
+    target = hbm(target)
+    q_fore, q_rest, keys, values, factors, lists = spread(
+        target,
         hbm(queries),
         hbm(key_cache),
         hbm(value_cache),
@@ -511,8 +613,8 @@
         hbm(value_scale.T),
         hbm(jnp.swapaxes(pattern, 1, 2)),
     )
-    part, extra = attend(lists, q_all, keys, values, factors)
-    return gather(part, extra)
+    part, rest, extra = attend(lists, q_fore, q_rest, keys, values, factors)
+    return gather(target, part, rest, extra)
 
 
 def solution(mesh):

time: 68.8 us -> 66.9 us (0.972)
  Pallas kernels: 68 us -> 66.1 us
    pallas_call x1, Pallas kernels: 21.3 us -> 19.2 us  [gather(): pl.pallas_call(gather_kernel, out_shape=jax.ShapeDtypeStruct((QB, ROWS, N...]
    pallas_call x1, Pallas kernels: 8 us -> 9.27 us  [attend(): pl.pallas_call(attend_kernel, out_shape=[jax.ShapeDtypeStruct((NY, QB, PA...]
    pallas_call x1, Pallas kernels: 38.7 us -> 37.6 us  [spread(): pl.pallas_call(spread_kernel, out_shape=[jax.ShapeDtypeStruct((NY, NX, QB...]
where the time goes in v7:
time: 66.9 us; the launch traced here: 66.8 us
  Pallas kernels  66.1 us (99%)
  local copies, waits for them, and re-layouts  0.69 us (1%)
    pallas_call x1, Pallas kernels, spread(): pl.pallas_call(spread_kernel, out_shape=[jax.ShapeDtypeStruct((NY, NX, QB...  37.6 us
    pallas_call x1, Pallas kernels, gather(): pl.pallas_call(gather_kernel, out_shape=jax.ShapeDtypeStruct((QB, ROWS, N...  19.2 us
    pallas_call x1, Pallas kernels, attend(): pl.pallas_call(attend_kernel, out_shape=[jax.ShapeDtypeStruct((NY, QB, PA...  9.27 us

profile of v7, /device:TPU:1, one launch (start us, length us, event | category | flops | bytes accessed | tf_op | source)
XLA Modules:
  0.0 66.8 jit_solution(5378696668402523580)
XLA Ops:
  0.0 37.6 %spread.1 = (bf16[4,4,4,8,640]{4,3,2,1,0:T(8,128)(2,1)S(1)}, bf16[4,4,4,8,256]{4,3,2,1,0:T(8,128)(2,1)S(1)}, bf16[4,1024,128]{2,1,0:T(8,128)(2,1)S(1)}, bf16[32,...) custom-call(s32[64]{0:T(128)} %target.3, bf16[4,8,3584]{2,1,0:T(8,128)(2,1)} %q.1, ...), custom_call_target="tpu_custom_call" | custom-call | tf_op jit(solution)/shard_map/spread/pallas_call | solution.py:300
  37.6 9.3 %attend.1 = (bf16[4,4,32,640]{3,2,1,0:T(8,128)(2,1)S(1)}, bf16[4,4,32,256]{3,2,1,0:T(8,128)(2,1)S(1)}, bf16[4,32,128]{2,1,0:T(8,128)(2,1)S(1)}) custom-call(s32[32,128]{1,0:T(8,128)S(1)} %get-tuple-element.14.ints, bf16[4,4,4,8,640]{4,3,2,1,0:T(8,128)(2,1)S(1)} %get-tuple-element.15.q_fore, bf16[4,4,4,8,256]{4,3,2,1,0:T(8,128)(2,1)S(1)} %get-tuple-element.16.q_rest, ...), custom_call_target="tpu_custom_call" | custom-call | tf_op jit(solution)/shard_map/attend/pallas_call | solution.py:428
  46.9 19.2 %gather.1 = bf16[4,8,3584]{2,1,0:T(8,128)(2,1)S(1)} custom-call(s32[64]{0:T(128)} %target.3, bf16[4,4,32,640]{3,2,1,0:T(8,128)(2,1)S(1)} %get-tuple-element.20.p, bf16[4,4,32,256]{3,2,1,0:T(8,128)(2,1)S(1)} %get-tuple-element.21.p_rest, bf16[4,32,128]{2,1,0:T(8,128)(2,1)S(1)} %get-tuple-element.22.extra_in), custom_call_target="tpu_custom_call" | custom-call | tf_op jit(solution)/shard_map/gather/pallas_call | solution.py:571
  66.1 0.7 %copy.9 = bf16[4,8,3584]{2,1,0:T(8,128)(2,1)} copy(bf16[4,8,3584]{2,1,0:T(8,128)(2,1)S(1)} %gather.1) | data formatting | bytes 458752

commit v8 on v7

--- a/solution.py
+++ b/solution.py
@@ -23,7 +23,7 @@
 KB = 32
 SHARD = 8
 SLICE = HEADS * D
-EARLY = 5
+EARLY = 6
 FORE = EARLY * D
 REST = SLICE - FORE
 ROWS = B // (NX * NY)

time: 66.9 us -> 67.3 us (level)
    pallas_call x1, Pallas kernels: 19.2 us -> 17.1 us  [gather(): pl.pallas_call(gather_kernel, out_shape=jax.ShapeDtypeStruct((QB, ROWS, N...]
    pallas_call x1, Pallas kernels: 9.27 us -> 10.7 us  [attend(): pl.pallas_call(attend_kernel, out_shape=[jax.ShapeDtypeStruct((NY, QB, PA...]
    pallas_call x1, Pallas kernels: 37.6 us -> 38.3 us  [spread(): pl.pallas_call(spread_kernel, out_shape=[jax.ShapeDtypeStruct((NY, NX, QB...]
where the time goes in v8:
time: 67.3 us; the launch traced here: 66.8 us
  Pallas kernels  66.1 us (98%)
  local copies, waits for them, and re-layouts  0.69 us (1%)
    pallas_call x1, Pallas kernels, spread(): pl.pallas_call(spread_kernel, out_shape=[jax.ShapeDtypeStruct((NY, NX, QB...  38.3 us
    pallas_call x1, Pallas kernels, gather(): pl.pallas_call(gather_kernel, out_shape=jax.ShapeDtypeStruct((QB, ROWS, N...  17.1 us
    pallas_call x1, Pallas kernels, attend(): pl.pallas_call(attend_kernel, out_shape=[jax.ShapeDtypeStruct((NY, QB, PA...  10.7 us

profile of v8, /device:TPU:1, one launch (start us, length us, event | category | flops | bytes accessed | tf_op | source)
XLA Modules:
  0.0 66.8 jit_solution(44487491684950814)
XLA Ops:
  0.0 38.3 %spread.1 = (bf16[4,4,4,8,768]{4,3,2,1,0:T(8,128)(2,1)S(1)}, bf16[4,4,4,8,128]{4,3,2,1,0:T(8,128)(2,1)S(1)}, bf16[4,1024,128]{2,1,0:T(8,128)(2,1)S(1)}, bf16[32,...) custom-call(s32[64]{0:T(128)} %target.3, bf16[4,8,3584]{2,1,0:T(8,128)(2,1)} %q.1, ...), custom_call_target="tpu_custom_call" | custom-call | tf_op jit(solution)/shard_map/spread/pallas_call | solution.py:300
  38.3 10.7 %attend.1 = (bf16[4,4,32,768]{3,2,1,0:T(8,128)(2,1)S(1)}, bf16[4,4,32,128]{3,2,1,0:T(8,128)(2,1)S(1)}, bf16[4,32,128]{2,1,0:T(8,128)(2,1)S(1)}) custom-call(s32[32,128]{1,0:T(8,128)S(1)} %get-tuple-element.14.ints, bf16[4,4,4,8,768]{4,3,2,1,0:T(8,128)(2,1)S(1)} %get-tuple-element.15.q_fore, bf16[4,4,4,8,128]{4,3,2,1,0:T(8,128)(2,1)S(1)} %get-tuple-element.16.q_rest, ...), custom_call_target="tpu_custom_call" | custom-call | tf_op jit(solution)/shard_map/attend/pallas_call | solution.py:428
  49.0 17.1 %gather.1 = bf16[4,8,3584]{2,1,0:T(8,128)(2,1)S(1)} custom-call(s32[64]{0:T(128)} %target.3, bf16[4,4,32,768]{3,2,1,0:T(8,128)(2,1)S(1)} %get-tuple-element.20.p, bf16[4,4,32,128]{3,2,1,0:T(8,128)(2,1)S(1)} %get-tuple-element.21.p_rest, bf16[4,32,128]{2,1,0:T(8,128)(2,1)S(1)} %get-tuple-element.22.extra_in), custom_call_target="tpu_custom_call" | custom-call | tf_op jit(solution)/shard_map/gather/pallas_call | solution.py:571
  66.1 0.7 %copy.9 = bf16[4,8,3584]{2,1,0:T(8,128)(2,1)} copy(bf16[4,8,3584]{2,1,0:T(8,128)(2,1)S(1)} %gather.1) | data formatting | bytes 458752

commit v9 on v7

--- a/solution.py
+++ b/solution.py
@@ -102,7 +102,7 @@
     return (((z + NZ - (source >> 1)) & (NZ - 1)) << 1) + ((source & 1) ^ c)
 
 
-def routes(goes, rep, groups):
+def blocks_out(goes, rep, groups):
     goes_to = [goes[rep * QB + b] for b in range(QB)]
     leaving = []
     for group in groups:
@@ -110,7 +110,10 @@
         for other in range(1, QB):
             b = jnp.where(goes_to[other] == group, other, b)
         leaving.append(b)
-
+    return leaving
+
+
+def blocks_in(goes, rep):
     def look(j, state):
         found, *at = state
         hit = goes[j] == rep
@@ -118,7 +121,7 @@
         return (found + hit.astype(I32), *at)
 
     _, *blocks = lax.fori_loop(0, 2 * NZ * QB, look, (jnp.int32(0),) * (1 + QB))
-    return leaving, blocks
+    return blocks
 
 
 def spread_kernel(
@@ -171,8 +174,12 @@
     qy, ry = ([[None] * NY for _ in range(NX)] for _ in range(2))
     qz = [[None] * len(groups) for _ in range(NX)]
 
+    pl.semaphore_wait(barrier, len(partners))
+    for d in FAR:
+        qx[d] = remote(fore(d), held[d], q_send.at[d], q_recv.at[d], at_x[d])
+        qx[d].start()
     stay[0].wait()
-    leaving, blocks = routes(goes, rep, groups)
+    leaving = blocks_out(goes, rep, groups)
 
     def pack(d):
         for n in ORDER:
@@ -189,33 +196,27 @@
 
     stay[1].wait()
     pack(0)
+    over_z(0)
+    for d in FAR:
+        kx[d] = remote(k.at[half, cols(d, D)], keys.at[x, half], k_send.at[d], k_recv.at[d], at_x[d])
+        vx[d] = remote(v.at[half, cols(d, D)], v_land.at[d, half], v_send.at[d], v_recv.at[d], at_x[d])
+        rx[d] = remote(rest(d), q_rest.at[y, x], r_send.at[d], r_recv.at[d], at_x[d])
+        rx[d].start()
+        kx[d].start()
+        vx[d].start()
+    for d in FAR:
+        qx[d].wait_recv()
+        pack(d)
+        over_z(d)
     scales[0] = jnp.zeros((2 * NX, 128), F32)
     stay[2].wait()
     stay[3].wait()
     scales[0, 0:NX, 0:SHARD] = k_loc[...]
     scales[0, NX : 2 * NX, 0:SHARD] = v_loc[...]
-
-    pl.semaphore_wait(barrier, len(partners))
-    for d in FAR:
-        qx[d] = remote(fore(d), held[d], q_send.at[d], q_recv.at[d], at_x[d])
-        qx[d].start()
-    over_z(0)
-    for d in FAR:
-        rx[d] = remote(rest(d), q_rest.at[y, x], r_send.at[d], r_recv.at[d], at_x[d])
-        rx[d].start()
     for d in FAR:
         sx[d] = remote(scales.at[0], scales.at[d], s_send.at[d], s_recv.at[d], at_x[d])
         sx[d].start()
-    for d in FAR:
-        kx[d] = remote(k.at[half, cols(d, D)], keys.at[x, half], k_send.at[d], k_recv.at[d], at_x[d])
-        vx[d] = remote(v.at[half, cols(d, D)], v_land.at[d, half], v_send.at[d], v_recv.at[d], at_x[d])
-        kx[d].start()
-        vx[d].start()
-
-    for d in FAR:
-        qx[d].wait_recv()
-        pack(d)
-        over_z(d)
+    blocks = blocks_in(goes, rep)
 
     stay[4].wait()
     lists[...] = block_lists(listed, blocks, rep, y)
@@ -467,8 +468,6 @@
         pl.semaphore_signal(barrier, inc=1, device_id=who, device_id_type=MESH)
     told = pltpu.make_async_copy(target, goes, own.at[QB])
     told.start()
-    told.wait()
-    leaving, blocks = routes(goes, rep, groups)
     pl.semaphore_wait(barrier, len(partners))
 
     ex, ty, rx = ([None] * NY for _ in range(3))
@@ -484,6 +483,9 @@
         for d in FAR:
             py[b][d] = remote(p.at[ys[d], b], parts.at[d, b], y_send.at[b, d], y_recv.at[b, d], at_y[d])
             py[b][d].start()
+    told.wait()
+    leaving = blocks_out(goes, rep, groups)
+    blocks = blocks_in(goes, rep)
     for d in FAR:
         ex[d].wait_recv()
     marks = [extra_in[y].astype(F32)] + [extra[d].astype(F32) for d in range(1, NY)]

time: 66.9 us -> 69.6 us (1.040)
  Pallas kernels: 66.1 us -> 68.3 us
    pallas_call x1, Pallas kernels: 19.2 us -> 21.1 us  [gather(): pl.pallas_call(gather_kernel, out_shape=jax.ShapeDtypeStruct((QB, ROWS, N...]
where the time goes in v9:
time: 69.6 us; the launch traced here: 69 us
  Pallas kernels  68.3 us (98%)
    pallas_call x1, Pallas kernels, spread(): pl.pallas_call(spread_kernel, out_shape=[jax.ShapeDtypeStruct((NY, NX, QB...  38 us
    pallas_call x1, Pallas kernels, gather(): pl.pallas_call(gather_kernel, out_shape=jax.ShapeDtypeStruct((QB, ROWS, N...  21.1 us
    pallas_call x1, Pallas kernels, attend(): pl.pallas_call(attend_kernel, out_shape=[jax.ShapeDtypeStruct((NY, QB, PA...  9.3 us

profile of v9, /device:TPU:1, one launch (start us, length us, event | category | flops | bytes accessed | tf_op | source)
XLA Modules:
  0.0 69.0 jit_solution(4727503140802711042)
XLA Ops:
  0.0 38.0 %spread.1 = (bf16[4,4,4,8,640]{4,3,2,1,0:T(8,128)(2,1)S(1)}, bf16[4,4,4,8,256]{4,3,2,1,0:T(8,128)(2,1)S(1)}, bf16[4,1024,128]{2,1,0:T(8,128)(2,1)S(1)}, bf16[32,...) custom-call(s32[64]{0:T(128)} %target.3, bf16[4,8,3584]{2,1,0:T(8,128)(2,1)} %q.1, ...), custom_call_target="tpu_custom_call" | custom-call | tf_op jit(solution)/shard_map/spread/pallas_call | solution.py:301
  38.0 9.3 %attend.1 = (bf16[4,4,32,640]{3,2,1,0:T(8,128)(2,1)S(1)}, bf16[4,4,32,256]{3,2,1,0:T(8,128)(2,1)S(1)}, bf16[4,32,128]{2,1,0:T(8,128)(2,1)S(1)}) custom-call(s32[32,128]{1,0:T(8,128)S(1)} %get-tuple-element.14.ints, bf16[4,4,4,8,640]{4,3,2,1,0:T(8,128)(2,1)S(1)} %get-tuple-element.15.q_fore, bf16[4,4,4,8,256]{4,3,2,1,0:T(8,128)(2,1)S(1)} %get-tuple-element.16.q_rest, ...), custom_call_target="tpu_custom_call" | custom-call | tf_op jit(solution)/shard_map/attend/pallas_call | solution.py:429
  47.3 21.1 %gather.1 = bf16[4,8,3584]{2,1,0:T(8,128)(2,1)S(1)} custom-call(s32[64]{0:T(128)} %target.3, bf16[4,4,32,640]{3,2,1,0:T(8,128)(2,1)S(1)} %get-tuple-element.20.p, bf16[4,4,32,256]{3,2,1,0:T(8,128)(2,1)S(1)} %get-tuple-element.21.p_rest, bf16[4,32,128]{2,1,0:T(8,128)(2,1)S(1)} %get-tuple-element.22.extra_in), custom_call_target="tpu_custom_call" | custom-call | tf_op jit(solution)/shard_map/gather/pallas_call | solution.py:573
  68.4 0.7 %copy.9 = bf16[4,8,3584]{2,1,0:T(8,128)(2,1)} copy(bf16[4,8,3584]{2,1,0:T(8,128)(2,1)S(1)} %gather.1) | data formatting | bytes 458752

commit v10 on v7

--- a/solution.py
+++ b/solution.py
@@ -102,7 +102,7 @@
     return (((z + NZ - (source >> 1)) & (NZ - 1)) << 1) + ((source & 1) ^ c)
 
 
-def routes(goes, rep, groups):
+def blocks_out(goes, rep, groups):
     goes_to = [goes[rep * QB + b] for b in range(QB)]
     leaving = []
     for group in groups:
@@ -110,7 +110,10 @@
         for other in range(1, QB):
             b = jnp.where(goes_to[other] == group, other, b)
         leaving.append(b)
-
+    return leaving
+
+
+def blocks_in(goes, rep):
     def look(j, state):
         found, *at = state
         hit = goes[j] == rep
@@ -118,7 +121,7 @@
         return (found + hit.astype(I32), *at)
 
     _, *blocks = lax.fori_loop(0, 2 * NZ * QB, look, (jnp.int32(0),) * (1 + QB))
-    return leaving, blocks
+    return blocks
 
 
 def spread_kernel(
@@ -172,7 +175,8 @@
     qz = [[None] * len(groups) for _ in range(NX)]
 
     stay[0].wait()
-    leaving, blocks = routes(goes, rep, groups)
+    leaving = blocks_out(goes, rep, groups)
+    blocks = blocks_in(goes, rep)
 
     def pack(d):
         for n in ORDER:
@@ -276,12 +280,12 @@
     hand_over(3)
     over_y(0)
     whole(1)
+    over_y(1)
     whole(3)
-    over_y(1)
+    over_y(3)
+    over_y(2)
     hand_over(2)
     whole(2)
-    over_y(3)
-    over_y(2)
     for d in range(NX):
         for e in FAR:
             for copy in (qy[d][e], ry[d][e]):
@@ -467,8 +471,6 @@
         pl.semaphore_signal(barrier, inc=1, device_id=who, device_id_type=MESH)
     told = pltpu.make_async_copy(target, goes, own.at[QB])
     told.start()
-    told.wait()
-    leaving, blocks = routes(goes, rep, groups)
     pl.semaphore_wait(barrier, len(partners))
 
     ex, ty, rx = ([None] * NY for _ in range(3))
@@ -484,6 +486,9 @@
         for d in FAR:
             py[b][d] = remote(p.at[ys[d], b], parts.at[d, b], y_send.at[b, d], y_recv.at[b, d], at_y[d])
             py[b][d].start()
+    told.wait()
+    leaving = blocks_out(goes, rep, groups)
+    blocks = blocks_in(goes, rep)
     for d in FAR:
         ex[d].wait_recv()
     marks = [extra_in[y].astype(F32)] + [extra[d].astype(F32) for d in range(1, NY)]
@@ -515,21 +520,21 @@
         rx[d] = remote(att_rest.at[xs[d]], held.at[d], r_send.at[d], r_recv.at[d], at_x[d])
         rx[d].start()
     held[0] = att_rest[x]
-    for d in FAR:
-        rx[d].wait_recv()
-    for n in ORDER:
-        for d in range(NX):
-            block = held[d, leaving[n]]
-            if n == 0:
-                came[n, d] = block
-            else:
-                packed[n, d] = block
-        if n > 0:
-            pz[n] = remote(packed.at[n], came.at[n], z_send.at[n], z_recv.at[n], at_group[n])
-            pz[n].start()
-
     mine = pl.ds(pl.multiple_of(x * SLICE, D), FORE)
     for b in range(QB):
+        if b == 1:
+            for d in FAR:
+                rx[d].wait_recv()
+            for n in ORDER:
+                for d in range(NX):
+                    block = held[d, leaving[n]]
+                    if n == 0:
+                        came[n, d] = block
+                    else:
+                        packed[n, d] = block
+                if n > 0:
+                    pz[n] = remote(packed.at[n], came.at[n], z_send.at[n], z_recv.at[n], at_group[n])
+                    pz[n].start()
         for d in FAR:
             py[b][d].wait_recv()
         for h in range(EARLY):

time: 66.9 us -> 65.1 us (0.973)
  Pallas kernels: 66.1 us -> 64.3 us
    pallas_call x1, Pallas kernels: 37.6 us -> 33.9 us  [spread(): pl.pallas_call(spread_kernel, out_shape=[jax.ShapeDtypeStruct((NY, NX, QB...]
    pallas_call x1, Pallas kernels: 19.2 us -> 22.4 us  [gather(): pl.pallas_call(gather_kernel, out_shape=jax.ShapeDtypeStruct((QB, ROWS, N...]
    pallas_call x1, Pallas kernels: 9.27 us -> 7.99 us  [attend(): pl.pallas_call(attend_kernel, out_shape=[jax.ShapeDtypeStruct((NY, QB, PA...]
where the time goes in v10:
time: 65.1 us
  Pallas kernels  64.3 us (99%)
  local copies, waits for them, and re-layouts  0.69 us (1%)
    pallas_call x1, Pallas kernels, spread(): pl.pallas_call(spread_kernel, out_shape=[jax.ShapeDtypeStruct((NY, NX, QB...  33.9 us
    pallas_call x1, Pallas kernels, gather(): pl.pallas_call(gather_kernel, out_shape=jax.ShapeDtypeStruct((QB, ROWS, N...  22.4 us
    pallas_call x1, Pallas kernels, attend(): pl.pallas_call(attend_kernel, out_shape=[jax.ShapeDtypeStruct((NY, QB, PA...  7.99 us

profile of v10, /device:TPU:1, one launch (start us, length us, event | category | flops | bytes accessed | tf_op | source)
XLA Modules:
  0.0 65.1 jit_solution(8124127955719066161)
XLA Ops:
  0.0 33.9 %spread.1 = (bf16[4,4,4,8,640]{4,3,2,1,0:T(8,128)(2,1)S(1)}, bf16[4,4,4,8,256]{4,3,2,1,0:T(8,128)(2,1)S(1)}, bf16[4,1024,128]{2,1,0:T(8,128)(2,1)S(1)}, bf16[32,...) custom-call(s32[64]{0:T(128)} %target.3, bf16[4,8,3584]{2,1,0:T(8,128)(2,1)} %q.1, ...), custom_call_target="tpu_custom_call" | custom-call | tf_op jit(solution)/shard_map/spread/pallas_call | solution.py:304
  33.9 8.0 %attend.1 = (bf16[4,4,32,640]{3,2,1,0:T(8,128)(2,1)S(1)}, bf16[4,4,32,256]{3,2,1,0:T(8,128)(2,1)S(1)}, bf16[4,32,128]{2,1,0:T(8,128)(2,1)S(1)}) custom-call(s32[32,128]{1,0:T(8,128)S(1)} %get-tuple-element.14.ints, bf16[4,4,4,8,640]{4,3,2,1,0:T(8,128)(2,1)S(1)} %get-tuple-element.15.q_fore, bf16[4,4,4,8,256]{4,3,2,1,0:T(8,128)(2,1)S(1)} %get-tuple-element.16.q_rest, ...), custom_call_target="tpu_custom_call" | custom-call | tf_op jit(solution)/shard_map/attend/pallas_call | solution.py:432
  41.9 22.4 %gather.1 = bf16[4,8,3584]{2,1,0:T(8,128)(2,1)S(1)} custom-call(s32[64]{0:T(128)} %target.3, bf16[4,4,32,640]{3,2,1,0:T(8,128)(2,1)S(1)} %get-tuple-element.20.p, bf16[4,4,32,256]{3,2,1,0:T(8,128)(2,1)S(1)} %get-tuple-element.21.p_rest, bf16[4,32,128]{2,1,0:T(8,128)(2,1)S(1)} %get-tuple-element.22.extra_in), custom_call_target="tpu_custom_call" | custom-call | tf_op jit(solution)/shard_map/gather/pallas_call | solution.py:576
  64.4 0.7 %copy.9 = bf16[4,8,3584]{2,1,0:T(8,128)(2,1)} copy(bf16[4,8,3584]{2,1,0:T(8,128)(2,1)S(1)} %gather.1) | data formatting | bytes 458752

commit v11 on v10

--- a/solution.py
+++ b/solution.py
@@ -176,7 +176,6 @@
 
     stay[0].wait()
     leaving = blocks_out(goes, rep, groups)
-    blocks = blocks_in(goes, rep)
 
     def pack(d):
         for n in ORDER:
@@ -220,6 +219,7 @@
         qx[d].wait_recv()
         pack(d)
         over_z(d)
+    blocks = blocks_in(goes, rep)
 
     stay[4].wait()
     lists[...] = block_lists(listed, blocks, rep, y)

time: 65.1 us -> 65 us (level)
    pallas_call x1, Pallas kernels: 22.4 us -> 20.9 us  [gather(): pl.pallas_call(gather_kernel, out_shape=jax.ShapeDtypeStruct((QB, ROWS, N...]
    pallas_call x1, Pallas kernels: 7.99 us -> 9.3 us  [attend(): pl.pallas_call(attend_kernel, out_shape=[jax.ShapeDtypeStruct((NY, QB, PA...]
where the time goes in v11:
time: 65 us; the launch traced here: 64.9 us
  Pallas kernels  64.1 us (99%)
  local copies, waits for them, and re-layouts  0.69 us (1%)
    pallas_call x1, Pallas kernels, spread(): pl.pallas_call(spread_kernel, out_shape=[jax.ShapeDtypeStruct((NY, NX, QB...  33.9 us
    pallas_call x1, Pallas kernels, gather(): pl.pallas_call(gather_kernel, out_shape=jax.ShapeDtypeStruct((QB, ROWS, N...  20.9 us
    pallas_call x1, Pallas kernels, attend(): pl.pallas_call(attend_kernel, out_shape=[jax.ShapeDtypeStruct((NY, QB, PA...  9.3 us

profile of v11, /device:TPU:1, one launch (start us, length us, event | category | flops | bytes accessed | tf_op | source)
XLA Modules:
  0.0 64.9 jit_solution(12061308224099037051)
XLA Ops:
  0.0 33.9 %spread.1 = (bf16[4,4,4,8,640]{4,3,2,1,0:T(8,128)(2,1)S(1)}, bf16[4,4,4,8,256]{4,3,2,1,0:T(8,128)(2,1)S(1)}, bf16[4,1024,128]{2,1,0:T(8,128)(2,1)S(1)}, bf16[32,...) custom-call(s32[64]{0:T(128)} %target.3, bf16[4,8,3584]{2,1,0:T(8,128)(2,1)} %q.1, ...), custom_call_target="tpu_custom_call" | custom-call | tf_op jit(solution)/shard_map/spread/pallas_call | solution.py:304
  33.9 9.3 %attend.1 = (bf16[4,4,32,640]{3,2,1,0:T(8,128)(2,1)S(1)}, bf16[4,4,32,256]{3,2,1,0:T(8,128)(2,1)S(1)}, bf16[4,32,128]{2,1,0:T(8,128)(2,1)S(1)}) custom-call(s32[32,128]{1,0:T(8,128)S(1)} %get-tuple-element.14.ints, bf16[4,4,4,8,640]{4,3,2,1,0:T(8,128)(2,1)S(1)} %get-tuple-element.15.q_fore, bf16[4,4,4,8,256]{4,3,2,1,0:T(8,128)(2,1)S(1)} %get-tuple-element.16.q_rest, ...), custom_call_target="tpu_custom_call" | custom-call | tf_op jit(solution)/shard_map/attend/pallas_call | solution.py:432
  43.3 20.9 %gather.1 = bf16[4,8,3584]{2,1,0:T(8,128)(2,1)S(1)} custom-call(s32[64]{0:T(128)} %target.3, bf16[4,4,32,640]{3,2,1,0:T(8,128)(2,1)S(1)} %get-tuple-element.20.p, bf16[4,4,32,256]{3,2,1,0:T(8,128)(2,1)S(1)} %get-tuple-element.21.p_rest, bf16[4,32,128]{2,1,0:T(8,128)(2,1)S(1)} %get-tuple-element.22.extra_in), custom_call_target="tpu_custom_call" | custom-call | tf_op jit(solution)/shard_map/gather/pallas_call | solution.py:576
  64.2 0.7 %copy.9 = bf16[4,8,3584]{2,1,0:T(8,128)(2,1)} copy(bf16[4,8,3584]{2,1,0:T(8,128)(2,1)S(1)} %gather.1) | data formatting | bytes 458752

commit v12 on v11

--- a/solution.py
+++ b/solution.py
@@ -32,7 +32,7 @@
 PAIRS = 32
 SUM_LANE = 64
 NEG = -(2.0**100)
-STEP = 24
+STEP = 32
 TOGETHER = 2
 LANES = 8 * TOGETHER
 FIRST = 64

time: 65 us -> 64.7 us (level)
  no operation moved by 1% of the time
where the time goes in v12:
time: 64.7 us; the launch traced here: 64.6 us
  Pallas kernels  63.9 us (99%)
  local copies, waits for them, and re-layouts  0.69 us (1%)
    pallas_call x1, Pallas kernels, spread(): pl.pallas_call(spread_kernel, out_shape=[jax.ShapeDtypeStruct((NY, NX, QB...  33.9 us
    pallas_call x1, Pallas kernels, gather(): pl.pallas_call(gather_kernel, out_shape=jax.ShapeDtypeStruct((QB, ROWS, N...  20.6 us
    pallas_call x1, Pallas kernels, attend(): pl.pallas_call(attend_kernel, out_shape=[jax.ShapeDtypeStruct((NY, QB, PA...  9.35 us

profile of v12, /device:TPU:1, one launch (start us, length us, event | category | flops | bytes accessed | tf_op | source)
XLA Modules:
  0.0 64.6 jit_solution(7021840397847164821)
XLA Ops:
  0.0 33.9 %spread.1 = (bf16[4,4,4,8,640]{4,3,2,1,0:T(8,128)(2,1)S(1)}, bf16[4,4,4,8,256]{4,3,2,1,0:T(8,128)(2,1)S(1)}, bf16[4,1024,128]{2,1,0:T(8,128)(2,1)S(1)}, bf16[32,...) custom-call(s32[64]{0:T(128)} %target.3, bf16[4,8,3584]{2,1,0:T(8,128)(2,1)} %q.1, ...), custom_call_target="tpu_custom_call" | custom-call | tf_op jit(solution)/shard_map/spread/pallas_call | solution.py:304
  33.9 9.4 %attend.1 = (bf16[4,4,32,640]{3,2,1,0:T(8,128)(2,1)S(1)}, bf16[4,4,32,256]{3,2,1,0:T(8,128)(2,1)S(1)}, bf16[4,32,128]{2,1,0:T(8,128)(2,1)S(1)}) custom-call(s32[32,128]{1,0:T(8,128)S(1)} %get-tuple-element.14.ints, bf16[4,4,4,8,640]{4,3,2,1,0:T(8,128)(2,1)S(1)} %get-tuple-element.15.q_fore, bf16[4,4,4,8,256]{4,3,2,1,0:T(8,128)(2,1)S(1)} %get-tuple-element.16.q_rest, ...), custom_call_target="tpu_custom_call" | custom-call | tf_op jit(solution)/shard_map/attend/pallas_call | solution.py:432
  43.3 20.6 %gather.1 = bf16[4,8,3584]{2,1,0:T(8,128)(2,1)S(1)} custom-call(s32[64]{0:T(128)} %target.3, bf16[4,4,32,640]{3,2,1,0:T(8,128)(2,1)S(1)} %get-tuple-element.20.p, bf16[4,4,32,256]{3,2,1,0:T(8,128)(2,1)S(1)} %get-tuple-element.21.p_rest, bf16[4,32,128]{2,1,0:T(8,128)(2,1)S(1)} %get-tuple-element.22.extra_in), custom_call_target="tpu_custom_call" | custom-call | tf_op jit(solution)/shard_map/gather/pallas_call | solution.py:576
  63.9 0.7 %copy.9 = bf16[4,8,3584]{2,1,0:T(8,128)(2,1)} copy(bf16[4,8,3584]{2,1,0:T(8,128)(2,1)S(1)} %gather.1) | data formatting | bytes 458752

commit v13 on v12

--- a/solution.py
+++ b/solution.py
@@ -23,7 +23,7 @@
 KB = 32
 SHARD = 8
 SLICE = HEADS * D
-EARLY = 5
+EARLY = 6
 FORE = EARLY * D
 REST = SLICE - FORE
 ROWS = B // (NX * NY)

time: 64.7 us -> 66.4 us (1.026)
  Pallas kernels: 63.9 us -> 65.4 us
    pallas_call x1, Pallas kernels: 33.9 us -> 35.7 us  [spread(): pl.pallas_call(spread_kernel, out_shape=[jax.ShapeDtypeStruct((NY, NX, QB...]
where the time goes in v13:
time: 66.4 us; the launch traced here: 66.2 us
  Pallas kernels  65.4 us (98%)
  local copies, waits for them, and re-layouts  0.69 us (1%)
    pallas_call x1, Pallas kernels, spread(): pl.pallas_call(spread_kernel, out_shape=[jax.ShapeDtypeStruct((NY, NX, QB...  35.7 us
    pallas_call x1, Pallas kernels, gather(): pl.pallas_call(gather_kernel, out_shape=jax.ShapeDtypeStruct((QB, ROWS, N...  20.4 us
    pallas_call x1, Pallas kernels, attend(): pl.pallas_call(attend_kernel, out_shape=[jax.ShapeDtypeStruct((NY, QB, PA...  9.31 us

profile of v13, /device:TPU:1, one launch (start us, length us, event | category | flops | bytes accessed | tf_op | source)
XLA Modules:
  0.0 66.2 jit_solution(12569682344549478895)
XLA Ops:
  0.0 35.7 %spread.1 = (bf16[4,4,4,8,768]{4,3,2,1,0:T(8,128)(2,1)S(1)}, bf16[4,4,4,8,128]{4,3,2,1,0:T(8,128)(2,1)S(1)}, bf16[4,1024,128]{2,1,0:T(8,128)(2,1)S(1)}, bf16[32,...) custom-call(s32[64]{0:T(128)} %target.3, bf16[4,8,3584]{2,1,0:T(8,128)(2,1)} %q.1, ...), custom_call_target="tpu_custom_call" | custom-call | tf_op jit(solution)/shard_map/spread/pallas_call | solution.py:304
  35.7 9.3 %attend.1 = (bf16[4,4,32,768]{3,2,1,0:T(8,128)(2,1)S(1)}, bf16[4,4,32,128]{3,2,1,0:T(8,128)(2,1)S(1)}, bf16[4,32,128]{2,1,0:T(8,128)(2,1)S(1)}) custom-call(s32[32,128]{1,0:T(8,128)S(1)} %get-tuple-element.14.ints, bf16[4,4,4,8,768]{4,3,2,1,0:T(8,128)(2,1)S(1)} %get-tuple-element.15.q_fore, bf16[4,4,4,8,128]{4,3,2,1,0:T(8,128)(2,1)S(1)} %get-tuple-element.16.q_rest, ...), custom_call_target="tpu_custom_call" | custom-call | tf_op jit(solution)/shard_map/attend/pallas_call | solution.py:432
  45.0 20.4 %gather.1 = bf16[4,8,3584]{2,1,0:T(8,128)(2,1)S(1)} custom-call(s32[64]{0:T(128)} %target.3, bf16[4,4,32,768]{3,2,1,0:T(8,128)(2,1)S(1)} %get-tuple-element.20.p, bf16[4,4,32,128]{3,2,1,0:T(8,128)(2,1)S(1)} %get-tuple-element.21.p_rest, bf16[4,32,128]{2,1,0:T(8,128)(2,1)S(1)} %get-tuple-element.22.extra_in), custom_call_target="tpu_custom_call" | custom-call | tf_op jit(solution)/shard_map/gather/pallas_call | solution.py:576
  65.5 0.7 %copy.9 = bf16[4,8,3584]{2,1,0:T(8,128)(2,1)} copy(bf16[4,8,3584]{2,1,0:T(8,128)(2,1)S(1)} %gather.1) | data formatting | bytes 458752

commit v14 on v12

--- a/solution.py
+++ b/solution.py
@@ -32,7 +32,7 @@
 PAIRS = 32
 SUM_LANE = 64
 NEG = -(2.0**100)
-STEP = 32
+STEP = 28
 TOGETHER = 2
 LANES = 8 * TOGETHER
 FIRST = 64

time: 64.7 us -> 64.7 us (level)
    pallas_call x1, Pallas kernels: 9.35 us -> 8.68 us  [attend(): pl.pallas_call(attend_kernel, out_shape=[jax.ShapeDtypeStruct((NY, QB, PA...]
where the time goes in v14:
time: 64.7 us; the launch traced here: 64.5 us
  Pallas kernels  63.8 us (99%)
  local copies, waits for them, and re-layouts  0.69 us (1%)
    pallas_call x1, Pallas kernels, spread(): pl.pallas_call(spread_kernel, out_shape=[jax.ShapeDtypeStruct((NY, NX, QB...  33.9 us
    pallas_call x1, Pallas kernels, gather(): pl.pallas_call(gather_kernel, out_shape=jax.ShapeDtypeStruct((QB, ROWS, N...  21.1 us
    pallas_call x1, Pallas kernels, attend(): pl.pallas_call(attend_kernel, out_shape=[jax.ShapeDtypeStruct((NY, QB, PA...  8.68 us

profile of v14, /device:TPU:1, one launch (start us, length us, event | category | flops | bytes accessed | tf_op | source)
XLA Modules:
  0.0 64.5 jit_solution(9133715945845743287)
XLA Ops:
  0.0 33.9 %spread.1 = (bf16[4,4,4,8,640]{4,3,2,1,0:T(8,128)(2,1)S(1)}, bf16[4,4,4,8,256]{4,3,2,1,0:T(8,128)(2,1)S(1)}, bf16[4,1024,128]{2,1,0:T(8,128)(2,1)S(1)}, bf16[32,...) custom-call(s32[64]{0:T(128)} %target.3, bf16[4,8,3584]{2,1,0:T(8,128)(2,1)} %q.1, ...), custom_call_target="tpu_custom_call" | custom-call | tf_op jit(solution)/shard_map/spread/pallas_call | solution.py:304
  33.9 8.7 %attend.1 = (bf16[4,4,32,640]{3,2,1,0:T(8,128)(2,1)S(1)}, bf16[4,4,32,256]{3,2,1,0:T(8,128)(2,1)S(1)}, bf16[4,32,128]{2,1,0:T(8,128)(2,1)S(1)}) custom-call(s32[32,128]{1,0:T(8,128)S(1)} %get-tuple-element.14.ints, bf16[4,4,4,8,640]{4,3,2,1,0:T(8,128)(2,1)S(1)} %get-tuple-element.15.q_fore, bf16[4,4,4,8,256]{4,3,2,1,0:T(8,128)(2,1)S(1)} %get-tuple-element.16.q_rest, ...), custom_call_target="tpu_custom_call" | custom-call | tf_op jit(solution)/shard_map/attend/pallas_call | solution.py:432
  42.6 21.1 %gather.1 = bf16[4,8,3584]{2,1,0:T(8,128)(2,1)S(1)} custom-call(s32[64]{0:T(128)} %target.3, bf16[4,4,32,640]{3,2,1,0:T(8,128)(2,1)S(1)} %get-tuple-element.20.p, bf16[4,4,32,256]{3,2,1,0:T(8,128)(2,1)S(1)} %get-tuple-element.21.p_rest, bf16[4,32,128]{2,1,0:T(8,128)(2,1)S(1)} %get-tuple-element.22.extra_in), custom_call_target="tpu_custom_call" | custom-call | tf_op jit(solution)/shard_map/gather/pallas_call | solution.py:576
  63.8 0.7 %copy.9 = bf16[4,8,3584]{2,1,0:T(8,128)(2,1)} copy(bf16[4,8,3584]{2,1,0:T(8,128)(2,1)S(1)} %gather.1) | data formatting | bytes 458752
